TPU v7x, 256 devices: a whole 4x4x8 slice. The times are simulated.
256 devices in a mesh: head: 4 (over z_lo, core), seq: 4 (over x), req: 16 (over z_hi, y).
Axes of the slice: x: 4, y: 4, z: 8 (z_hi: 4, z_lo: 2; z = z_hi * 2 + z_lo), core: 2. Of those that a mesh axis runs over, the one named last changes fastest.
Arguments:
- stream: bfloat16 [8192, 2048], P(('req', 'seq', 'head')), may hold values from -12 to 12
- queries: bfloat16 [8192, 4096], P(('req', 'seq'), 'head'), may hold values from -16 to 16
- cache_pairs: bfloat16 [8192, 4, 128, 256], P(('req', 'seq'), 'head'), may hold values from -16 to 16
- fresh_pairs: bfloat16 [8192, 4, 256], P(('req', 'seq'), 'head'), may hold values from -16 to 16
- kept_slots: int32 [8192, 4, 96], P(('req', 'seq'), 'head'), may hold values from 0 to 31, as said below
- segment_kept_count: int32 [8192, 4, 4], P(('req', 'seq'), 'head'), may hold values from 1 to 24, 60 in all within a row
- output_weight: bfloat16 [4096, 2048], P('head', 'seq'), may hold values from -0.09375 to 0.09375
- norm_gain: float32 [2048], replicated, may hold values from 0.1 to 1.9
- routes: int32 [8192, 8], P(('req', 'seq', 'head')), may hold values from 0 to 63, all different within a row; in each aligned block of 32 rows (0 to 31, 32 to 63, ...) at most 8 rows name the same one
- gate_codes: int32 [8192, 8], P(('req', 'seq', 'head')), may hold values from 1 to 16
- gate_weight: bfloat16 [64, 2048, 768], P(('seq', 'req')), may hold values from -0.125 to 0.125
- up_weight: bfloat16 [64, 2048, 768], P(('seq', 'req')), may hold values from -0.125 to 0.125
- down_weight: bfloat16 [64, 768, 2048], P(('seq', 'req')), may hold values from -0.21875 to 0.21875
Outputs:
- layer_out: bfloat16 [8192, 2048], P(('req', 'seq', 'head'))
Inputs may be any that keep to these rules, and one draw needn't show every extreme that they name: `kept_slots`: entries s * 24 to (s + 1) * 24 - 1 of a list are distinct positions within segment s, counted from the segment's start; only the first segment_kept_count[r, h, s] of them are used. `segment_kept_count`: the 4 counts of a request's head add up to 60. `routes`: A token names 8 different experts. In each aligned block of 32 rows (the tokens of one device) no expert is named more than 8 times.
All inputs are finite; a program needn't handle non-finite values.
Results may differ from a plain program's by a relative error of at most 0.01.
Values may be sent and summed in bfloat16 or wider, within the bound.
No kernel may reach another device: no remote copies, remote signals or barrier semaphores. Data moves between devices by JAX's collectives and lax.ppermute only.
A program may use at most 128 MiB of HBM per device.

v0:
```python
import jax
import jax.numpy as jnp
from jax import lax
from jax.sharding import PartitionSpec as P

epsilon = 1e-06


def finish_heads(top_score, denom_sum, numer_sum, query_matrix, fresh_rows, head_dim, score_scale):
    own_score = (
        jnp.einsum(
            "rgd,rd->rg", query_matrix, fresh_rows[:, :head_dim], preferred_element_type=jnp.float32
        )
        * score_scale
    )
    new_top = jnp.maximum(top_score, own_score)
    keep_old = jnp.exp(top_score - new_top)
    take_new = jnp.exp(own_score - new_top)
    denom_sum = denom_sum * keep_old + take_new
    numer_sum = numer_sum * keep_old[..., None] + take_new[..., None] * fresh_rows[
        :, None, head_dim:
    ].astype(jnp.float32)
    return (
        (numer_sum / denom_sum[..., None]).reshape(query_matrix.shape[0], -1).astype(jnp.bfloat16)
    )


def on_device(
    stream,
    queries,
    cache_pairs,
    fresh_pairs,
    kept_slots,
    segment_kept_count,
    output_weight,
    norm_gain,
    routes,
    gate_codes,
    gate_weight,
    up_weight,
    down_weight,
):
    head_dim = cache_pairs.shape[-1] // 2
    req_rows = queries.shape[0]
    query_group_width = queries.shape[1] // head_dim
    score_scale = head_dim ** (-0.5)
    segment_count = segment_kept_count.shape[2]
    seg_keep = kept_slots.shape[2] // segment_count
    seg_length = cache_pairs.shape[2] // segment_count
    query_matrix = queries.reshape(req_rows, query_group_width, head_dim)
    seg_cache = cache_pairs[:, 0].reshape(req_rows, segment_count, seg_length, 2 * head_dim)
    slot_lists = kept_slots[:, 0].reshape(req_rows, segment_count, seg_keep)
    picker = (
        slot_lists[..., None] == jnp.arange(seg_length, dtype=jnp.int32)[None, None, None, :]
    ).astype(jnp.bfloat16)
    kept_rows = jnp.einsum(
        "rskl,rslc->rskc", picker, seg_cache, preferred_element_type=jnp.float32
    ).astype(jnp.bfloat16)
    scores = (
        jnp.einsum(
            "rgd,rskd->rgsk",
            query_matrix,
            kept_rows[..., :head_dim],
            preferred_element_type=jnp.float32,
        )
        * score_scale
    )
    valid_mask = (
        jnp.arange(seg_keep, dtype=jnp.int32)[None, None, None, :]
        < segment_kept_count[:, 0][:, None, :, None]
    )
    seg_max = jnp.max(jnp.where(valid_mask, scores, -jnp.inf), axis=-1)
    soft_probs = jnp.where(valid_mask, jnp.exp(scores - seg_max[..., None]), 0.0).astype(
        jnp.bfloat16
    )
    seg_sum = jnp.sum(soft_probs.astype(jnp.float32), axis=-1)
    seg_acc = jnp.einsum(
        "rgsk,rskd->rgsd", soft_probs, kept_rows[..., head_dim:], preferred_element_type=jnp.float32
    )
    top_score = jnp.max(seg_max, axis=2)
    factor = jnp.exp(seg_max - top_score[:, :, None])
    denom_sum = jnp.sum(factor * seg_sum, axis=2)
    numer_sum = jnp.sum(factor[..., None] * seg_acc, axis=2)
    head_out = finish_heads(
        top_score, denom_sum, numer_sum, query_matrix, fresh_pairs[:, 0], head_dim, score_scale
    )
    partial_value = jnp.dot(
        head_out,
        lax.all_gather(output_weight, "seq", axis=1, tiled=True),
        preferred_element_type=jnp.float32,
    )
    partial_value = partial_value.reshape(1, req_rows, -1)
    summed = lax.psum_scatter(
        partial_value.astype(jnp.bfloat16), "head", scatter_dimension=1, tiled=True
    ).astype(jnp.float32)
    attention = summed.reshape(stream.shape[0], -1)
    residual = (stream.astype(jnp.float32) + attention).astype(jnp.bfloat16)
    widened = residual.astype(jnp.float32)
    normed = (
        widened
        * lax.rsqrt(jnp.mean(widened * widened, axis=-1, keepdims=True) + epsilon)
        * norm_gain
    ).astype(jnp.bfloat16)
    tok_rows = routes.shape[0]
    top_count = routes.shape[1]
    local_experts = gate_weight.shape[0]
    owners = lax.axis_size(("seq", "req"))
    experts_all = local_experts * owners
    capacity = min(tok_rows, max(2, 2 * tok_rows * top_count // experts_all))
    flat_ids = routes.reshape(-1)
    flat_count = flat_ids.shape[0]
    match_bool = flat_ids[:, None] == jnp.arange(experts_all, dtype=jnp.int32)[None, :]
    row_pos = jnp.arange(flat_count, dtype=jnp.int32)
    strictly_before = (row_pos[None, :] < row_pos[:, None]).astype(jnp.bfloat16)
    earlier = jnp.dot(
        strictly_before, match_bool.astype(jnp.bfloat16), preferred_element_type=jnp.float32
    )
    slot_rank = jnp.sum(jnp.where(match_bool, earlier, 0.0), axis=1).astype(jnp.int32)
    target = flat_ids * capacity + slot_rank
    slot_ids = jnp.arange(experts_all * capacity, dtype=jnp.int32)
    placing = (target[None, :] == slot_ids[:, None]).astype(jnp.float32)
    token_place = jnp.sum(
        placing.reshape(experts_all * capacity, tok_rows, top_count), axis=-1
    ).astype(jnp.bfloat16)
    outgoing = jnp.dot(token_place, normed, preferred_element_type=jnp.float32).astype(jnp.bfloat16)
    outgoing = outgoing.reshape(owners, local_experts, capacity, -1)
    arrived = lax.all_to_all(outgoing, ("seq", "req"), split_axis=0, concat_axis=0, tiled=True)
    gate_val = jnp.einsum(
        "sjnd,jdf->sjnf", arrived, gate_weight, preferred_element_type=jnp.float32
    )
    upward = jnp.einsum("sjnd,jdf->sjnf", arrived, up_weight, preferred_element_type=jnp.float32)
    activated = (jax.nn.silu(gate_val) * upward).astype(jnp.bfloat16)
    expert_part = jnp.einsum(
        "sjnf,jfd->sjnd", activated, down_weight, preferred_element_type=jnp.float32
    )
    code_float = gate_codes.astype(jnp.float32)
    weights = (code_float / jnp.sum(code_float, axis=-1, keepdims=True)).reshape(-1)
    mixing = jnp.sum(
        (placing * weights[None, :]).reshape(experts_all * capacity, tok_rows, top_count), axis=-1
    ).T
    returned = lax.all_to_all(
        expert_part.astype(jnp.bfloat16), ("seq", "req"), split_axis=0, concat_axis=0, tiled=True
    ).astype(expert_part.dtype)
    mixture = jnp.dot(
        mixing,
        returned.reshape(experts_all * capacity, -1),
        precision=lax.Precision.HIGHEST,
        preferred_element_type=jnp.float32,
    )
    return (widened + mixture).astype(jnp.bfloat16)


def solution(mesh):
    placed = (
        P(("req", "seq", "head"), None),
        P(("req", "seq"), "head"),
        P(("req", "seq"), "head", None, None),
        P(("req", "seq"), "head", None),
        P(("req", "seq"), "head", None),
        P(("req", "seq"), "head", None),
        P("head", "seq"),
        P(),
        P(("req", "seq", "head"), None),
        P(("req", "seq", "head"), None),
        P(("seq", "req"), None, None),
        P(("seq", "req"), None, None),
        P(("seq", "req"), None, None),
    )
    return jax.shard_map(
        on_device,
        mesh=mesh,
        in_specs=placed,
        out_specs=P(("req", "seq", "head"), None),
        check_vma=False,
    )
```

profile of v0, /device:TPU:1, one launch (start us, length us, event | category | flops | bytes accessed | tf_op | source)
XLA Modules:
  0.0 228.2 jit_solution(3299606800916144169)
XLA Ops:
  7.3 1.0 copy.48
  8.3 0.9 copy.49
  9.2 1.0 copy.64
  10.4 5.3 %fusion.1 = bf16[128,4,24,256]{3,2,1,0:T(8,128)(2,1)S(1)} fusion(bf16[128,4,32,256]{3,2,1,0:T(8,128)(2,1)} %bitcast.151, s32[128,4,24]{2,1,0:T(4,128)S(1)} %copy.49), kind=kOutput, calls=%fused_computation.2 | convolution fusion | flops 204865536 | bytes 14729216 | tf_op jit(solution)/shard_map/rskl,rslc->rskc/dot_general | solution.py:56
  15.8 5.5 %fusion.30 = (f32[128,8,4]{1,2,0:T(4,128)S(1)}, f32[128,4,24,8]{2,3,1,0:T(8,128)S(1)}) fusion(pred[128,4,24]{2,1,0:T(4,128)(4,1)S(1)} %iota_compare_fusion.6, bf16[128,8,128,1]{2,1,0,3:T(8,128)(2,1)S(1)} %bitcast.154, bf16[128,4,24,256]{3,2,1,0:T(8,128)(2,1)S(1)} %fusion.1), kind=kOutput, calls=%fused_computation.34 | convolution fusion | flops 25456640 | bytes 3883008 | tf_op jit(solution)/shard_map/rgd,rskd->rgsk/dot_general | solution.py:60
  21.3 1.3 copy-done.2
  22.6 2.8 %convert_reduce_fusion = (f32[128,8,4]{1,2,0:T(4,128)}, f32[128,8]{1,0:T(8,128)S(1)}) fusion(f32[128,8,4]{1,2,0:T(4,128)S(1)} %get-tuple-element.16, f32[128,4,24,8]{2,3,1,0:T(8,128)S(1)} %get-tuple-element.17, pred[128,4,24]{2,1,0:T(4,128)(4,1)S(1)} %iota_compare_fusion.6), kind=kLoop, calls=%fused_computation.32 | loop fusion | flops 781312 | bytes 442368 | tf_op jit(solution)/shard_map/reduce_sum | solution.py:76
  25.5 1.9 multiply_reduce_fusion
  27.4 1.4 slice_convert_fusion
  28.8 1.2 fusion.62
  30.1 0.8 copy.52
  31.6 0.7 copy.55
  32.3 4.0 %fusion.25 = f32[128,8,128]{2,1,0:T(8,128)S(1)} fusion(bf16[128,4,24,256]{3,2,1,0:T(8,128)(2,1)} %copy-done.1, f32[128,8,4]{1,2,0:T(4,128)} %get-tuple-element.13, f32[128,4,24,8]{2,3,1,0:T(8,128)} %copy-done.2, f32[128,8,4]{1,2,0:T(4,128)S(1)} %get-tuple-element.16, pred[128,4,24]{2,1,0:T(4,128)(4,1)} %copy-done.6), kind=kOutput, calls=%fused_computation.26 | convolution fusion | flops 26476544 | bytes 6111232 | tf_op jit(solution)/shard_map/rgsk,rskd->rgsd/dot_general | solution.py:77
  36.8 26.7 %all-gather.2.cloned.1.call-done = bf16[1024,2048]{1,0:T(8,128)(2,1)} async-done(((bf16[1024,512]{1,0:T(8,128)(2,1)}), bf16[1024,2048]{1,0:T(8,128)(2,1)}) %all-gather.2.cloned.1.call-update) | async-done | bytes 4194320 | tf_op jit(solution)/shard_map/all_gather | solution.py:89
  63.5 3.7 %fusion.20 = bf16[1,128,2048]{2,1,0:T(8,128)(2,1)} fusion(bf16[1024,2048]{1,0:T(8,128)(2,1)} %all-gather.2.cloned.1.call-done, bf16[16,8,8,128]{3,2,1,0:T(8,128)(2,1)S(1)} %bitcast.152), kind=kOutput, calls=%fused_computation.19 | convolution fusion | flops 537133056 | bytes 4980736 | tf_op jit(solution)/shard_map/dot_general | solution.py:87
  68.3 21.2 %reduce-scatter.2.cloned.1.call-done = bf16[1,32,2048]{2,1,0:T(8,128)(2,1)} async-done(((bf16[1,128,2048]{2,1,0:T(8,128)(2,1)}), bf16[1,32,2048]{2,1,0:T(8,128)(2,1)}) %reduce-scatter.2.cloned.1.call-update) | async-done | bytes 131088 | tf_op jit(solution)/shard_map/reduce_scatter | solution.py:93
  89.5 1.1 fusion.52
  90.6 1.7 fusion.16
  92.3 54.3 %all_to_all.10 = bf16[64,1,8,2048]{3,2,1,0:T(8,128)(2,1)S(1)} all-to-all(bf16[64,1,8,2048]{3,2,1,0:T(8,128)(2,1)S(1)} %fusion.16), channel_id=1, replica_groups=mesh['head'=4,'seq'=4,'req'=16] {'seq','req'}, dimensions={0} | all-to-all | bytes 4194304 | tf_op jit(solution)/shard_map/all_to_all | solution.py:127
  146.6 1.3 copy-done.3
  147.9 3.0 %fusion.10 = f32[64,8,768]{2,1,0:T(8,128)} fusion(bf16[1,2048,768]{2,1,0:T(8,128)(2,1)S(1)} %copy-done.15, bf16[64,1,8,2048]{3,2,1,0:T(8,128)(2,1)S(1)} %all_to_all.10), kind=kOutput, calls=%fused_computation.11 | convolution fusion | flops 1610612736 | bytes 6815744 | tf_op jit(solution)/shard_map/sjnd,jdf->sjnf/dot_general | solution.py:128
  150.9 8.2 %fusion.17 = bf16[64,1,8,2048]{3,2,1,0:T(8,128)(2,1)} fusion(bf16[1,768,2048]{2,1,0:T(8,128)(2,1)S(1)} %copy-done, bf16[1,2048,768]{2,1,0:T(8,128)(2,1)} %param.24, bf16[64,1,8,2048]{3,2,1,0:T(8,128)(2,1)} %copy-done.3, f32[64,8,768]{2,1,0:T(8,128)} %fusion.10), kind=kOutput, calls=%fused_computation.17 | convolution fusion | flops 3224633344 | bytes 12058624 | tf_op jit(solution)/shard_map/sjnf,jfd->sjnd/dot_general | solution.py:133
  159.1 60.5 %all_to_all.11 = bf16[64,1,8,2048]{3,2,1,0:T(8,128)(2,1)S(1)} all-to-all(bf16[64,1,8,2048]{3,2,1,0:T(8,128)(2,1)} %fusion.17), channel_id=1, replica_groups=mesh['head'=4,'seq'=4,'req'=16] {'seq','req'}, dimensions={0} | all-to-all | bytes 4194304 | tf_op jit(solution)/shard_map/all_to_all | solution.py:141
  219.6 1.8 fusion.21
  (52 shorter events, 3.4 us)
Async XLA Ops:
  6.5 144.4 %copy-start = (bf16[1,768,2048]{2,1,0:T(8,128)(2,1)S(1)}, bf16[1,768,2048]{2,1,0:T(8,128)(2,1)}, u32[]{:S(2)}) copy-start(bf16[1,768,2048]{2,1,0:T(8,128)(2,1)} %param.25) | copy-start | bytes 9437188
  6.5 57.0 %all-gather.2.cloned.1.call-start = ((), (), s32[]{:S(2)}) async-start(), calls=%async_computation.3 | async-start | bytes 5242880 | tf_op jit(solution)/shard_map/all_gather | solution.py:89
  7.3 82.3 %reduce-scatter.2.cloned.1.call-start = ((), (), s32[]{:S(2)}) async-start(), calls=%async_computation.4 | async-start | bytes 655360 | tf_op jit(solution)/shard_map/reduce_scatter | solution.py:93
  10.2 5.6 %copy-start.11 = (bf16[16,8,8,128]{3,2,1,0:T(8,128)(2,1)}, bf16[16,8,8,128]{3,2,1,0:T(8,128)(2,1)S(1)}, u32[]{:S(2)}) copy-start(bf16[16,8,8,128]{3,2,1,0:T(8,128)(2,1)S(1)} %copy.64) | copy-start | bytes 786436
  10.4 10.9 %copy-start.6 = (pred[128,4,24]{2,1,0:T(4,128)(4,1)}, pred[128,4,24]{2,1,0:T(4,128)(4,1)S(1)}, u32[]{:S(2)}) copy-start(pred[128,4,24]{2,1,0:T(4,128)(4,1)S(1)} %iota_compare_fusion.6) | copy-start | bytes 36868
  15.8 5.5 %copy-start.1 = (bf16[128,4,24,256]{3,2,1,0:T(8,128)(2,1)}, bf16[128,4,24,256]{3,2,1,0:T(8,128)(2,1)S(1)}, u32[]{:S(2)}) copy-start(bf16[128,4,24,256]{3,2,1,0:T(8,128)(2,1)S(1)} %fusion.1) | copy-start | bytes 18874372
  21.3 1.3 copy-start.2
  32.3 4.0 %copy-start.7 = (f32[128,128]{1,0:T(8,128)S(1)}, f32[128,128]{1,0:T(8,128)}, u32[]{:S(2)}) copy-start(f32[128,128]{1,0:T(8,128)} %get-tuple-element.14) | copy-start | bytes 196612
  32.3 4.0 %copy-start.8 = (f32[128,8]{1,0:T(8,128)S(1)}, f32[128,8]{1,0:T(8,128)}, u32[]{:S(2)}) copy-start(f32[128,8]{1,0:T(8,128)} %copy.52) | copy-start | bytes 12292
  32.3 4.0 %copy-start.9 = (f32[128,8]{1,0:T(8,128)S(1)}, f32[128,8]{1,0:T(8,128)}, u32[]{:S(2)}) copy-start(f32[128,8]{1,0:T(8,128)} %copy.53) | copy-start | bytes 12292
  32.3 4.0 %copy-start.10 = (f32[128,8]{1,0:T(8,128)S(1)}, f32[128,8]{1,0:T(8,128)}, u32[]{:S(2)}) copy-start(f32[128,8]{1,0:T(8,128)} %copy.55) | copy-start | bytes 12292
  63.5 3.8 %copy-start.14 = (s32[32,8]{0,1:T(8,128)S(1)}, s32[32,8]{0,1:T(8,128)}, u32[]{:S(2)}) copy-start(s32[32,8]{0,1:T(8,128)} %param.21) | copy-start | bytes 3076
  63.5 4.2 %copy-start.12 = (s32[32,8]{0,1:T(8,128)S(1)}, s32[32,8]{0,1:T(8,128)}, u32[]{:S(2)}) copy-start(s32[32,8]{0,1:T(8,128)} %param.22) | copy-start | bytes 3076
  63.5 26.0 %copy-start.4 = (bf16[32,2048]{1,0:T(8,128)(2,1)S(1)}, bf16[32,2048]{1,0:T(8,128)(2,1)}, u32[]{:S(2)}) copy-start(bf16[32,2048]{1,0:T(8,128)(2,1)} %param.13) | copy-start | bytes 393220
  63.5 27.1 %copy-start.13 = (f32[2048]{0:T(1024)S(1)}, f32[2048]{0:T(1024)}, u32[]{:S(2)}) copy-start(f32[2048]{0:T(1024)} %param.20) | copy-start | bytes 24580
  92.3 55.6 %copy-start.15 = (bf16[1,2048,768]{2,1,0:T(8,128)(2,1)S(1)}, bf16[1,2048,768]{2,1,0:T(8,128)(2,1)}, u32[]{:S(2)}) copy-start(bf16[1,2048,768]{2,1,0:T(8,128)(2,1)} %param.23) | copy-start | bytes 9437188
  146.6 1.4 copy-start.3
  159.1 60.5 %copy-start.5 = (bf16[1,32,2048]{2,1,0:T(8,128)(2,1)S(1)}, bf16[1,32,2048]{2,1,0:T(8,128)(2,1)}, u32[]{:S(2)}) copy-start(bf16[1,32,2048]{2,1,0:T(8,128)(2,1)} %reduce-scatter.2.cloned.1.call-done) | copy-start | bytes 393220
Sparse Core Ops, SparseCore 0:
  9.1 54.3 all-gather.1
  67.4 22.0 reduce-scatter.1
where the time goes:
time: 231 us; the launch traced here: 228 us
  blocking collectives  115 us (50%)
  waiting for transfers between devices  48.6 us (21%)
  matrix products  34.6 us (15%)
  between operations  13.6 us (6%)
  other arithmetic  8.29 us (4%)
  local copies, waits for them, and re-layouts  8.25 us (4%)
    all_to_all x1, blocking collectives, on_device(): lax.all_to_all(expert_part.astype(jnp.bfloat16), ('seq', 'req'), split_ax...  60.5 us
    all_to_all x1, blocking collectives, on_device(): lax.all_to_all(outgoing, ('seq', 'req'), split_axis=0, concat_axis=0, til...  54.3 us
    all_gather x1, waiting for transfers between devices, on_device(): lax.all_gather(output_weight, 'seq', axis=1, tiled=True)  26.7 us
    reduce_scatter x1, waiting for transfers between devices, on_device(): lax.psum_scatter(partial_value.astype(jnp.bfloat16), 'head', scatter_dime...  21.2 us
    dot_general x1, matrix products, on_device(): jnp.einsum('sjnf,jfd->sjnd', activated, down_weight, preferred_element_ty...  8.21 us
    dot_general x1, matrix products, on_device(): jnp.einsum('rgd,rskd->rgsk', query_matrix, kept_rows[..., :head_dim], pre...  5.51 us
    dot_general x1, matrix products, on_device(): jnp.einsum('rskl,rslc->rskc', picker, seg_cache, preferred_element_type=j...  5.33 us
  transfers between devices with their start and end apart: 2, of which 2 were waited for; matrix products, arithmetic and copies ran while one was open for 13% of the time, Pallas kernels for 0%

commit v1 on v0

v1 whole, which is shorter than its diff:
```python
import jax
import jax.numpy as jnp
from jax import lax
from jax.experimental import pallas as pl
from jax.experimental.pallas import tpu as pltpu
from jax.sharding import Mesh
from jax.sharding import PartitionSpec as P

epsilon = 1e-06
LANES = 128
ATT_BLOCK = 32
HID_BLOCK = 256
MESH_AXES = ("zl", "core", "seq", "zh", "y")
PLANE = ("seq", "y")
HEADS = ("zl", "core")
STEPS = (0, 1, 3, 2)


def iota(shape, dim):
    return lax.broadcasted_iota(jnp.int32, shape, dim)


def div(a, b):
    return lax.div(a, jnp.full_like(a, b))


def rem(a, b):
    return lax.rem(a, jnp.full_like(a, b))


def attention_body(slots_ref, counts_ref, query_ref, cache_ref, fresh_ref, out_ref, bias_ref):
    rows, _, positions, pair = cache_ref.shape
    head_dim = pair // 2
    group = query_ref.shape[1] // head_dim
    scale = head_dim ** (-0.5)
    step = pl.program_id(0)

    @pl.when(step == 0)
    def _():
        listed, all_rows = slots_ref.shape
        segments = counts_ref.shape[0]
        keep = listed // segments
        seg_length = positions // segments
        counts = counts_ref[...].astype(jnp.float32)
        limit = jnp.concatenate(
            [jnp.broadcast_to(counts[s : s + 1], (keep, all_rows)) for s in range(segments)], axis=0
        )
        rank = rem(iota((listed, all_rows), 0), keep).astype(jnp.float32)
        valid = jnp.where(rank < limit, slots_ref[...].astype(jnp.float32), 99.0)
        valid = valid.astype(jnp.bfloat16)
        place = rem(iota((positions, all_rows), 0), seg_length).astype(jnp.float32)
        source = iota((positions, listed), 1)
        wanted = div(iota((positions, listed), 0), seg_length) * keep
        bias = jnp.full((positions, all_rows), -1e30, jnp.float32)
        for j in range(keep):
            pick = jnp.where(source == wanted + j, 1.0, 0.0).astype(jnp.bfloat16)
            here = jnp.dot(pick, valid, preferred_element_type=jnp.float32)
            bias = jnp.where(here == place, 0.0, bias)
        bias_ref[...] = bias.T

    query = query_ref[...].reshape(rows, group, head_dim)
    keys = cache_ref[:, 0, :, :head_dim]
    values = cache_ref[:, 0, :, head_dim:]
    fresh = fresh_ref[...].astype(jnp.float32)
    scores = jnp.einsum("rgd,rpd->rgp", query, keys, preferred_element_type=jnp.float32) * scale
    bias = bias_ref[pl.ds(pl.multiple_of(step * rows, rows), rows), :]
    scores = scores + bias[:, None, :]
    own = jnp.sum(
        query.astype(jnp.float32) * fresh[:, None, :head_dim], axis=-1, keepdims=True
    ) * scale
    top = jnp.maximum(jnp.max(scores, axis=-1, keepdims=True), own)
    probs = jnp.exp(scores - top).astype(jnp.bfloat16)
    take_new = jnp.exp(own - top)
    denom = jnp.sum(probs.astype(jnp.float32), axis=-1, keepdims=True) + take_new
    numer = jnp.einsum("rgp,rpd->rgd", probs, values, preferred_element_type=jnp.float32)
    numer = numer + take_new * fresh[:, None, head_dim:]
    out_ref[...] = (numer / denom).astype(jnp.bfloat16).reshape(rows, group * head_dim)


def attention(slots, counts, queries, cache_pairs, fresh):
    rows, width = queries.shape
    block = min(ATT_BLOCK, rows)
    return pl.pallas_call(
        attention_body,
        grid=(rows // block,),
        in_specs=[
            pl.BlockSpec(slots.shape, lambda i: (0, 0)),
            pl.BlockSpec(counts.shape, lambda i: (0, 0)),
            pl.BlockSpec((block, width), lambda i: (i, 0)),
            pl.BlockSpec((block,) + cache_pairs.shape[1:], lambda i: (i, 0, 0, 0)),
            pl.BlockSpec((block, fresh.shape[1]), lambda i: (i, 0)),
        ],
        out_specs=pl.BlockSpec((block, width), lambda i: (i, 0)),
        out_shape=jax.ShapeDtypeStruct((rows, width), jnp.bfloat16),
        scratch_shapes=[pltpu.VMEM((rows, cache_pairs.shape[2]), jnp.float32)],
        name="attention",
    )(slots, counts, queries, cache_pairs, fresh)


def project_body(seq_ref, *refs):
    *head_refs, weight_ref, out_ref = refs
    count = len(head_refs)
    weight = weight_ref[...]
    for step, head_ref in zip(STEPS, head_refs):
        part = jnp.dot(head_ref[...], weight, preferred_element_type=jnp.float32)
        out_ref[(seq_ref[0] + (count - step)) & (count - 1)] = part.astype(jnp.bfloat16)


def project(seq, blocks, weight):
    rows = blocks[0].shape[0]
    return pl.pallas_call(
        project_body,
        in_specs=[pl.BlockSpec(memory_space=pltpu.SMEM)]
        + [pl.BlockSpec(memory_space=pltpu.VMEM)] * (len(blocks) + 1),
        out_shape=jax.ShapeDtypeStruct((len(blocks), rows, weight.shape[1]), jnp.bfloat16),
        name="project",
    )(seq, *blocks, weight)


def norm_body(parts_ref, stream_ref, gain_ref, routes_ref, codes_ref, residual_ref, payload_ref):
    seqs, heads, rows, width = parts_ref.shape
    wide = seqs * width
    total = jnp.zeros((rows, 1), jnp.float32)
    for s in range(seqs):
        at = slice(s * width, (s + 1) * width)
        attn = parts_ref[s, 0].astype(jnp.float32)
        for h in range(1, heads):
            attn = attn + parts_ref[s, h].astype(jnp.float32)
        residual = (stream_ref[:, at].astype(jnp.float32) + attn).astype(jnp.bfloat16)
        residual_ref[:, at] = residual
        widened = residual.astype(jnp.float32)
        total = total + jnp.sum(widened * widened, axis=-1, keepdims=True)
    factor = lax.rsqrt(total / wide + epsilon)
    for s in range(seqs):
        at = slice(s * width, (s + 1) * width)
        widened = residual_ref[:, at].astype(jnp.float32)
        payload_ref[:, at] = (widened * factor * gain_ref[:, at]).astype(jnp.bfloat16)
    top = routes_ref.shape[0]
    tail = jnp.concatenate(
        [
            routes_ref[...].astype(jnp.float32),
            codes_ref[...].astype(jnp.float32),
            jnp.zeros((LANES - 2 * top, rows), jnp.float32),
        ],
        axis=0,
    )
    payload_ref[:, wide:] = tail.T.astype(jnp.bfloat16)


def norm(parts, stream, gain, routes, codes):
    rows, wide = stream.shape
    return pl.pallas_call(
        norm_body,
        out_shape=[
            jax.ShapeDtypeStruct((rows, wide), jnp.bfloat16),
            jax.ShapeDtypeStruct((rows, wide + LANES), jnp.bfloat16),
        ],
        name="norm",
    )(parts, stream, gain, routes, codes)


def placement(tail, zh, blocks, top, experts_shape, capacity):
    seqs, zs, ys = experts_shape
    tokens = tail.shape[0]
    rows = tokens // blocks
    experts = seqs * ys
    slots = experts * blocks * capacity
    column = iota((tokens, experts), 1)
    name = (div(column, ys) * zs + zh) * ys + rem(column, ys)
    name = name.astype(jnp.float32)
    match = jnp.zeros((tokens, experts), jnp.float32)
    code = jnp.zeros((tokens, experts), jnp.float32)
    for k in range(top):
        hit = tail[:, k : k + 1] == name
        match = jnp.where(hit, 1.0, match)
        code = jnp.where(hit, tail[:, top + k : top + k + 1], code)
    row, col = iota((tokens, tokens), 0), iota((tokens, tokens), 1)
    before = jnp.where((div(row, rows) == div(col, rows)) & (col < row), 1.0, 0.0)
    rank = jnp.dot(
        before.astype(jnp.bfloat16), match.astype(jnp.bfloat16), preferred_element_type=jnp.float32
    )
    rank = jnp.where(match > 0.0, rank, 99.0)
    spread = jnp.where(
        div(iota((experts, slots), 1), blocks * capacity) == iota((experts, slots), 0), 1.0, 0.0
    ).astype(jnp.bfloat16)
    rank = jnp.dot(rank.astype(jnp.bfloat16), spread, preferred_element_type=jnp.float32)
    code = jnp.dot(code.astype(jnp.bfloat16), spread, preferred_element_type=jnp.float32)
    slot = rem(iota((tokens, slots), 1), blocks * capacity)
    at = div(iota((tokens, slots), 0), rows) * capacity + rank.astype(jnp.int32)
    return jnp.where((slot == at) & (rank < capacity), code, 0.0)


def dispatch_body(zh_ref, *refs, top, experts_shape, capacity):
    *payload_refs, out_ref = refs
    blocks = len(payload_refs)
    wide = out_ref.shape[1]
    tail = jnp.concatenate([r[:, wide:].astype(jnp.float32) for r in payload_refs], axis=0)
    code = placement(tail, zh_ref[0], blocks, top, experts_shape, capacity)
    place = jnp.where(code > 0.0, 1.0, 0.0).T.astype(jnp.bfloat16)
    tokens = jnp.concatenate([r[:, :wide] for r in payload_refs], axis=0)
    out_ref[...] = jnp.dot(place, tokens, preferred_element_type=jnp.float32).astype(jnp.bfloat16)


def dispatch(zh, payloads, wide, static):
    seqs, _, ys = static["experts_shape"]
    slots = seqs * ys * len(payloads) * static["capacity"]
    out = pl.pallas_call(
        lambda *refs: dispatch_body(*refs, **static),
        in_specs=[pl.BlockSpec(memory_space=pltpu.SMEM)]
        + [pl.BlockSpec(memory_space=pltpu.VMEM)] * len(payloads),
        out_shape=jax.ShapeDtypeStruct((slots, wide), jnp.bfloat16),
        name="dispatch",
    )(zh, *payloads)
    return out.reshape(seqs * ys, -1, wide)


def expert_body(rows_ref, gate_ref, up_ref, down_ref, out_ref, acc_ref):
    step = pl.program_id(0)
    rows = rows_ref[...]
    gate = jnp.dot(rows, gate_ref[0], preferred_element_type=jnp.float32)
    up = jnp.dot(rows, up_ref[0], preferred_element_type=jnp.float32)
    act = (gate / (1.0 + jnp.exp(-gate)) * up).astype(jnp.bfloat16)
    part = jnp.dot(act, down_ref[0], preferred_element_type=jnp.float32)
    last = pl.num_programs(0) - 1

    @pl.when(step == 0)
    def _():
        acc_ref[...] = part

    @pl.when((step > 0) & (step < last))
    def _():
        acc_ref[...] += part

    @pl.when(step == last)
    def _():
        out_ref[...] = (acc_ref[...] + part).astype(jnp.bfloat16)


def expert(arrived, gate_weight, up_weight, down_weight):
    shape = arrived.shape
    wide = shape[-1]
    rows = shape[0] * shape[1]
    hidden = gate_weight.shape[2]
    out = pl.pallas_call(
        expert_body,
        grid=(hidden // HID_BLOCK,),
        in_specs=[
            pl.BlockSpec((rows, wide), lambda i: (0, 0)),
            pl.BlockSpec((1, wide, HID_BLOCK), lambda i: (0, 0, i)),
            pl.BlockSpec((1, wide, HID_BLOCK), lambda i: (0, 0, i)),
            pl.BlockSpec((1, HID_BLOCK, wide), lambda i: (0, i, 0)),
        ],
        out_specs=pl.BlockSpec((rows, wide), lambda i: (0, 0)),
        out_shape=jax.ShapeDtypeStruct((rows, wide), jnp.bfloat16),
        scratch_shapes=[pltpu.VMEM((rows, wide), jnp.float32)],
        name="expert",
    )(arrived.reshape(rows, wide), gate_weight, up_weight, down_weight)
    return out.reshape(shape)


def mixed(zh_ref, tail, returned, blocks, static):
    top = static["top"]
    code = placement(tail, zh_ref[0], blocks, **static)
    total = jnp.sum(
        jnp.where(
            (iota(tail.shape, 1) >= top) & (iota(tail.shape, 1) < 2 * top), tail, 0.0
        ),
        axis=-1,
        keepdims=True,
    )
    part = jnp.dot(code.astype(jnp.bfloat16), returned, preferred_element_type=jnp.float32)
    return part / total


def combine_body(zh_ref, *refs, static):
    *tail_refs, returned_ref, o0_ref, o1_ref, o2_ref = refs
    outs = (o0_ref, o1_ref, o2_ref)
    tail = jnp.concatenate([r[...].astype(jnp.float32) for r in tail_refs], axis=0)
    part = mixed(zh_ref, tail, returned_ref[...], len(tail_refs), static)
    rows = part.shape[0] // len(tail_refs)
    for b, out_ref in enumerate(outs):
        out_ref[...] = part[b * rows : (b + 1) * rows].astype(jnp.bfloat16)


def tail_spec(payload):
    rows, wide = payload.shape
    return pl.BlockSpec((rows, LANES), lambda i: (0, wide // LANES - 1))


def combine(zh, payloads, returned, static):
    wide = returned.shape[-1]
    rows = payloads[0].shape[0]
    returned = returned.reshape(-1, wide)
    return pl.pallas_call(
        lambda *refs: combine_body(*refs, static=static),
        grid=(1,),
        in_specs=[pl.BlockSpec(memory_space=pltpu.SMEM)]
        + [tail_spec(p) for p in payloads]
        + [pl.BlockSpec(returned.shape, lambda i: (0, 0))],
        out_specs=[pl.BlockSpec((rows, wide), lambda i: (0, 0))] * len(payloads),
        out_shape=[jax.ShapeDtypeStruct((rows, wide), jnp.bfloat16)] * len(payloads),
        name="combine",
    )(zh, *payloads, returned)


def finish_body(zh_ref, tail_ref, returned_ref, residual_ref, a_ref, b_ref, c_ref, out_ref, *, static):
    tail = tail_ref[...].astype(jnp.float32)
    part = mixed(zh_ref, tail, returned_ref[...], 1, static)
    for ref in (a_ref, b_ref, c_ref, residual_ref):
        part = part + ref[...].astype(jnp.float32)
    out_ref[...] = part.astype(jnp.bfloat16)


def finish(zh, payload, returned, residual, others, static):
    rows, wide = residual.shape
    returned = returned.reshape(-1, wide)
    row_spec = pl.BlockSpec((rows, wide), lambda i: (0, 0))
    return pl.pallas_call(
        lambda *refs: finish_body(*refs, static=static),
        grid=(1,),
        in_specs=[
            pl.BlockSpec(memory_space=pltpu.SMEM),
            tail_spec(payload),
            pl.BlockSpec(returned.shape, lambda i: (0, 0)),
        ]
        + [row_spec] * 4,
        out_specs=row_spec,
        out_shape=jax.ShapeDtypeStruct((rows, wide), jnp.bfloat16),
        name="finish",
    )(zh, payload, returned, residual, *others)


def shift(size, by):
    return [(i, (i + by) % size) for i in range(size)]


def exchange(blocks, axes):
    return lax.all_to_all(blocks, axes, split_axis=0, concat_axis=0, tiled=True)


def on_device(
    stream,
    queries,
    cache_pairs,
    fresh_pairs,
    kept_slots,
    segment_kept_count,
    output_weight,
    norm_gain,
    routes,
    gate_codes,
    gate_weight,
    up_weight,
    down_weight,
):
    rows, wide = stream.shape
    seqs, zs, ys = (lax.axis_size(a) for a in ("seq", "zh", "y"))
    seq = lax.axis_index("seq").astype(jnp.int32).reshape(1)
    zh = lax.axis_index("zh").astype(jnp.int32).reshape(1)
    experts = seqs * zs * ys
    static = dict(
        top=routes.shape[1],
        experts_shape=(seqs, zs, ys),
        capacity=min(rows, max(2, 2 * rows * routes.shape[1] // experts)),
    )

    head_out = attention(
        kept_slots[:, 0].T, segment_kept_count[:, 0].T, queries, cache_pairs, fresh_pairs[:, 0]
    )
    head_blocks = [head_out] + [
        lax.ppermute(head_out, "seq", shift(seqs, d)) for d in STEPS[1:]
    ]
    parts = project(seq, head_blocks, output_weight)
    parts = exchange(parts.reshape(-1, rows, parts.shape[-1]), ("seq",) + HEADS)
    parts = parts.reshape(seqs, -1, rows, parts.shape[-1])
    residual, payload = norm(parts, stream, norm_gain.reshape(1, -1), routes.T, gate_codes.T)

    far = [lax.ppermute(payload, "zh", shift(zs, d)) for d in STEPS[1:]]
    near_rows = exchange(dispatch(zh, [payload], wide, static), PLANE)
    far_rows = exchange(dispatch(zh, far, wide, static), PLANE)
    near_out = expert(near_rows, gate_weight, up_weight, down_weight)
    far_out = exchange(expert(far_rows, gate_weight, up_weight, down_weight), PLANE)
    sums = combine(zh, far, far_out, static)
    others = [lax.ppermute(s, "zh", shift(zs, -d)) for s, d in zip(sums, STEPS[1:])]
    near_out = exchange(near_out, PLANE)
    return finish(zh, payload, near_out, residual, others, static)


def solution(mesh):
    fine = Mesh(mesh.devices.reshape(2, 2, mesh.shape["seq"], 4, 4), MESH_AXES)
    heads, req = HEADS, ("zh", "y")
    tokens = P(req + ("seq",) + heads, None)
    requests = req + ("seq",)
    owned = P(("seq",) + req, None, None)
    placed = (
        tokens,
        P(requests, heads),
        P(requests, heads, None, None),
        P(requests, heads, None),
        P(requests, heads, None),
        P(requests, heads, None),
        P(heads, "seq"),
        P(),
        tokens,
        tokens,
        owned,
        owned,
        owned,
    )
    return jax.shard_map(
        on_device, mesh=fine, in_specs=placed, out_specs=tokens, check_vma=False
    )
```

time: 231 us -> 165 us (0.71)
  blocking collectives: 115 us -> 16 us
  starting transfers between devices: 0.04 us -> 43.3 us
  Pallas kernels: 0 us -> 39.9 us
  matrix products: 34.6 us -> 0 us
  between operations: 13.6 us -> 0.09 us
  waiting for transfers between devices: 48.6 us -> 60.7 us
  other arithmetic: 8.29 us -> 0 us
  local copies, waits for them, and re-layouts: 8.25 us -> 2.04 us
    all_to_all x2 -> x1, blocking collectives: 115 us -> 16 us  [exchange(): return lax.all_to_all(blocks, axes, split_axis=0, concat_axis=0, tiled=True)]
    pallas_call x0 -> x9, Pallas kernels: none -> 39.9 us  [the longest x2 15.8 us: expert(): pl.pallas_call(expert_body, grid=(hidden // HID_BLOCK,), in_specs=[pl.Blo...]
    dot_general x10 -> x0, matrix products: 34.6 us -> none  [the longest x1 8.21 us: on_device(): jnp.einsum('sjnf,jfd->sjnd', activated, down_weight, preferred_element_ty...]
    all_to_all x0 -> x4, waiting for transfers between devices: none -> 32.3 us  [exchange(): return lax.all_to_all(blocks, axes, split_axis=0, concat_axis=0, tiled=True)]
    ppermute x0 -> x9, waiting for transfers between devices: none -> 28.3 us  [the longest x3 11 us: on_device(): lax.ppermute(head_out, 'seq', shift(seqs, d))]
    all_gather x1 -> x0, waiting for transfers between devices: 26.7 us -> none  [on_device(): lax.all_gather(output_weight, 'seq', axis=1, tiled=True)]
    all_to_all x0 -> x4, starting transfers between devices: none -> 23.6 us  [exchange(): return lax.all_to_all(blocks, axes, split_axis=0, concat_axis=0, tiled=True)]
    reduce_scatter x1 -> x0, waiting for transfers between devices: 21.2 us -> none  [on_device(): lax.psum_scatter(partial_value.astype(jnp.bfloat16), 'head', scatter_dime...]
  transfers between devices with their start and end apart: 2 -> 13, of which waited for: 2 -> 10; matrix products, arithmetic and copies ran while one was open for 13% -> 0% of each run, Pallas kernels for 0% -> 13%
where the time goes in v1:
time: 165 us; the launch traced here: 162 us
  waiting for transfers between devices  60.7 us (37%)
  starting transfers between devices  43.3 us (26%)
  Pallas kernels  39.9 us (24%)
  blocking collectives  16 us (10%)
  local copies, waits for them, and re-layouts  2.04 us (1%)
    all_to_all x4, waiting for transfers between devices, exchange(): return lax.all_to_all(blocks, axes, split_axis=0, concat_axis=0, tiled=True)  32.3 us
    all_to_all x4, starting transfers between devices, exchange(): return lax.all_to_all(blocks, axes, split_axis=0, concat_axis=0, tiled=True)  23.6 us
    all_to_all x1, blocking collectives, exchange(): return lax.all_to_all(blocks, axes, split_axis=0, concat_axis=0, tiled=True)  16 us
    pallas_call x2, Pallas kernels, expert(): pl.pallas_call(expert_body, grid=(hidden // HID_BLOCK,), in_specs=[pl.Blo...  15.8 us
    ppermute x3, waiting for transfers between devices, on_device(): lax.ppermute(head_out, 'seq', shift(seqs, d))  11 us
    ppermute x3, starting transfers between devices, on_device(): far = [lax.ppermute(payload, 'zh', shift(zs, d)) for d in STEPS[1:]]  9.81 us
    ppermute x3, waiting for transfers between devices, on_device(): far = [lax.ppermute(payload, 'zh', shift(zs, d)) for d in STEPS[1:]]  8.7 us
    ppermute x3, waiting for transfers between devices, on_device(): lax.ppermute(s, 'zh', shift(zs, -d))  8.63 us
  transfers between devices with their start and end apart: 13, of which 10 were waited for; matrix products, arithmetic and copies ran while one was open for 0% of the time, Pallas kernels for 13%

profile of v1, /device:TPU:1, one launch (start us, length us, event | category | flops | bytes accessed | tf_op | source)
XLA Modules:
  0.0 161.9 jit_solution(12275413806399469665)
XLA Ops:
  0.0 7.9 %attention.1.refs_0_ = bf16[128,1024]{1,0:T(8,128)(2,1)} custom-call(s32[96,128]{1,0:T(8,128)} %bitcast.33, s32[4,128]{1,0:T(4,128)} %bitcast.37, bf16[128,1024]{1,0:T(8,128)(2,1)} %query_ref.1, bf16[128,1,128,256]{3,2,1,0:T(8,128)(2,1)} %cache_ref.1, bf16[128,256]{1,0:T(8,128)(2,1)} %bitcast.32), custom_call_target="tpu_custom_call" | custom-call | tf_op jit(solution)/shard_map/attention/pallas_call | solution.py:83
  16.8 7.1 %collective-permute-done.2.refs_3_ = bf16[128,1024]{1,0:T(8,128)(2,1)S(1)} collective-permute-done((bf16[128,1024]{1,0:T(8,128)(2,1)}, bf16[128,1024]{1,0:T(8,128)(2,1)S(1)}, u32[]{:S(2)}, u32[]{:S(2)}) %collective-permute-start.2) | collective-permute-done | bytes 262176 | tf_op jit(solution)/shard_map/ppermute | solution.py:371
  24.6 3.1 %project.1 = bf16[4,128,512]{2,1,0:T(8,128)(2,1)} custom-call(s32[1]{0:T(128)} %bitcast.1.seq_ref, bf16[128,1024]{1,0:T(8,128)(2,1)} %attention.1.refs_0_, bf16[128,1024]{1,0:T(8,128)(2,1)} %copy-done.7, bf16[128,1024]{1,0:T(8,128)(2,1)} %copy-done.8, bf16[128,1024]{1,0:T(8,128)(2,1)} %copy-done.9, bf16[1024,512]{1,0:T(8,128)(2,1)} %refs_4_.1), custom_call_target="tpu_custom_call" | custom-call | tf_op jit(solution)/shard_map/project/pallas_call | solution.py:111
  27.7 16.0 %all_to_all.25 = bf16[16,32,512]{2,1,0:T(8,128)(2,1)} all-to-all(bf16[16,32,512]{2,1,0:T(8,128)(2,1)} %bitcast.31), channel_id=1, replica_groups=mesh['zl'=2,'core'=2,'seq'=4,'zh'=4,'y'=4] {'seq','zl','core'}, dimensions={0} | all-to-all | bytes 1048576 | tf_op jit(solution)/shard_map/all_to_all | solution.py:338
  45.7 3.0 %collective-permute-start.3 = (bf16[32,2176]{1,0:T(8,128)(2,1)}, bf16[32,2176]{1,0:T(8,128)(2,1)S(1)}, u32[]{:S(2)}, u32[]{:S(2)}) collective-permute-start(bf16[32,2176]{1,0:T(8,128)(2,1)} %get-tuple-element.10.refs_1_), channel_id=1, source_target_pairs={{0,4},{4,8},{8,12},{12,0},{1,5},{5,9},{9,13},{13,1},{2,6},{6,10},{... | collective-permute-start | bytes 417800 | tf_op jit(solution)/shard_map/ppermute | solution.py:378
  48.7 2.4 %collective-permute-start.4 = (bf16[32,2176]{1,0:T(8,128)(2,1)}, bf16[32,2176]{1,0:T(8,128)(2,1)S(1)}, u32[]{:S(2)}, u32[]{:S(2)}) collective-permute-start(bf16[32,2176]{1,0:T(8,128)(2,1)} %get-tuple-element.10.refs_1_), channel_id=1, source_target_pairs={{0,12},{4,0},{8,4},{12,8},{1,13},{5,1},{9,5},{13,9},{2,14},{6,2},{... | collective-permute-start | bytes 417800 | tf_op jit(solution)/shard_map/ppermute | solution.py:378
  51.1 4.5 %collective-permute-start.5 = (bf16[32,2176]{1,0:T(8,128)(2,1)}, bf16[32,2176]{1,0:T(8,128)(2,1)S(1)}, u32[]{:S(2)}, u32[]{:S(2)}) collective-permute-start(bf16[32,2176]{1,0:T(8,128)(2,1)} %get-tuple-element.10.refs_1_), channel_id=1, source_target_pairs={{0,8},{4,12},{8,0},{12,4},{1,9},{5,13},{9,1},{13,5},{2,10},{6,14},... | collective-permute-start | bytes 417800 | tf_op jit(solution)/shard_map/ppermute | solution.py:378
  55.5 2.3 %collective-permute-done.4.refs_2_ = bf16[32,2176]{1,0:T(8,128)(2,1)S(1)} collective-permute-done((bf16[32,2176]{1,0:T(8,128)(2,1)}, bf16[32,2176]{1,0:T(8,128)(2,1)S(1)}, u32[]{:S(2)}, u32[]{:S(2)}) %collective-permute-start.4) | collective-permute-done | bytes 139296 | tf_op jit(solution)/shard_map/ppermute | solution.py:378
  57.8 6.4 %collective-permute-done.5.refs_3_ = bf16[32,2176]{1,0:T(8,128)(2,1)S(1)} collective-permute-done((bf16[32,2176]{1,0:T(8,128)(2,1)}, bf16[32,2176]{1,0:T(8,128)(2,1)S(1)}, u32[]{:S(2)}, u32[]{:S(2)}) %collective-permute-start.5) | collective-permute-done | bytes 139296 | tf_op jit(solution)/shard_map/ppermute | solution.py:378
  64.9 3.3 %dispatch.3 = bf16[384,2048]{1,0:T(8,128)(2,1)} custom-call(s32[1]{0:T(128)} %bitcast.refs_0_, bf16[32,2176]{1,0:T(8,128)(2,1)} %copy-done.4, bf16[32,2176]{1,0:T(8,128)(2,1)} %copy-done.5, bf16[32,2176]{1,0:T(8,128)(2,1)} %copy-done.6), custom_call_target="tpu_custom_call" | custom-call | tf_op jit(solution)/shard_map/dispatch/pallas_call | solution.py:207
  68.2 6.0 %all-to-all-start.3 = ((bf16[16,24,2048]{2,1,0:T(8,128)(2,1)}), bf16[16,24,2048]{2,1,0:T(8,128)(2,1)S(1)}, u32[]{:S(2)}, u32[]{:S(2)}) async-start(bf16[16,24,2048]{2,1,0:T(8,128)(2,1)} %bitcast.25), calls=%async_computation.3 | async-start | bytes 3145728 | tf_op jit(solution)/shard_map/all_to_all | solution.py:338
  74.2 2.4 %dispatch.2 = bf16[128,2048]{1,0:T(8,128)(2,1)} custom-call(s32[1]{0:T(128)} %bitcast.refs_0_, bf16[32,2176]{1,0:T(8,128)(2,1)} %get-tuple-element.10.refs_1_), custom_call_target="tpu_custom_call" | custom-call | tf_op jit(solution)/shard_map/dispatch/pallas_call | solution.py:207
  76.5 18.3 %all-to-all-done.3 = bf16[16,24,2048]{2,1,0:T(8,128)(2,1)S(1)} async-done(((bf16[16,24,2048]{2,1,0:T(8,128)(2,1)}), bf16[16,24,2048]{2,1,0:T(8,128)(2,1)S(1)}, u32[]{:S(2)}, u32[]{:S(2)}) %all-to-all-start.3) | async-done | bytes 1572896 | tf_op jit(solution)/shard_map/all_to_all | solution.py:338
  94.9 4.9 %all-to-all-start.1 = ((bf16[16,8,2048]{2,1,0:T(8,128)(2,1)}), bf16[16,8,2048]{2,1,0:T(8,128)(2,1)S(1)}, u32[]{:S(2)}, u32[]{:S(2)}) async-start(bf16[16,8,2048]{2,1,0:T(8,128)(2,1)} %bitcast.29), calls=%async_computation.1 | async-start | bytes 1048576 | tf_op jit(solution)/shard_map/all_to_all | solution.py:338
  99.8 9.2 %expert.3 = bf16[384,2048]{1,0:T(8,128)(2,1)} custom-call(bf16[384,2048]{1,0:T(8,128)(2,1)} %bitcast.23, bf16[1,2048,768]{2,1,0:T(8,128)(2,1)} %gate_ref.3, bf16[1,2048,768]{2,1,0:T(8,128)(2,1)} %up_ref.3, bf16[1,768,2048]{2,1,0:T(8,128)(2,1)} %down_ref.3), custom_call_target="tpu_custom_call" | custom-call | tf_op jit(solution)/shard_map/expert/pallas_call | solution.py:244
  109.0 6.7 %all-to-all-start.4 = ((bf16[16,24,2048]{2,1,0:T(8,128)(2,1)}), bf16[16,24,2048]{2,1,0:T(8,128)(2,1)S(1)}, u32[]{:S(2)}, u32[]{:S(2)}) async-start(bf16[16,24,2048]{2,1,0:T(8,128)(2,1)} %bitcast.24), calls=%async_computation.4 | async-start | bytes 3145728 | tf_op jit(solution)/shard_map/all_to_all | solution.py:338
  115.7 6.6 %expert.2 = bf16[128,2048]{1,0:T(8,128)(2,1)} custom-call(bf16[128,2048]{1,0:T(8,128)(2,1)} %bitcast.28, bf16[1,2048,768]{2,1,0:T(8,128)(2,1)} %gate_ref.3, bf16[1,2048,768]{2,1,0:T(8,128)(2,1)} %up_ref.3, bf16[1,768,2048]{2,1,0:T(8,128)(2,1)} %down_ref.3), custom_call_target="tpu_custom_call" | custom-call | tf_op jit(solution)/shard_map/expert/pallas_call | solution.py:244
  122.3 12.6 %all-to-all-done.4 = bf16[16,24,2048]{2,1,0:T(8,128)(2,1)S(1)} async-done(((bf16[16,24,2048]{2,1,0:T(8,128)(2,1)}), bf16[16,24,2048]{2,1,0:T(8,128)(2,1)S(1)}, u32[]{:S(2)}, u32[]{:S(2)}) %all-to-all-start.4) | async-done | bytes 1572896 | tf_op jit(solution)/shard_map/all_to_all | solution.py:338
  134.9 6.1 %all-to-all-start.2 = ((bf16[16,8,2048]{2,1,0:T(8,128)(2,1)}), bf16[16,8,2048]{2,1,0:T(8,128)(2,1)S(1)}, u32[]{:S(2)}, u32[]{:S(2)}) async-start(bf16[16,8,2048]{2,1,0:T(8,128)(2,1)} %bitcast.27), calls=%async_computation.2 | async-start | bytes 1048576 | tf_op jit(solution)/shard_map/all_to_all | solution.py:338
  141.0 3.0 %combine.1 = (bf16[32,2048]{1,0:T(8,128)(2,1)}, bf16[32,2048]{1,0:T(8,128)(2,1)}, bf16[32,2048]{1,0:T(8,128)(2,1)}) custom-call(s32[1]{0:T(128)} %bitcast.refs_0_, bf16[32,2176]{1,0:T(8,128)(2,1)} %copy-done.4, bf16[32,2176]{1,0:T(8,128)(2,1)} %copy-done.5, bf16[32,2176]{1,0:T(8,128)(2,1)} %copy-done.6, bf16[384,2048]{1,0:T(8,128)(2,1)} %bitcast.22), custom_call_target="tpu_custom_call" | custom-call | tf_op jit(solution)/shard_map/combine/pallas_call | solution.py:294
  146.4 2.5 %collective-permute-start.8 = (bf16[32,2048]{1,0:T(8,128)(2,1)}, bf16[32,2048]{1,0:T(8,128)(2,1)S(1)}, u32[]{:S(2)}, u32[]{:S(2)}) collective-permute-start(bf16[32,2048]{1,0:T(8,128)(2,1)} %get-tuple-element.14), channel_id=1, source_target_pairs={{0,8},{4,12},{8,0},{12,4},{1,9},{5,13},{9,1},{13,5},{2,10},{6,14},... | collective-permute-start | bytes 393224 | tf_op jit(solution)/shard_map/ppermute | solution.py:384
  150.3 3.1 %collective-permute-done.7.refs_5_ = bf16[32,2048]{1,0:T(8,128)(2,1)S(1)} collective-permute-done((bf16[32,2048]{1,0:T(8,128)(2,1)}, bf16[32,2048]{1,0:T(8,128)(2,1)S(1)}, u32[]{:S(2)}, u32[]{:S(2)}) %collective-permute-start.7) | collective-permute-done | bytes 131104 | tf_op jit(solution)/shard_map/ppermute | solution.py:384
  153.4 5.5 %collective-permute-done.8.refs_6_ = bf16[32,2048]{1,0:T(8,128)(2,1)S(1)} collective-permute-done((bf16[32,2048]{1,0:T(8,128)(2,1)}, bf16[32,2048]{1,0:T(8,128)(2,1)S(1)}, u32[]{:S(2)}, u32[]{:S(2)}) %collective-permute-start.8) | collective-permute-done | bytes 131104 | tf_op jit(solution)/shard_map/ppermute | solution.py:384
  159.5 2.4 %finish.1 = bf16[32,2048]{1,0:T(8,128)(2,1)} custom-call(s32[1]{0:T(128)} %bitcast.refs_0_, bf16[32,2176]{1,0:T(8,128)(2,1)} %get-tuple-element.10.refs_1_, bf16[128,2048]{1,0:T(8,128)(2,1)} %bitcast.26, bf16[32,2048]{1,0:T(8,128)(2,1)} %get-tuple-element.11.refs_3_, bf16[32,2048]{1,0:T(8,128)(2,1)} %copy-done.10, bf16[32,2048]{1,0:T(8,128)(2,1)} %copy-done.11, ...), custom_call_target="tpu_custom_call" | custom-call | tf_op jit(solution)/shard_map/finish/pallas_call | solution.py:318
  (38 shorter events, 16.8 us)
Async XLA Ops:
  7.9 7.3 %collective-permute-start = (bf16[128,1024]{1,0:T(8,128)(2,1)}, bf16[128,1024]{1,0:T(8,128)(2,1)S(1)}, u32[]{:S(2)}, u32[]{:S(2)}) collective-permute-start(bf16[128,1024]{1,0:T(8,128)(2,1)} %attention.1.refs_0_), channel_id=1, source_target_pairs={{0,16},{16,32},{32,48},{48,0},{1,17},{17,33},{33,49},{49,1},{2,18}... | collective-permute-start | bytes 786440 | tf_op jit(solution)/shard_map/ppermute | solution.py:371
  9.9 6.9 %collective-permute-start.1 = (bf16[128,1024]{1,0:T(8,128)(2,1)}, bf16[128,1024]{1,0:T(8,128)(2,1)S(1)}, u32[]{:S(2)}, u32[]{:S(2)}) collective-permute-start(bf16[128,1024]{1,0:T(8,128)(2,1)} %attention.1.refs_0_), channel_id=1, source_target_pairs={{0,48},{16,0},{32,16},{48,32},{1,49},{17,1},{33,17},{49,33},{2,50}... | collective-permute-start | bytes 786440 | tf_op jit(solution)/shard_map/ppermute | solution.py:371
  11.2 12.7 %collective-permute-start.2 = (bf16[128,1024]{1,0:T(8,128)(2,1)}, bf16[128,1024]{1,0:T(8,128)(2,1)S(1)}, u32[]{:S(2)}, u32[]{:S(2)}) collective-permute-start(bf16[128,1024]{1,0:T(8,128)(2,1)} %attention.1.refs_0_), channel_id=1, source_target_pairs={{0,32},{16,48},{32,0},{48,16},{1,33},{17,49},{33,1},{49,17},{2,34}... | collective-permute-start | bytes 786440 | tf_op jit(solution)/shard_map/ppermute | solution.py:371
  15.2 8.8 %copy-start.7 = (bf16[128,1024]{1,0:T(8,128)(2,1)}, bf16[128,1024]{1,0:T(8,128)(2,1)S(1)}, u32[]{:S(2)}) copy-start(bf16[128,1024]{1,0:T(8,128)(2,1)S(1)} %collective-permute-done.refs_1_) | copy-start | bytes 786436
  16.8 7.1 %copy-start.8 = (bf16[128,1024]{1,0:T(8,128)(2,1)}, bf16[128,1024]{1,0:T(8,128)(2,1)S(1)}, u32[]{:S(2)}) copy-start(bf16[128,1024]{1,0:T(8,128)(2,1)S(1)} %collective-permute-done.1.refs_2_) | copy-start | bytes 786436
  23.9 0.7 copy-start.9
  45.7 9.8 %collective-permute-start.3 = (bf16[32,2176]{1,0:T(8,128)(2,1)}, bf16[32,2176]{1,0:T(8,128)(2,1)S(1)}, u32[]{:S(2)}, u32[]{:S(2)}) collective-permute-start(bf16[32,2176]{1,0:T(8,128)(2,1)} %get-tuple-element.10.refs_1_), channel_id=1, source_target_pairs={{0,4},{4,8},{8,12},{12,0},{1,5},{5,9},{9,13},{13,1},{2,6},{6,10},{... | collective-permute-start | bytes 417800 | tf_op jit(solution)/shard_map/ppermute | solution.py:378
  48.7 9.1 %collective-permute-start.4 = (bf16[32,2176]{1,0:T(8,128)(2,1)}, bf16[32,2176]{1,0:T(8,128)(2,1)S(1)}, u32[]{:S(2)}, u32[]{:S(2)}) collective-permute-start(bf16[32,2176]{1,0:T(8,128)(2,1)} %get-tuple-element.10.refs_1_), channel_id=1, source_target_pairs={{0,12},{4,0},{8,4},{12,8},{1,13},{5,1},{9,5},{13,9},{2,14},{6,2},{... | collective-permute-start | bytes 417800 | tf_op jit(solution)/shard_map/ppermute | solution.py:378
  51.1 13.2 %collective-permute-start.5 = (bf16[32,2176]{1,0:T(8,128)(2,1)}, bf16[32,2176]{1,0:T(8,128)(2,1)S(1)}, u32[]{:S(2)}, u32[]{:S(2)}) collective-permute-start(bf16[32,2176]{1,0:T(8,128)(2,1)} %get-tuple-element.10.refs_1_), channel_id=1, source_target_pairs={{0,8},{4,12},{8,0},{12,4},{1,9},{5,13},{9,1},{13,5},{2,10},{6,14},... | collective-permute-start | bytes 417800 | tf_op jit(solution)/shard_map/ppermute | solution.py:378
  55.5 8.7 %copy-start.4 = (bf16[32,2176]{1,0:T(8,128)(2,1)}, bf16[32,2176]{1,0:T(8,128)(2,1)S(1)}, u32[]{:S(2)}) copy-start(bf16[32,2176]{1,0:T(8,128)(2,1)S(1)} %collective-permute-done.3.refs_1_) | copy-start | bytes 417796
  57.8 6.4 %copy-start.5 = (bf16[32,2176]{1,0:T(8,128)(2,1)}, bf16[32,2176]{1,0:T(8,128)(2,1)S(1)}, u32[]{:S(2)}) copy-start(bf16[32,2176]{1,0:T(8,128)(2,1)S(1)} %collective-permute-done.4.refs_2_) | copy-start | bytes 417796
  68.2 26.7 %all-to-all-start.3 = ((bf16[16,24,2048]{2,1,0:T(8,128)(2,1)}), bf16[16,24,2048]{2,1,0:T(8,128)(2,1)S(1)}, u32[]{:S(2)}, u32[]{:S(2)}) async-start(bf16[16,24,2048]{2,1,0:T(8,128)(2,1)} %bitcast.25), calls=%async_computation.3 | async-start | bytes 3145728 | tf_op jit(solution)/shard_map/all_to_all | solution.py:338
  94.9 4.9 %copy-start.1 = (bf16[16,24,2048]{2,1,0:T(8,128)(2,1)}, bf16[16,24,2048]{2,1,0:T(8,128)(2,1)S(1)}, u32[]{:S(2)}) copy-start(bf16[16,24,2048]{2,1,0:T(8,128)(2,1)S(1)} %all-to-all-done.3) | copy-start | bytes 4718596
  94.9 14.1 %all-to-all-start.1 = ((bf16[16,8,2048]{2,1,0:T(8,128)(2,1)}), bf16[16,8,2048]{2,1,0:T(8,128)(2,1)S(1)}, u32[]{:S(2)}, u32[]{:S(2)}) async-start(bf16[16,8,2048]{2,1,0:T(8,128)(2,1)} %bitcast.29), calls=%async_computation.1 | async-start | bytes 1048576 | tf_op jit(solution)/shard_map/all_to_all | solution.py:338
  109.0 6.7 %copy-start.3 = (bf16[16,8,2048]{2,1,0:T(8,128)(2,1)}, bf16[16,8,2048]{2,1,0:T(8,128)(2,1)S(1)}, u32[]{:S(2)}) copy-start(bf16[16,8,2048]{2,1,0:T(8,128)(2,1)S(1)} %all-to-all-done.1) | copy-start | bytes 1572868
  109.0 25.9 %all-to-all-start.4 = ((bf16[16,24,2048]{2,1,0:T(8,128)(2,1)}), bf16[16,24,2048]{2,1,0:T(8,128)(2,1)S(1)}, u32[]{:S(2)}, u32[]{:S(2)}) async-start(bf16[16,24,2048]{2,1,0:T(8,128)(2,1)} %bitcast.24), calls=%async_computation.4 | async-start | bytes 3145728 | tf_op jit(solution)/shard_map/all_to_all | solution.py:338
  134.9 6.1 %copy-start = (bf16[16,24,2048]{2,1,0:T(8,128)(2,1)}, bf16[16,24,2048]{2,1,0:T(8,128)(2,1)S(1)}, u32[]{:S(2)}) copy-start(bf16[16,24,2048]{2,1,0:T(8,128)(2,1)S(1)} %all-to-all-done.4) | copy-start | bytes 4718596
  134.9 15.3 %all-to-all-start.2 = ((bf16[16,8,2048]{2,1,0:T(8,128)(2,1)}), bf16[16,8,2048]{2,1,0:T(8,128)(2,1)S(1)}, u32[]{:S(2)}, u32[]{:S(2)}) async-start(bf16[16,8,2048]{2,1,0:T(8,128)(2,1)} %bitcast.27), calls=%async_computation.2 | async-start | bytes 1048576 | tf_op jit(solution)/shard_map/all_to_all | solution.py:338
  144.0 6.3 %collective-permute-start.6 = (bf16[32,2048]{1,0:T(8,128)(2,1)}, bf16[32,2048]{1,0:T(8,128)(2,1)S(1)}, u32[]{:S(2)}, u32[]{:S(2)}) collective-permute-start(bf16[32,2048]{1,0:T(8,128)(2,1)} %get-tuple-element.12), channel_id=1, source_target_pairs={{0,12},{4,0},{8,4},{12,8},{1,13},{5,1},{9,5},{13,9},{2,14},{6,2},{... | collective-permute-start | bytes 393224 | tf_op jit(solution)/shard_map/ppermute | solution.py:384
  145.8 7.6 %collective-permute-start.7 = (bf16[32,2048]{1,0:T(8,128)(2,1)}, bf16[32,2048]{1,0:T(8,128)(2,1)S(1)}, u32[]{:S(2)}, u32[]{:S(2)}) collective-permute-start(bf16[32,2048]{1,0:T(8,128)(2,1)} %get-tuple-element.13), channel_id=1, source_target_pairs={{0,4},{4,8},{8,12},{12,0},{1,5},{5,9},{9,13},{13,1},{2,6},{6,10},{... | collective-permute-start | bytes 393224 | tf_op jit(solution)/shard_map/ppermute | solution.py:384
  146.4 12.5 %collective-permute-start.8 = (bf16[32,2048]{1,0:T(8,128)(2,1)}, bf16[32,2048]{1,0:T(8,128)(2,1)S(1)}, u32[]{:S(2)}, u32[]{:S(2)}) collective-permute-start(bf16[32,2048]{1,0:T(8,128)(2,1)} %get-tuple-element.14), channel_id=1, source_target_pairs={{0,8},{4,12},{8,0},{12,4},{1,9},{5,13},{9,1},{13,5},{2,10},{6,14},... | collective-permute-start | bytes 393224 | tf_op jit(solution)/shard_map/ppermute | solution.py:384
  150.3 8.6 %copy-start.2 = (bf16[16,8,2048]{2,1,0:T(8,128)(2,1)}, bf16[16,8,2048]{2,1,0:T(8,128)(2,1)S(1)}, u32[]{:S(2)}) copy-start(bf16[16,8,2048]{2,1,0:T(8,128)(2,1)S(1)} %all-to-all-done.2) | copy-start | bytes 1572868
  150.3 8.6 %copy-start.10 = (bf16[32,2048]{1,0:T(8,128)(2,1)}, bf16[32,2048]{1,0:T(8,128)(2,1)S(1)}, u32[]{:S(2)}) copy-start(bf16[32,2048]{1,0:T(8,128)(2,1)S(1)} %collective-permute-done.6.refs_4_) | copy-start | bytes 393220
  153.4 5.5 %copy-start.11 = (bf16[32,2048]{1,0:T(8,128)(2,1)}, bf16[32,2048]{1,0:T(8,128)(2,1)S(1)}, u32[]{:S(2)}) copy-start(bf16[32,2048]{1,0:T(8,128)(2,1)S(1)} %collective-permute-done.7.refs_5_) | copy-start | bytes 393220
  (2 other events, 1.3 us)

commit v2 on v1

--- a/solution.py
+++ b/solution.py
@@ -9,11 +9,18 @@
 epsilon = 1e-06
 LANES = 128
 ATT_BLOCK = 32
-HID_BLOCK = 256
 MESH_AXES = ("zl", "core", "seq", "zh", "y")
 PLANE = ("seq", "y")
 HEADS = ("zl", "core")
 STEPS = (0, 1, 3, 2)
+
+
+def grant(mib):
+    return pltpu.CompilerParams(vmem_limit_bytes=mib * 2**20)
+
+
+def in_hbm(*arrays):
+    return [pltpu.with_memory_space_constraint(a, pltpu.HBM) for a in arrays]
 
 
 def iota(shape, dim):
@@ -93,8 +100,9 @@
         out_specs=pl.BlockSpec((block, width), lambda i: (i, 0)),
         out_shape=jax.ShapeDtypeStruct((rows, width), jnp.bfloat16),
         scratch_shapes=[pltpu.VMEM((rows, cache_pairs.shape[2]), jnp.float32)],
+        compiler_params=grant(24),
         name="attention",
-    )(slots, counts, queries, cache_pairs, fresh)
+    )(*in_hbm(slots, counts, queries, cache_pairs, fresh))
 
 
 def project_body(seq_ref, *refs):
@@ -113,6 +121,7 @@
         in_specs=[pl.BlockSpec(memory_space=pltpu.SMEM)]
         + [pl.BlockSpec(memory_space=pltpu.VMEM)] * (len(blocks) + 1),
         out_shape=jax.ShapeDtypeStruct((len(blocks), rows, weight.shape[1]), jnp.bfloat16),
+        compiler_params=grant(12),
         name="project",
     )(seq, *blocks, weight)
 
@@ -134,7 +143,9 @@
     for s in range(seqs):
         at = slice(s * width, (s + 1) * width)
         widened = residual_ref[:, at].astype(jnp.float32)
-        payload_ref[:, at] = (widened * factor * gain_ref[:, at]).astype(jnp.bfloat16)
+        normed = (widened * factor * gain_ref[:, at]).astype(jnp.bfloat16)
+        for z in range(payload_ref.shape[0]):
+            payload_ref[z, :, at] = normed
     top = routes_ref.shape[0]
     tail = jnp.concatenate(
         [
@@ -144,17 +155,20 @@
         ],
         axis=0,
     )
-    payload_ref[:, wide:] = tail.T.astype(jnp.bfloat16)
-
-
-def norm(parts, stream, gain, routes, codes):
+    tail = tail.T.astype(jnp.bfloat16)
+    for z in range(payload_ref.shape[0]):
+        payload_ref[z, :, wide:] = tail
+
+
+def norm(parts, stream, gain, routes, codes, copies):
     rows, wide = stream.shape
     return pl.pallas_call(
         norm_body,
         out_shape=[
             jax.ShapeDtypeStruct((rows, wide), jnp.bfloat16),
-            jax.ShapeDtypeStruct((rows, wide + LANES), jnp.bfloat16),
-        ],
+            pltpu.HBM((copies, rows, wide + LANES), jnp.bfloat16),
+        ],
+        compiler_params=grant(8),
         name="norm",
     )(parts, stream, gain, routes, codes)
 
@@ -190,50 +204,57 @@
     return jnp.where((slot == at) & (rank < capacity), code, 0.0)
 
 
-def dispatch_body(zh_ref, *refs, top, experts_shape, capacity):
-    *payload_refs, out_ref = refs
-    blocks = len(payload_refs)
+def dispatch_body(zh_ref, payload_ref, out_ref, code_ref, total_ref, *, steps, static):
+    planes, rows, _ = payload_ref.shape
     wide = out_ref.shape[1]
-    tail = jnp.concatenate([r[:, wide:].astype(jnp.float32) for r in payload_refs], axis=0)
-    code = placement(tail, zh_ref[0], blocks, top, experts_shape, capacity)
+    top = static["top"]
+    ats = [(zh_ref[0] + (planes - d)) & (planes - 1) for d in steps]
+    tail = jnp.concatenate([payload_ref[at, :, wide:].astype(jnp.float32) for at in ats], axis=0)
+    code = placement(tail, zh_ref[0], len(steps), **static)
     place = jnp.where(code > 0.0, 1.0, 0.0).T.astype(jnp.bfloat16)
-    tokens = jnp.concatenate([r[:, :wide] for r in payload_refs], axis=0)
+    tokens = jnp.concatenate([payload_ref[at, :, :wide] for at in ats], axis=0)
     out_ref[...] = jnp.dot(place, tokens, preferred_element_type=jnp.float32).astype(jnp.bfloat16)
-
-
-def dispatch(zh, payloads, wide, static):
+    code_ref[...] = code.astype(jnp.bfloat16)
+    lane = iota(tail.shape, 1)
+    listed = jnp.where((lane >= top) & (lane < 2 * top), tail, 0.0)
+    total_ref[...] = jnp.broadcast_to(jnp.sum(listed, axis=-1, keepdims=True), tail.shape)
+
+
+def dispatch(zh, payload, steps, static):
     seqs, _, ys = static["experts_shape"]
-    slots = seqs * ys * len(payloads) * static["capacity"]
-    out = pl.pallas_call(
-        lambda *refs: dispatch_body(*refs, **static),
-        in_specs=[pl.BlockSpec(memory_space=pltpu.SMEM)]
-        + [pl.BlockSpec(memory_space=pltpu.VMEM)] * len(payloads),
-        out_shape=jax.ShapeDtypeStruct((slots, wide), jnp.bfloat16),
+    rows, wide = payload.shape[1], payload.shape[2] - LANES
+    tokens, slots = rows * len(steps), seqs * ys * len(steps) * static["capacity"]
+    out, code, total = pl.pallas_call(
+        lambda *refs: dispatch_body(*refs, steps=steps, static=static),
+        in_specs=[
+            pl.BlockSpec(memory_space=pltpu.SMEM),
+            pl.BlockSpec(memory_space=pltpu.VMEM),
+        ],
+        out_shape=[
+            pltpu.HBM((slots, wide), jnp.bfloat16),
+            jax.ShapeDtypeStruct((tokens, slots), jnp.bfloat16),
+            jax.ShapeDtypeStruct((tokens, LANES), jnp.float32),
+        ],
+        compiler_params=grant(12),
         name="dispatch",
-    )(zh, *payloads)
-    return out.reshape(seqs * ys, -1, wide)
-
-
-def expert_body(rows_ref, gate_ref, up_ref, down_ref, out_ref, acc_ref):
-    step = pl.program_id(0)
+    )(zh, payload)
+    return out.reshape(seqs * ys, -1, wide), (code, total)
+
+
+def expert_body(rows_ref, gate_ref, up_hbm, down_hbm, out_ref, up_ref, down_ref, sems):
+    fetch_up = pltpu.make_async_copy(up_hbm.at[0], up_ref, sems.at[0])
+    fetch_down = pltpu.make_async_copy(down_hbm.at[0], down_ref, sems.at[1])
+    fetch_up.start()
+    fetch_down.start()
     rows = rows_ref[...]
     gate = jnp.dot(rows, gate_ref[0], preferred_element_type=jnp.float32)
-    up = jnp.dot(rows, up_ref[0], preferred_element_type=jnp.float32)
-    act = (gate / (1.0 + jnp.exp(-gate)) * up).astype(jnp.bfloat16)
-    part = jnp.dot(act, down_ref[0], preferred_element_type=jnp.float32)
-    last = pl.num_programs(0) - 1
-
-    @pl.when(step == 0)
-    def _():
-        acc_ref[...] = part
-
-    @pl.when((step > 0) & (step < last))
-    def _():
-        acc_ref[...] += part
-
-    @pl.when(step == last)
-    def _():
-        out_ref[...] = (acc_ref[...] + part).astype(jnp.bfloat16)
+    gate = gate / (1.0 + jnp.exp(-gate))
+    fetch_up.wait()
+    up = jnp.dot(rows, up_ref[...], preferred_element_type=jnp.float32)
+    act = (gate * up).astype(jnp.bfloat16)
+    fetch_down.wait()
+    part = jnp.dot(act, down_ref[...], preferred_element_type=jnp.float32)
+    out_ref[...] = part.astype(jnp.bfloat16)
 
 
 def expert(arrived, gate_weight, up_weight, down_weight):
@@ -241,93 +262,66 @@
     wide = shape[-1]
     rows = shape[0] * shape[1]
     hidden = gate_weight.shape[2]
+    up_weight, down_weight = in_hbm(up_weight, down_weight)
     out = pl.pallas_call(
         expert_body,
-        grid=(hidden // HID_BLOCK,),
         in_specs=[
-            pl.BlockSpec((rows, wide), lambda i: (0, 0)),
-            pl.BlockSpec((1, wide, HID_BLOCK), lambda i: (0, 0, i)),
-            pl.BlockSpec((1, wide, HID_BLOCK), lambda i: (0, 0, i)),
-            pl.BlockSpec((1, HID_BLOCK, wide), lambda i: (0, i, 0)),
-        ],
-        out_specs=pl.BlockSpec((rows, wide), lambda i: (0, 0)),
-        out_shape=jax.ShapeDtypeStruct((rows, wide), jnp.bfloat16),
-        scratch_shapes=[pltpu.VMEM((rows, wide), jnp.float32)],
+            pl.BlockSpec(memory_space=pltpu.VMEM),
+            pl.BlockSpec(memory_space=pltpu.VMEM),
+            pl.BlockSpec(memory_space=pl.ANY),
+            pl.BlockSpec(memory_space=pl.ANY),
+        ],
+        out_shape=pltpu.HBM((rows, wide), jnp.bfloat16),
+        scratch_shapes=[
+            pltpu.VMEM((wide, hidden), jnp.bfloat16),
+            pltpu.VMEM((hidden, wide), jnp.bfloat16),
+            pltpu.SemaphoreType.DMA((2,)),
+        ],
+        compiler_params=grant(30),
         name="expert",
     )(arrived.reshape(rows, wide), gate_weight, up_weight, down_weight)
     return out.reshape(shape)
 
 
-def mixed(zh_ref, tail, returned, blocks, static):
-    top = static["top"]
-    code = placement(tail, zh_ref[0], blocks, **static)
-    total = jnp.sum(
-        jnp.where(
-            (iota(tail.shape, 1) >= top) & (iota(tail.shape, 1) < 2 * top), tail, 0.0
-        ),
-        axis=-1,
-        keepdims=True,
-    )
-    part = jnp.dot(code.astype(jnp.bfloat16), returned, preferred_element_type=jnp.float32)
-    return part / total
-
-
-def combine_body(zh_ref, *refs, static):
-    *tail_refs, returned_ref, o0_ref, o1_ref, o2_ref = refs
-    outs = (o0_ref, o1_ref, o2_ref)
-    tail = jnp.concatenate([r[...].astype(jnp.float32) for r in tail_refs], axis=0)
-    part = mixed(zh_ref, tail, returned_ref[...], len(tail_refs), static)
-    rows = part.shape[0] // len(tail_refs)
+def mixed(code_ref, total_ref, returned_ref):
+    part = jnp.dot(code_ref[...], returned_ref[...], preferred_element_type=jnp.float32)
+    return part / total_ref[:, :1]
+
+
+def combine_body(code_ref, total_ref, returned_ref, *outs):
+    part = mixed(code_ref, total_ref, returned_ref)
+    rows = part.shape[0] // len(outs)
     for b, out_ref in enumerate(outs):
         out_ref[...] = part[b * rows : (b + 1) * rows].astype(jnp.bfloat16)
 
 
-def tail_spec(payload):
-    rows, wide = payload.shape
-    return pl.BlockSpec((rows, LANES), lambda i: (0, wide // LANES - 1))
-
-
-def combine(zh, payloads, returned, static):
+def combine(mix, returned, blocks):
     wide = returned.shape[-1]
-    rows = payloads[0].shape[0]
-    returned = returned.reshape(-1, wide)
+    rows = mix[0].shape[0] // blocks
     return pl.pallas_call(
-        lambda *refs: combine_body(*refs, static=static),
-        grid=(1,),
-        in_specs=[pl.BlockSpec(memory_space=pltpu.SMEM)]
-        + [tail_spec(p) for p in payloads]
-        + [pl.BlockSpec(returned.shape, lambda i: (0, 0))],
-        out_specs=[pl.BlockSpec((rows, wide), lambda i: (0, 0))] * len(payloads),
-        out_shape=[jax.ShapeDtypeStruct((rows, wide), jnp.bfloat16)] * len(payloads),
+        combine_body,
+        out_shape=[jax.ShapeDtypeStruct((rows, wide), jnp.bfloat16)] * blocks,
+        compiler_params=grant(8),
         name="combine",
-    )(zh, *payloads, returned)
-
-
-def finish_body(zh_ref, tail_ref, returned_ref, residual_ref, a_ref, b_ref, c_ref, out_ref, *, static):
-    tail = tail_ref[...].astype(jnp.float32)
-    part = mixed(zh_ref, tail, returned_ref[...], 1, static)
-    for ref in (a_ref, b_ref, c_ref, residual_ref):
+    )(*mix, returned.reshape(-1, wide))
+
+
+def finish_body(code_ref, total_ref, returned_ref, *refs):
+    *more, out_ref = refs
+    part = mixed(code_ref, total_ref, returned_ref)
+    for ref in more:
         part = part + ref[...].astype(jnp.float32)
     out_ref[...] = part.astype(jnp.bfloat16)
 
 
-def finish(zh, payload, returned, residual, others, static):
-    rows, wide = residual.shape
-    returned = returned.reshape(-1, wide)
-    row_spec = pl.BlockSpec((rows, wide), lambda i: (0, 0))
+def finish(mix, returned, *more):
+    wide = returned.shape[-1]
     return pl.pallas_call(
-        lambda *refs: finish_body(*refs, static=static),
-        grid=(1,),
-        in_specs=[
-            pl.BlockSpec(memory_space=pltpu.SMEM),
-            tail_spec(payload),
-            pl.BlockSpec(returned.shape, lambda i: (0, 0)),
-        ]
-        + [row_spec] * 4,
-        out_specs=row_spec,
-        out_shape=jax.ShapeDtypeStruct((rows, wide), jnp.bfloat16),
+        finish_body,
+        out_shape=jax.ShapeDtypeStruct(more[0].shape, jnp.bfloat16),
+        compiler_params=grant(8),
         name="finish",
-    )(zh, payload, returned, residual, *others)
+    )(*mix, returned.reshape(-1, wide), *more)
 
 
 def shift(size, by):
@@ -373,17 +367,21 @@
     parts = project(seq, head_blocks, output_weight)
     parts = exchange(parts.reshape(-1, rows, parts.shape[-1]), ("seq",) + HEADS)
     parts = parts.reshape(seqs, -1, rows, parts.shape[-1])
-    residual, payload = norm(parts, stream, norm_gain.reshape(1, -1), routes.T, gate_codes.T)
-
-    far = [lax.ppermute(payload, "zh", shift(zs, d)) for d in STEPS[1:]]
-    near_rows = exchange(dispatch(zh, [payload], wide, static), PLANE)
-    far_rows = exchange(dispatch(zh, far, wide, static), PLANE)
-    near_out = expert(near_rows, gate_weight, up_weight, down_weight)
-    far_out = exchange(expert(far_rows, gate_weight, up_weight, down_weight), PLANE)
-    sums = combine(zh, far, far_out, static)
+    residual, payload = norm(
+        parts, stream, norm_gain.reshape(1, -1), routes.T, gate_codes.T, zs
+    )
+    weights = (gate_weight, up_weight, down_weight)
+
+    gathered = exchange(payload, "zh")
+    near_rows, near_mix = dispatch(zh, payload, STEPS[:1], static)
+    far_rows, far_mix = dispatch(zh, gathered, STEPS[1:], static)
+    near_rows, far_rows = exchange(near_rows, PLANE), exchange(far_rows, PLANE)
+    near_out = expert(near_rows, *weights)
+    far_out = exchange(expert(far_rows, *weights), PLANE)
+    sums = combine(far_mix, far_out, len(STEPS) - 1)
     others = [lax.ppermute(s, "zh", shift(zs, -d)) for s, d in zip(sums, STEPS[1:])]
     near_out = exchange(near_out, PLANE)
-    return finish(zh, payload, near_out, residual, others, static)
+    return finish(near_mix, near_out, residual, *others)
 
 
 def solution(mesh):

time: 165 us -> 160 us (0.970)
  the two profiles are of different devices: /device:TPU:1 before, /device:TPU:34 now
where the time goes in v2:
time: 160 us
  waiting for transfers between devices  71.4 us (45%)
  starting transfers between devices  42.7 us (27%)
  Pallas kernels  31.5 us (20%)
  blocking collectives  12.8 us (8%)
    all_to_all x5, waiting for transfers between devices, exchange(): return lax.all_to_all(blocks, axes, split_axis=0, concat_axis=0, tiled=True)  51.5 us
    all_to_all x5, starting transfers between devices, exchange(): return lax.all_to_all(blocks, axes, split_axis=0, concat_axis=0, tiled=True)  34.5 us
    pallas_call x2, Pallas kernels, expert(): pl.pallas_call(expert_body, in_specs=[pl.BlockSpec(memory_space=pltpu.VME...  14.9 us
    all_to_all x1, blocking collectives, exchange(): return lax.all_to_all(blocks, axes, split_axis=0, concat_axis=0, tiled=True)  12.8 us
    ppermute x3, waiting for transfers between devices, on_device(): lax.ppermute(head_out, 'seq', shift(seqs, d))  11.1 us
    ppermute x3, waiting for transfers between devices, on_device(): lax.ppermute(s, 'zh', shift(zs, -d))  8.82 us
    pallas_call x1, Pallas kernels, attention(): pl.pallas_call(attention_body, grid=(rows // block,), in_specs=[pl.BlockS...  7.35 us
    pallas_call x2, Pallas kernels, dispatch(): pl.pallas_call(lambda *refs: dispatch_body(*refs, steps=steps, static=sta...  4.69 us
  transfers between devices with their start and end apart: 11, of which 9 were waited for; matrix products, arithmetic and copies ran while one was open for 0% of the time, Pallas kernels for 11%

profile of v2, /device:TPU:34, one launch (start us, length us, event | category | flops | bytes accessed | tf_op | source)
XLA Modules:
  0.0 159.5 jit_solution(2017327270727245508)
XLA Ops:
  0.0 7.3 %attention.1.refs_0_ = bf16[128,1024]{1,0:T(8,128)(2,1)S(1)} custom-call(s32[96,128]{1,0:T(8,128)} %bitcast.33, s32[4,128]{1,0:T(4,128)} %bitcast.34, bf16[128,1024]{1,0:T(8,128)(2,1)} %query_ref.1, bf16[128,1,128,256]{3,2,1,0:T(8,128)(2,1)} %cache_ref.1, bf16[128,256]{1,0:T(8,128)(2,1)} %bitcast.32), custom_call_target="tpu_custom_call" | custom-call | tf_op jit(solution)/shard_map/attention/pallas_call | solution.py:90
  7.4 2.2 %collective-permute-start.2 = (bf16[128,1024]{1,0:T(8,128)(2,1)S(1)}, bf16[128,1024]{1,0:T(8,128)(2,1)S(1)}, u32[]{:S(2)}, u32[]{:S(2)}) collective-permute-start(bf16[128,1024]{1,0:T(8,128)(2,1)S(1)} %attention.1.refs_0_), channel_id=1, source_target_pairs={{0,32},{16,48},{32,0},{48,16},{1,33},{17,49},{33,1},{49,17},{2,34}... | collective-permute-start | bytes 786440 | tf_op jit(solution)/shard_map/ppermute | solution.py:365
  9.6 1.4 collective-permute-start.1
  11.6 6.6 %collective-permute-done.2.refs_3_ = bf16[128,1024]{1,0:T(8,128)(2,1)S(1)} collective-permute-done((bf16[128,1024]{1,0:T(8,128)(2,1)S(1)}, bf16[128,1024]{1,0:T(8,128)(2,1)S(1)}, u32[]{:S(2)}, u32[]{:S(2)}) %collective-permute-start.2) | collective-permute-done | bytes 262176 | tf_op jit(solution)/shard_map/ppermute | solution.py:365
  18.2 4.4 %collective-permute-done.1.refs_2_ = bf16[128,1024]{1,0:T(8,128)(2,1)S(1)} collective-permute-done((bf16[128,1024]{1,0:T(8,128)(2,1)S(1)}, bf16[128,1024]{1,0:T(8,128)(2,1)S(1)}, u32[]{:S(2)}, u32[]{:S(2)}) %collective-permute-start.1) | collective-permute-done | bytes 262176 | tf_op jit(solution)/shard_map/ppermute | solution.py:365
  23.5 12.8 %all_to_all.30 = bf16[16,32,512]{2,1,0:T(8,128)(2,1)S(1)} all-to-all(bf16[16,32,512]{2,1,0:T(8,128)(2,1)S(1)} %bitcast.24), channel_id=1, replica_groups=mesh['zl'=2,'core'=2,'seq'=4,'zh'=4,'y'=4] {'seq','zl','core'}, dimensions={0} | all-to-all | bytes 1048576 | tf_op jit(solution)/shard_map/all_to_all | solution.py:332
  37.3 7.8 %all-to-all-start.3 = ((bf16[4,32,2176]{2,1,0:T(8,128)(2,1)}), bf16[4,32,2176]{2,1,0:T(8,128)(2,1)}, u32[]{:S(2)}, u32[]{:S(2)}) async-start(bf16[4,32,2176]{2,1,0:T(8,128)(2,1)} %get-tuple-element.16.refs_1_), calls=%async_computation.3 | async-start | bytes 1114112 | tf_op jit(solution)/shard_map/all_to_all | solution.py:332
  45.2 18.6 %all-to-all-done.3.refs_1_ = bf16[4,32,2176]{2,1,0:T(8,128)(2,1)} async-done(((bf16[4,32,2176]{2,1,0:T(8,128)(2,1)}), bf16[4,32,2176]{2,1,0:T(8,128)(2,1)}, u32[]{:S(2)}, u32[]{:S(2)}) %all-to-all-start.3) | async-done | bytes 557088 | tf_op jit(solution)/shard_map/all_to_all | solution.py:332
  63.8 3.2 %dispatch.3 = (bf16[384,2048]{1,0:T(8,128)(2,1)}, bf16[96,384]{1,0:T(8,128)(2,1)S(1)}, f32[96,128]{1,0:T(8,128)S(1)}) custom-call(s32[1]{0:T(128)} %bitcast.refs_0_, bf16[4,32,2176]{2,1,0:T(8,128)(2,1)} %all-to-all-done.3.refs_1_), custom_call_target="tpu_custom_call" | custom-call | tf_op jit(solution)/shard_map/dispatch/pallas_call | solution.py:227
  67.0 7.2 %all-to-all-start.4 = ((bf16[16,24,2048]{2,1,0:T(8,128)(2,1)}), bf16[16,24,2048]{2,1,0:T(8,128)(2,1)}, u32[]{:S(2)}, u32[]{:S(2)}) async-start(bf16[16,24,2048]{2,1,0:T(8,128)(2,1)} %bitcast.30), calls=%async_computation.4 | async-start | bytes 3145728 | tf_op jit(solution)/shard_map/all_to_all | solution.py:332
  74.2 1.0 copy-done.1
  75.3 1.5 dispatch.2
  76.7 18.1 %all-to-all-done.4 = bf16[16,24,2048]{2,1,0:T(8,128)(2,1)} async-done(((bf16[16,24,2048]{2,1,0:T(8,128)(2,1)}), bf16[16,24,2048]{2,1,0:T(8,128)(2,1)}, u32[]{:S(2)}, u32[]{:S(2)}) %all-to-all-start.4) | async-done | bytes 1572896 | tf_op jit(solution)/shard_map/all_to_all | solution.py:332
  94.8 6.9 %all-to-all-start.1 = ((bf16[16,8,2048]{2,1,0:T(8,128)(2,1)}), bf16[16,8,2048]{2,1,0:T(8,128)(2,1)}, u32[]{:S(2)}, u32[]{:S(2)}) async-start(bf16[16,8,2048]{2,1,0:T(8,128)(2,1)} %bitcast.31), calls=%async_computation.1 | async-start | bytes 1048576 | tf_op jit(solution)/shard_map/all_to_all | solution.py:332
  101.7 9.1 %expert.3 = bf16[384,2048]{1,0:T(8,128)(2,1)} custom-call(bf16[384,2048]{1,0:T(8,128)(2,1)} %bitcast.17.rows_ref, bf16[1,2048,768]{2,1,0:T(8,128)(2,1)S(1)} %copy-done, bf16[1,2048,768]{2,1,0:T(8,128)(2,1)} %up_hbm.3, bf16[1,768,2048]{2,1,0:T(8,128)(2,1)} %down_hbm.3), custom_call_target="tpu_custom_call" | custom-call | tf_op jit(solution)/shard_map/expert/pallas_call | solution.py:266
  110.8 7.3 %all-to-all-start.5 = ((bf16[16,24,2048]{2,1,0:T(8,128)(2,1)}), bf16[16,24,2048]{2,1,0:T(8,128)(2,1)}, u32[]{:S(2)}, u32[]{:S(2)}) async-start(bf16[16,24,2048]{2,1,0:T(8,128)(2,1)} %bitcast.28), calls=%async_computation.5 | async-start | bytes 3145728 | tf_op jit(solution)/shard_map/all_to_all | solution.py:332
  118.1 5.8 %expert.2 = bf16[128,2048]{1,0:T(8,128)(2,1)} custom-call(bf16[128,2048]{1,0:T(8,128)(2,1)} %bitcast.13.rows_ref, bf16[1,2048,768]{2,1,0:T(8,128)(2,1)S(1)} %copy-done, bf16[1,2048,768]{2,1,0:T(8,128)(2,1)} %up_hbm.3, bf16[1,768,2048]{2,1,0:T(8,128)(2,1)} %down_hbm.3), custom_call_target="tpu_custom_call" | custom-call | tf_op jit(solution)/shard_map/expert/pallas_call | solution.py:266
  123.9 12.7 %all-to-all-done.5 = bf16[16,24,2048]{2,1,0:T(8,128)(2,1)} async-done(((bf16[16,24,2048]{2,1,0:T(8,128)(2,1)}), bf16[16,24,2048]{2,1,0:T(8,128)(2,1)}, u32[]{:S(2)}, u32[]{:S(2)}) %all-to-all-start.5) | async-done | bytes 1572896 | tf_op jit(solution)/shard_map/all_to_all | solution.py:332
  136.7 5.3 %all-to-all-start.2 = ((bf16[16,8,2048]{2,1,0:T(8,128)(2,1)}), bf16[16,8,2048]{2,1,0:T(8,128)(2,1)S(1)}, u32[]{:S(2)}, u32[]{:S(2)}) async-start(bf16[16,8,2048]{2,1,0:T(8,128)(2,1)} %bitcast.29), calls=%async_computation.2 | async-start | bytes 1048576 | tf_op jit(solution)/shard_map/all_to_all | solution.py:332
  142.0 1.8 %combine.1 = (bf16[32,2048]{1,0:T(8,128)(2,1)S(1)}, bf16[32,2048]{1,0:T(8,128)(2,1)S(1)}, bf16[32,2048]{1,0:T(8,128)(2,1)S(1)}) custom-call(bf16[96,384]{1,0:T(8,128)(2,1)S(1)} %get-tuple-element.21.code_ref, f32[96,128]{1,0:T(8,128)S(1)} %get-tuple-element.22.total_ref, bf16[384,2048]{1,0:T(8,128)(2,1)} %bitcast.19.returned_ref), custom_call_target="tpu_custom_call" | custom-call | tf_op jit(solution)/shard_map/combine/pallas_call | solution.py:301
  144.8 2.0 %collective-permute-start.4 = (bf16[32,2048]{1,0:T(8,128)(2,1)S(1)}, bf16[32,2048]{1,0:T(8,128)(2,1)S(1)}, u32[]{:S(2)}, u32[]{:S(2)}) collective-permute-start(bf16[32,2048]{1,0:T(8,128)(2,1)S(1)} %get-tuple-element.25), channel_id=1, source_target_pairs={{0,4},{4,8},{8,12},{12,0},{1,5},{5,9},{9,13},{13,1},{2,6},{6,10},{... | collective-permute-start | bytes 393224 | tf_op jit(solution)/shard_map/ppermute | solution.py:382
  147.7 2.1 %all-to-all-done.2 = bf16[16,8,2048]{2,1,0:T(8,128)(2,1)S(1)} async-done(((bf16[16,8,2048]{2,1,0:T(8,128)(2,1)}), bf16[16,8,2048]{2,1,0:T(8,128)(2,1)S(1)}, u32[]{:S(2)}, u32[]{:S(2)}) %all-to-all-start.2) | async-done | bytes 524320 | tf_op jit(solution)/shard_map/all_to_all | solution.py:332
  149.8 2.5 %collective-permute-done.3.refs_1_ = bf16[32,2048]{1,0:T(8,128)(2,1)S(1)} collective-permute-done((bf16[32,2048]{1,0:T(8,128)(2,1)S(1)}, bf16[32,2048]{1,0:T(8,128)(2,1)S(1)}, u32[]{:S(2)}, u32[]{:S(2)}) %collective-permute-start.3) | collective-permute-done | bytes 131104 | tf_op jit(solution)/shard_map/ppermute | solution.py:382
  152.3 6.3 %collective-permute-done.4.refs_2_ = bf16[32,2048]{1,0:T(8,128)(2,1)S(1)} collective-permute-done((bf16[32,2048]{1,0:T(8,128)(2,1)S(1)}, bf16[32,2048]{1,0:T(8,128)(2,1)S(1)}, u32[]{:S(2)}, u32[]{:S(2)}) %collective-permute-start.4) | collective-permute-done | bytes 131104 | tf_op jit(solution)/shard_map/ppermute | solution.py:382
  (22 shorter events, 5.3 us)
Async XLA Ops:
  0.0 22.7 %copy-start.2 = (bf16[1024,512]{1,0:T(8,128)(2,1)S(1)}, bf16[1024,512]{1,0:T(8,128)(2,1)}, u32[]{:S(2)}) copy-start(bf16[1024,512]{1,0:T(8,128)(2,1)} %refs_4_.1) | copy-start | bytes 3145732
  7.4 28.9 %copy-start.3 = (bf16[32,2048]{1,0:T(8,128)(2,1)S(1)}, bf16[32,2048]{1,0:T(8,128)(2,1)}, u32[]{:S(2)}) copy-start(bf16[32,2048]{1,0:T(8,128)(2,1)} %stream_ref.1) | copy-start | bytes 393220
  7.4 28.9 %copy-start.4 = (f32[2048]{0:T(1024)S(1)}, f32[2048]{0:T(1024)}, u32[]{:S(2)}) copy-start(f32[2048]{0:T(1024)} %param.20) | copy-start | bytes 24580
  7.4 28.9 %copy-start.5 = (s32[32,8]{0,1:T(8,128)S(1)}, s32[32,8]{0,1:T(8,128)}, u32[]{:S(2)}) copy-start(s32[32,8]{0,1:T(8,128)} %param.21) | copy-start | bytes 3076
  7.4 28.9 %copy-start.6 = (s32[32,8]{0,1:T(8,128)S(1)}, s32[32,8]{0,1:T(8,128)}, u32[]{:S(2)}) copy-start(s32[32,8]{0,1:T(8,128)} %param.22) | copy-start | bytes 3076
  7.4 10.8 %collective-permute-start.2 = (bf16[128,1024]{1,0:T(8,128)(2,1)S(1)}, bf16[128,1024]{1,0:T(8,128)(2,1)S(1)}, u32[]{:S(2)}, u32[]{:S(2)}) collective-permute-start(bf16[128,1024]{1,0:T(8,128)(2,1)S(1)} %attention.1.refs_0_), channel_id=1, source_target_pairs={{0,32},{16,48},{32,0},{48,16},{1,33},{17,49},{33,1},{49,17},{2,34}... | collective-permute-start | bytes 786440 | tf_op jit(solution)/shard_map/ppermute | solution.py:365
  9.6 13.0 %collective-permute-start.1 = (bf16[128,1024]{1,0:T(8,128)(2,1)S(1)}, bf16[128,1024]{1,0:T(8,128)(2,1)S(1)}, u32[]{:S(2)}, u32[]{:S(2)}) collective-permute-start(bf16[128,1024]{1,0:T(8,128)(2,1)S(1)} %attention.1.refs_0_), channel_id=1, source_target_pairs={{0,48},{16,0},{32,16},{48,32},{1,49},{17,1},{33,17},{49,33},{2,50}... | collective-permute-start | bytes 786440 | tf_op jit(solution)/shard_map/ppermute | solution.py:365
  11.1 11.7 %collective-permute-start = (bf16[128,1024]{1,0:T(8,128)(2,1)S(1)}, bf16[128,1024]{1,0:T(8,128)(2,1)S(1)}, u32[]{:S(2)}, u32[]{:S(2)}) collective-permute-start(bf16[128,1024]{1,0:T(8,128)(2,1)S(1)} %attention.1.refs_0_), channel_id=1, source_target_pairs={{0,16},{16,32},{32,48},{48,0},{1,17},{17,33},{33,49},{49,1},{2,18}... | collective-permute-start | bytes 786440 | tf_op jit(solution)/shard_map/ppermute | solution.py:365
  37.3 64.3 %copy-start = (bf16[1,2048,768]{2,1,0:T(8,128)(2,1)S(1)}, bf16[1,2048,768]{2,1,0:T(8,128)(2,1)}, u32[]{:S(2)}) copy-start(bf16[1,2048,768]{2,1,0:T(8,128)(2,1)} %gate_ref.3) | copy-start | bytes 9437188
  37.3 26.4 %all-to-all-start.3 = ((bf16[4,32,2176]{2,1,0:T(8,128)(2,1)}), bf16[4,32,2176]{2,1,0:T(8,128)(2,1)}, u32[]{:S(2)}, u32[]{:S(2)}) async-start(bf16[4,32,2176]{2,1,0:T(8,128)(2,1)} %get-tuple-element.16.refs_1_), calls=%async_computation.3 | async-start | bytes 1114112 | tf_op jit(solution)/shard_map/all_to_all | solution.py:332
  67.0 27.8 %all-to-all-start.4 = ((bf16[16,24,2048]{2,1,0:T(8,128)(2,1)}), bf16[16,24,2048]{2,1,0:T(8,128)(2,1)}, u32[]{:S(2)}, u32[]{:S(2)}) async-start(bf16[16,24,2048]{2,1,0:T(8,128)(2,1)} %bitcast.30), calls=%async_computation.4 | async-start | bytes 3145728 | tf_op jit(solution)/shard_map/all_to_all | solution.py:332
  74.2 1.1 copy-start.1
  94.8 16.0 %all-to-all-start.1 = ((bf16[16,8,2048]{2,1,0:T(8,128)(2,1)}), bf16[16,8,2048]{2,1,0:T(8,128)(2,1)}, u32[]{:S(2)}, u32[]{:S(2)}) async-start(bf16[16,8,2048]{2,1,0:T(8,128)(2,1)} %bitcast.31), calls=%async_computation.1 | async-start | bytes 1048576 | tf_op jit(solution)/shard_map/all_to_all | solution.py:332
  110.8 25.9 %all-to-all-start.5 = ((bf16[16,24,2048]{2,1,0:T(8,128)(2,1)}), bf16[16,24,2048]{2,1,0:T(8,128)(2,1)}, u32[]{:S(2)}, u32[]{:S(2)}) async-start(bf16[16,24,2048]{2,1,0:T(8,128)(2,1)} %bitcast.28), calls=%async_computation.5 | async-start | bytes 3145728 | tf_op jit(solution)/shard_map/all_to_all | solution.py:332
  136.7 13.2 %all-to-all-start.2 = ((bf16[16,8,2048]{2,1,0:T(8,128)(2,1)}), bf16[16,8,2048]{2,1,0:T(8,128)(2,1)S(1)}, u32[]{:S(2)}, u32[]{:S(2)}) async-start(bf16[16,8,2048]{2,1,0:T(8,128)(2,1)} %bitcast.29), calls=%async_computation.2 | async-start | bytes 1048576 | tf_op jit(solution)/shard_map/all_to_all | solution.py:332
  143.8 8.5 %collective-permute-start.3 = (bf16[32,2048]{1,0:T(8,128)(2,1)S(1)}, bf16[32,2048]{1,0:T(8,128)(2,1)S(1)}, u32[]{:S(2)}, u32[]{:S(2)}) collective-permute-start(bf16[32,2048]{1,0:T(8,128)(2,1)S(1)} %get-tuple-element.24), channel_id=1, source_target_pairs={{0,12},{4,0},{8,4},{12,8},{1,13},{5,1},{9,5},{13,9},{2,14},{6,2},{... | collective-permute-start | bytes 393224 | tf_op jit(solution)/shard_map/ppermute | solution.py:382
  144.8 13.8 %collective-permute-start.4 = (bf16[32,2048]{1,0:T(8,128)(2,1)S(1)}, bf16[32,2048]{1,0:T(8,128)(2,1)S(1)}, u32[]{:S(2)}, u32[]{:S(2)}) collective-permute-start(bf16[32,2048]{1,0:T(8,128)(2,1)S(1)} %get-tuple-element.25), channel_id=1, source_target_pairs={{0,4},{4,8},{8,12},{12,0},{1,5},{5,9},{9,13},{13,1},{2,6},{6,10},{... | collective-permute-start | bytes 393224 | tf_op jit(solution)/shard_map/ppermute | solution.py:382
  146.8 11.8 %collective-permute-start.5 = (bf16[32,2048]{1,0:T(8,128)(2,1)S(1)}, bf16[32,2048]{1,0:T(8,128)(2,1)S(1)}, u32[]{:S(2)}, u32[]{:S(2)}) collective-permute-start(bf16[32,2048]{1,0:T(8,128)(2,1)S(1)} %get-tuple-element.26), channel_id=1, source_target_pairs={{0,8},{4,12},{8,0},{12,4},{1,9},{5,13},{9,1},{13,5},{2,10},{6,14},... | collective-permute-start | bytes 393224 | tf_op jit(solution)/shard_map/ppermute | solution.py:382

commit v3 on v2

--- a/solution.py
+++ b/solution.py
@@ -105,16 +105,16 @@
     )(*in_hbm(slots, counts, queries, cache_pairs, fresh))
 
 
-def project_body(seq_ref, *refs):
+def project_body(here_ref, *refs):
     *head_refs, weight_ref, out_ref = refs
     count = len(head_refs)
     weight = weight_ref[...]
     for step, head_ref in zip(STEPS, head_refs):
         part = jnp.dot(head_ref[...], weight, preferred_element_type=jnp.float32)
-        out_ref[(seq_ref[0] + (count - step)) & (count - 1)] = part.astype(jnp.bfloat16)
-
-
-def project(seq, blocks, weight):
+        out_ref[(here_ref[0] + (count - step)) & (count - 1)] = part.astype(jnp.bfloat16)
+
+
+def project(here, blocks, weight):
     rows = blocks[0].shape[0]
     return pl.pallas_call(
         project_body,
@@ -123,7 +123,7 @@
         out_shape=jax.ShapeDtypeStruct((len(blocks), rows, weight.shape[1]), jnp.bfloat16),
         compiler_params=grant(12),
         name="project",
-    )(seq, *blocks, weight)
+    )(here, *blocks, weight)
 
 
 def norm_body(parts_ref, stream_ref, gain_ref, routes_ref, codes_ref, residual_ref, payload_ref):
@@ -166,7 +166,7 @@
         norm_body,
         out_shape=[
             jax.ShapeDtypeStruct((rows, wide), jnp.bfloat16),
-            pltpu.HBM((copies, rows, wide + LANES), jnp.bfloat16),
+            jax.ShapeDtypeStruct((copies, rows, wide + LANES), jnp.bfloat16),
         ],
         compiler_params=grant(8),
         name="norm",
@@ -204,15 +204,16 @@
     return jnp.where((slot == at) & (rank < capacity), code, 0.0)
 
 
-def dispatch_body(zh_ref, payload_ref, out_ref, code_ref, total_ref, *, steps, static):
+def dispatch_body(here_ref, payload_ref, out_ref, code_ref, total_ref, *, static):
     planes, rows, _ = payload_ref.shape
     wide = out_ref.shape[1]
     top = static["top"]
-    ats = [(zh_ref[0] + (planes - d)) & (planes - 1) for d in steps]
-    tail = jnp.concatenate([payload_ref[at, :, wide:].astype(jnp.float32) for at in ats], axis=0)
-    code = placement(tail, zh_ref[0], len(steps), **static)
+    tail = jnp.concatenate(
+        [payload_ref[z, :, wide:].astype(jnp.float32) for z in range(planes)], axis=0
+    )
+    code = placement(tail, here_ref[1], planes, **static)
     place = jnp.where(code > 0.0, 1.0, 0.0).T.astype(jnp.bfloat16)
-    tokens = jnp.concatenate([payload_ref[at, :, :wide] for at in ats], axis=0)
+    tokens = jnp.concatenate([payload_ref[z, :, :wide] for z in range(planes)], axis=0)
     out_ref[...] = jnp.dot(place, tokens, preferred_element_type=jnp.float32).astype(jnp.bfloat16)
     code_ref[...] = code.astype(jnp.bfloat16)
     lane = iota(tail.shape, 1)
@@ -220,39 +221,36 @@
     total_ref[...] = jnp.broadcast_to(jnp.sum(listed, axis=-1, keepdims=True), tail.shape)
 
 
-def dispatch(zh, payload, steps, static):
+def dispatch(here, payload, static):
     seqs, _, ys = static["experts_shape"]
-    rows, wide = payload.shape[1], payload.shape[2] - LANES
-    tokens, slots = rows * len(steps), seqs * ys * len(steps) * static["capacity"]
+    planes, rows, wide = payload.shape
+    wide = wide - LANES
+    tokens, slots = planes * rows, seqs * ys * planes * static["capacity"]
     out, code, total = pl.pallas_call(
-        lambda *refs: dispatch_body(*refs, steps=steps, static=static),
+        lambda *refs: dispatch_body(*refs, static=static),
         in_specs=[
             pl.BlockSpec(memory_space=pltpu.SMEM),
             pl.BlockSpec(memory_space=pltpu.VMEM),
         ],
         out_shape=[
-            pltpu.HBM((slots, wide), jnp.bfloat16),
+            jax.ShapeDtypeStruct((slots, wide), jnp.bfloat16),
             jax.ShapeDtypeStruct((tokens, slots), jnp.bfloat16),
             jax.ShapeDtypeStruct((tokens, LANES), jnp.float32),
         ],
-        compiler_params=grant(12),
+        compiler_params=grant(16),
         name="dispatch",
-    )(zh, payload)
+    )(here, payload)
     return out.reshape(seqs * ys, -1, wide), (code, total)
 
 
-def expert_body(rows_ref, gate_ref, up_hbm, down_hbm, out_ref, up_ref, down_ref, sems):
-    fetch_up = pltpu.make_async_copy(up_hbm.at[0], up_ref, sems.at[0])
-    fetch_down = pltpu.make_async_copy(down_hbm.at[0], down_ref, sems.at[1])
-    fetch_up.start()
-    fetch_down.start()
+def expert_body(rows_ref, gate_ref, up_ref, down_hbm, out_ref, down_ref, sem):
+    fetch = pltpu.make_async_copy(down_hbm.at[0], down_ref, sem)
+    fetch.start()
     rows = rows_ref[...]
     gate = jnp.dot(rows, gate_ref[0], preferred_element_type=jnp.float32)
-    gate = gate / (1.0 + jnp.exp(-gate))
-    fetch_up.wait()
-    up = jnp.dot(rows, up_ref[...], preferred_element_type=jnp.float32)
-    act = (gate * up).astype(jnp.bfloat16)
-    fetch_down.wait()
+    up = jnp.dot(rows, up_ref[0], preferred_element_type=jnp.float32)
+    act = (gate / (1.0 + jnp.exp(-gate)) * up).astype(jnp.bfloat16)
+    fetch.wait()
     part = jnp.dot(act, down_ref[...], preferred_element_type=jnp.float32)
     out_ref[...] = part.astype(jnp.bfloat16)
 
@@ -261,67 +259,54 @@
     shape = arrived.shape
     wide = shape[-1]
     rows = shape[0] * shape[1]
-    hidden = gate_weight.shape[2]
-    up_weight, down_weight = in_hbm(up_weight, down_weight)
+    return pl.pallas_call(
+        expert_body,
+        in_specs=[pl.BlockSpec(memory_space=pltpu.VMEM)] * 3 + [pl.BlockSpec(memory_space=pl.ANY)],
+        out_shape=jax.ShapeDtypeStruct((rows, wide), jnp.bfloat16),
+        scratch_shapes=[
+            pltpu.VMEM(down_weight.shape[1:], jnp.bfloat16),
+            pltpu.SemaphoreType.DMA,
+        ],
+        compiler_params=grant(24),
+        name="expert",
+    )(
+        arrived.reshape(rows, wide),
+        pltpu.with_memory_space_constraint(gate_weight, pltpu.VMEM),
+        pltpu.with_memory_space_constraint(up_weight, pltpu.VMEM),
+        *in_hbm(down_weight),
+    ).reshape(shape)
+
+
+def combine_body(code_ref, total_ref, returned_ref, out_ref):
+    part = jnp.dot(code_ref[...], returned_ref[...], preferred_element_type=jnp.float32)
+    out_ref[...] = (part / total_ref[:, :1]).astype(jnp.bfloat16)
+
+
+def combine(code, total, returned, planes):
+    wide = returned.shape[-1]
     out = pl.pallas_call(
-        expert_body,
-        in_specs=[
-            pl.BlockSpec(memory_space=pltpu.VMEM),
-            pl.BlockSpec(memory_space=pltpu.VMEM),
-            pl.BlockSpec(memory_space=pl.ANY),
-            pl.BlockSpec(memory_space=pl.ANY),
-        ],
-        out_shape=pltpu.HBM((rows, wide), jnp.bfloat16),
-        scratch_shapes=[
-            pltpu.VMEM((wide, hidden), jnp.bfloat16),
-            pltpu.VMEM((hidden, wide), jnp.bfloat16),
-            pltpu.SemaphoreType.DMA((2,)),
-        ],
-        compiler_params=grant(30),
-        name="expert",
-    )(arrived.reshape(rows, wide), gate_weight, up_weight, down_weight)
-    return out.reshape(shape)
-
-
-def mixed(code_ref, total_ref, returned_ref):
-    part = jnp.dot(code_ref[...], returned_ref[...], preferred_element_type=jnp.float32)
-    return part / total_ref[:, :1]
-
-
-def combine_body(code_ref, total_ref, returned_ref, *outs):
-    part = mixed(code_ref, total_ref, returned_ref)
-    rows = part.shape[0] // len(outs)
-    for b, out_ref in enumerate(outs):
-        out_ref[...] = part[b * rows : (b + 1) * rows].astype(jnp.bfloat16)
-
-
-def combine(mix, returned, blocks):
-    wide = returned.shape[-1]
-    rows = mix[0].shape[0] // blocks
-    return pl.pallas_call(
         combine_body,
-        out_shape=[jax.ShapeDtypeStruct((rows, wide), jnp.bfloat16)] * blocks,
-        compiler_params=grant(8),
+        out_shape=jax.ShapeDtypeStruct((code.shape[0], wide), jnp.bfloat16),
+        compiler_params=grant(10),
         name="combine",
-    )(*mix, returned.reshape(-1, wide))
-
-
-def finish_body(code_ref, total_ref, returned_ref, *refs):
-    *more, out_ref = refs
-    part = mixed(code_ref, total_ref, returned_ref)
-    for ref in more:
-        part = part + ref[...].astype(jnp.float32)
+    )(code, total, returned.reshape(-1, wide))
+    return out.reshape(planes, -1, wide)
+
+
+def finish_body(residual_ref, sums_ref, out_ref):
+    part = residual_ref[...].astype(jnp.float32)
+    for z in range(sums_ref.shape[0]):
+        part = part + sums_ref[z].astype(jnp.float32)
     out_ref[...] = part.astype(jnp.bfloat16)
 
 
-def finish(mix, returned, *more):
-    wide = returned.shape[-1]
+def finish(residual, sums):
     return pl.pallas_call(
         finish_body,
-        out_shape=jax.ShapeDtypeStruct(more[0].shape, jnp.bfloat16),
+        out_shape=jax.ShapeDtypeStruct(residual.shape, jnp.bfloat16),
         compiler_params=grant(8),
         name="finish",
-    )(*mix, returned.reshape(-1, wide), *more)
+    )(residual, sums)
 
 
 def shift(size, by):
@@ -349,8 +334,7 @@
 ):
     rows, wide = stream.shape
     seqs, zs, ys = (lax.axis_size(a) for a in ("seq", "zh", "y"))
-    seq = lax.axis_index("seq").astype(jnp.int32).reshape(1)
-    zh = lax.axis_index("zh").astype(jnp.int32).reshape(1)
+    here = jnp.stack([lax.axis_index("seq"), lax.axis_index("zh")]).astype(jnp.int32)
     experts = seqs * zs * ys
     static = dict(
         top=routes.shape[1],
@@ -364,24 +348,16 @@
     head_blocks = [head_out] + [
         lax.ppermute(head_out, "seq", shift(seqs, d)) for d in STEPS[1:]
     ]
-    parts = project(seq, head_blocks, output_weight)
+    parts = project(here, head_blocks, output_weight)
     parts = exchange(parts.reshape(-1, rows, parts.shape[-1]), ("seq",) + HEADS)
     parts = parts.reshape(seqs, -1, rows, parts.shape[-1])
     residual, payload = norm(
         parts, stream, norm_gain.reshape(1, -1), routes.T, gate_codes.T, zs
     )
-    weights = (gate_weight, up_weight, down_weight)
-
-    gathered = exchange(payload, "zh")
-    near_rows, near_mix = dispatch(zh, payload, STEPS[:1], static)
-    far_rows, far_mix = dispatch(zh, gathered, STEPS[1:], static)
-    near_rows, far_rows = exchange(near_rows, PLANE), exchange(far_rows, PLANE)
-    near_out = expert(near_rows, *weights)
-    far_out = exchange(expert(far_rows, *weights), PLANE)
-    sums = combine(far_mix, far_out, len(STEPS) - 1)
-    others = [lax.ppermute(s, "zh", shift(zs, -d)) for s, d in zip(sums, STEPS[1:])]
-    near_out = exchange(near_out, PLANE)
-    return finish(near_mix, near_out, residual, *others)
+    sent, mix = dispatch(here, exchange(payload, "zh"), static)
+    made = expert(exchange(sent, PLANE), gate_weight, up_weight, down_weight)
+    sums = combine(*mix, exchange(made, PLANE), zs)
+    return finish(residual, exchange(sums, "zh"))
 
 
 def solution(mesh):

time: 160 us -> 154 us (0.963)
  the two profiles are of different devices: /device:TPU:34 before, /device:TPU:8 now
where the time goes in v3:
time: 154 us
  blocking collectives  120 us (78%)
  Pallas kernels  18.6 us (12%)
  waiting for transfers between devices  10.2 us (7%)
  starting transfers between devices  5.14 us (3%)
    all_to_all x5, blocking collectives, exchange(): return lax.all_to_all(blocks, axes, split_axis=0, concat_axis=0, tiled=True)  120 us
    ppermute x3, waiting for transfers between devices, on_device(): lax.ppermute(head_out, 'seq', shift(seqs, d))  10.2 us
    pallas_call x1, Pallas kernels, attention(): pl.pallas_call(attention_body, grid=(rows // block,), in_specs=[pl.BlockS...  7.35 us
    pallas_call x1, Pallas kernels, expert(): pl.pallas_call(expert_body, in_specs=[pl.BlockSpec(memory_space=pltpu.VME...  6.77 us
    ppermute x3, starting transfers between devices, on_device(): lax.ppermute(head_out, 'seq', shift(seqs, d))  5.14 us
  transfers between devices with their start and end apart: 3, of which 2 were waited for; matrix products, arithmetic and copies ran while one was open for 0% of the time, Pallas kernels for 0%

profile of v3, /device:TPU:8, one launch (start us, length us, event | category | flops | bytes accessed | tf_op | source)
XLA Modules:
  0.0 153.9 jit_solution(9270903181008275599)
XLA Ops:
  0.0 7.3 %attention.1.refs_0_ = bf16[128,1024]{1,0:T(8,128)(2,1)S(1)} custom-call(s32[96,128]{1,0:T(8,128)} %bitcast.30, s32[4,128]{1,0:T(4,128)} %bitcast.31, bf16[128,1024]{1,0:T(8,128)(2,1)} %query_ref.1, bf16[128,1,128,256]{3,2,1,0:T(8,128)(2,1)} %cache_ref.1, bf16[128,256]{1,0:T(8,128)(2,1)} %bitcast.29), custom_call_target="tpu_custom_call" | custom-call | tf_op jit(solution)/shard_map/attention/pallas_call | solution.py:90
  7.4 0.0 copy-start.3
  7.4 0.0 copy-start.4
  7.4 0.0 copy-start.5
  7.4 0.0 copy-start.6
  7.4 3.1 %collective-permute-start.2 = (bf16[128,1024]{1,0:T(8,128)(2,1)S(1)}, bf16[128,1024]{1,0:T(8,128)(2,1)S(1)}, u32[]{:S(2)}, u32[]{:S(2)}) collective-permute-start(bf16[128,1024]{1,0:T(8,128)(2,1)S(1)} %attention.1.refs_0_), channel_id=1, source_target_pairs={{0,32},{16,48},{32,0},{48,16},{1,33},{17,49},{33,1},{49,17},{2,34}... | collective-permute-start | bytes 786440 | tf_op jit(solution)/shard_map/ppermute | solution.py:349
  10.5 1.1 collective-permute-start.1
  11.7 0.9 collective-permute-start
  12.5 0.1 pad_add_fusion.here_ref.refs_0_
  12.6 5.6 %collective-permute-done.2.refs_3_ = bf16[128,1024]{1,0:T(8,128)(2,1)S(1)} collective-permute-done((bf16[128,1024]{1,0:T(8,128)(2,1)S(1)}, bf16[128,1024]{1,0:T(8,128)(2,1)S(1)}, u32[]{:S(2)}, u32[]{:S(2)}) %collective-permute-start.2) | collective-permute-done | bytes 262176 | tf_op jit(solution)/shard_map/ppermute | solution.py:349
  18.2 4.6 %collective-permute-done.1.refs_2_ = bf16[128,1024]{1,0:T(8,128)(2,1)S(1)} collective-permute-done((bf16[128,1024]{1,0:T(8,128)(2,1)S(1)}, bf16[128,1024]{1,0:T(8,128)(2,1)S(1)}, u32[]{:S(2)}, u32[]{:S(2)}) %collective-permute-start.1) | collective-permute-done | bytes 262176 | tf_op jit(solution)/shard_map/ppermute | solution.py:349
  22.8 1.3 project.1
  24.1 16.3 %all_to_all.25 = bf16[16,32,512]{2,1,0:T(8,128)(2,1)S(1)} all-to-all(bf16[16,32,512]{2,1,0:T(8,128)(2,1)S(1)} %bitcast.24), channel_id=1, replica_groups=mesh['zl'=2,'core'=2,'seq'=4,'zh'=4,'y'=4] {'seq','zl','core'}, dimensions={0} | all-to-all | bytes 1048576 | tf_op jit(solution)/shard_map/all_to_all | solution.py:317
  40.3 0.0 copy-start
  40.3 0.0 copy-start.1
  40.4 0.2 norm.1
  40.6 25.1 %all_to_all.26.refs_1_ = bf16[4,32,2176]{2,1,0:T(8,128)(2,1)S(1)} all-to-all(bf16[4,32,2176]{2,1,0:T(8,128)(2,1)S(1)} %get-tuple-element.11), channel_id=1, replica_groups=mesh['zl'=2,'core'=2,'seq'=4,'zh'=4,'y'=4] {'zh'}, dimensions={0} | all-to-all | bytes 1114112 | tf_op jit(solution)/shard_map/all_to_all | solution.py:317
  65.7 1.8 %dispatch.1 = (bf16[512,2048]{1,0:T(8,128)(2,1)S(1)}, bf16[128,512]{1,0:T(8,128)(2,1)S(1)}, f32[128,128]{1,0:T(8,128)S(1)}) custom-call(s32[2]{0:T(128)S(1)} %pad_add_fusion.here_ref.refs_0_, bf16[4,32,2176]{2,1,0:T(8,128)(2,1)S(1)} %all_to_all.26.refs_1_), custom_call_target="tpu_custom_call" | custom-call | tf_op jit(solution)/shard_map/dispatch/pallas_call | solution.py:229
  67.5 28.8 %all_to_all.27 = bf16[16,32,2048]{2,1,0:T(8,128)(2,1)S(1)} all-to-all(bf16[16,32,2048]{2,1,0:T(8,128)(2,1)S(1)} %bitcast.22), channel_id=1, replica_groups=mesh['zl'=2,'core'=2,'seq'=4,'zh'=4,'y'=4] {'seq','y'}, dimensions={0} | all-to-all | bytes 4194304 | tf_op jit(solution)/shard_map/all_to_all | solution.py:317
  96.3 6.8 %expert.1 = bf16[512,2048]{1,0:T(8,128)(2,1)S(1)} custom-call(bf16[512,2048]{1,0:T(8,128)(2,1)S(1)} %bitcast.20, bf16[1,2048,768]{2,1,0:T(8,128)(2,1)S(1)} %copy-done, bf16[1,2048,768]{2,1,0:T(8,128)(2,1)S(1)} %copy-done.1, bf16[1,768,2048]{2,1,0:T(8,128)(2,1)} %down_hbm.1), custom_call_target="tpu_custom_call" | custom-call | tf_op jit(solution)/shard_map/expert/pallas_call | solution.py:262
  103.0 27.0 %all_to_all.28 = bf16[16,32,2048]{2,1,0:T(8,128)(2,1)S(1)} all-to-all(bf16[16,32,2048]{2,1,0:T(8,128)(2,1)S(1)} %bitcast.21), channel_id=1, replica_groups=mesh['zl'=2,'core'=2,'seq'=4,'zh'=4,'y'=4] {'seq','y'}, dimensions={0} | all-to-all | bytes 4194304 | tf_op jit(solution)/shard_map/all_to_all | solution.py:317
  130.0 0.4 combine.1
  130.5 22.7 %all_to_all.29.sums_ref = bf16[4,32,2048]{2,1,0:T(8,128)(2,1)S(1)} all-to-all(bf16[4,32,2048]{2,1,0:T(8,128)(2,1)S(1)} %bitcast.25), channel_id=1, replica_groups=mesh['zl'=2,'core'=2,'seq'=4,'zh'=4,'y'=4] {'zh'}, dimensions={0} | all-to-all | bytes 1048576 | tf_op jit(solution)/shard_map/all_to_all | solution.py:317
  153.2 0.7 finish.1
  (9 shorter events, 0.0 us)
Async XLA Ops:
  0.0 22.8 %copy-start.2 = (bf16[1024,512]{1,0:T(8,128)(2,1)S(1)}, bf16[1024,512]{1,0:T(8,128)(2,1)}, u32[]{:S(2)}) copy-start(bf16[1024,512]{1,0:T(8,128)(2,1)} %refs_4_.1) | copy-start | bytes 3145732
  7.4 33.0 %copy-start.3 = (bf16[32,2048]{1,0:T(8,128)(2,1)S(1)}, bf16[32,2048]{1,0:T(8,128)(2,1)}, u32[]{:S(2)}) copy-start(bf16[32,2048]{1,0:T(8,128)(2,1)} %stream_ref.1) | copy-start | bytes 393220
  7.4 33.0 %copy-start.4 = (f32[2048]{0:T(1024)S(1)}, f32[2048]{0:T(1024)}, u32[]{:S(2)}) copy-start(f32[2048]{0:T(1024)} %param.20) | copy-start | bytes 24580
  7.4 32.9 %copy-start.5 = (s32[32,8]{0,1:T(8,128)S(1)}, s32[32,8]{0,1:T(8,128)}, u32[]{:S(2)}) copy-start(s32[32,8]{0,1:T(8,128)} %param.21) | copy-start | bytes 3076
  7.4 32.9 %copy-start.6 = (s32[32,8]{0,1:T(8,128)S(1)}, s32[32,8]{0,1:T(8,128)}, u32[]{:S(2)}) copy-start(s32[32,8]{0,1:T(8,128)} %param.22) | copy-start | bytes 3076
  7.4 10.8 %collective-permute-start.2 = (bf16[128,1024]{1,0:T(8,128)(2,1)S(1)}, bf16[128,1024]{1,0:T(8,128)(2,1)S(1)}, u32[]{:S(2)}, u32[]{:S(2)}) collective-permute-start(bf16[128,1024]{1,0:T(8,128)(2,1)S(1)} %attention.1.refs_0_), channel_id=1, source_target_pairs={{0,32},{16,48},{32,0},{48,16},{1,33},{17,49},{33,1},{49,17},{2,34}... | collective-permute-start | bytes 786440 | tf_op jit(solution)/shard_map/ppermute | solution.py:349
  10.5 12.3 %collective-permute-start.1 = (bf16[128,1024]{1,0:T(8,128)(2,1)S(1)}, bf16[128,1024]{1,0:T(8,128)(2,1)S(1)}, u32[]{:S(2)}, u32[]{:S(2)}) collective-permute-start(bf16[128,1024]{1,0:T(8,128)(2,1)S(1)} %attention.1.refs_0_), channel_id=1, source_target_pairs={{0,48},{16,0},{32,16},{48,32},{1,49},{17,1},{33,17},{49,33},{2,50}... | collective-permute-start | bytes 786440 | tf_op jit(solution)/shard_map/ppermute | solution.py:349
  11.7 11.1 %collective-permute-start = (bf16[128,1024]{1,0:T(8,128)(2,1)S(1)}, bf16[128,1024]{1,0:T(8,128)(2,1)S(1)}, u32[]{:S(2)}, u32[]{:S(2)}) collective-permute-start(bf16[128,1024]{1,0:T(8,128)(2,1)S(1)} %attention.1.refs_0_), channel_id=1, source_target_pairs={{0,16},{16,32},{32,48},{48,0},{1,17},{17,33},{33,49},{49,1},{2,18}... | collective-permute-start | bytes 786440 | tf_op jit(solution)/shard_map/ppermute | solution.py:349
  40.3 55.9 %copy-start = (bf16[1,2048,768]{2,1,0:T(8,128)(2,1)S(1)}, bf16[1,2048,768]{2,1,0:T(8,128)(2,1)}, u32[]{:S(2)}) copy-start(bf16[1,2048,768]{2,1,0:T(8,128)(2,1)} %gate_ref.1) | copy-start | bytes 9437188
  40.3 55.9 %copy-start.1 = (bf16[1,2048,768]{2,1,0:T(8,128)(2,1)S(1)}, bf16[1,2048,768]{2,1,0:T(8,128)(2,1)}, u32[]{:S(2)}) copy-start(bf16[1,2048,768]{2,1,0:T(8,128)(2,1)} %up_ref.1) | copy-start | bytes 9437188

commit v4 on v3

--- a/solution.py
+++ b/solution.py
@@ -144,8 +144,7 @@
         at = slice(s * width, (s + 1) * width)
         widened = residual_ref[:, at].astype(jnp.float32)
         normed = (widened * factor * gain_ref[:, at]).astype(jnp.bfloat16)
-        for z in range(payload_ref.shape[0]):
-            payload_ref[z, :, at] = normed
+        payload_ref[:, at] = normed
     top = routes_ref.shape[0]
     tail = jnp.concatenate(
         [
@@ -155,18 +154,16 @@
         ],
         axis=0,
     )
-    tail = tail.T.astype(jnp.bfloat16)
-    for z in range(payload_ref.shape[0]):
-        payload_ref[z, :, wide:] = tail
-
-
-def norm(parts, stream, gain, routes, codes, copies):
+    payload_ref[:, wide:] = tail.T.astype(jnp.bfloat16)
+
+
+def norm(parts, stream, gain, routes, codes):
     rows, wide = stream.shape
     return pl.pallas_call(
         norm_body,
         out_shape=[
             jax.ShapeDtypeStruct((rows, wide), jnp.bfloat16),
-            jax.ShapeDtypeStruct((copies, rows, wide + LANES), jnp.bfloat16),
+            jax.ShapeDtypeStruct((rows, wide + LANES), jnp.bfloat16),
         ],
         compiler_params=grant(8),
         name="norm",
@@ -204,16 +201,15 @@
     return jnp.where((slot == at) & (rank < capacity), code, 0.0)
 
 
-def dispatch_body(here_ref, payload_ref, out_ref, code_ref, total_ref, *, static):
-    planes, rows, _ = payload_ref.shape
+def dispatch_body(here_ref, *refs, static):
+    *payload_refs, out_ref, code_ref, total_ref = refs
+    planes = len(payload_refs)
     wide = out_ref.shape[1]
     top = static["top"]
-    tail = jnp.concatenate(
-        [payload_ref[z, :, wide:].astype(jnp.float32) for z in range(planes)], axis=0
-    )
+    tail = jnp.concatenate([r[:, wide:].astype(jnp.float32) for r in payload_refs], axis=0)
     code = placement(tail, here_ref[1], planes, **static)
     place = jnp.where(code > 0.0, 1.0, 0.0).T.astype(jnp.bfloat16)
-    tokens = jnp.concatenate([payload_ref[z, :, :wide] for z in range(planes)], axis=0)
+    tokens = jnp.concatenate([r[:, :wide] for r in payload_refs], axis=0)
     out_ref[...] = jnp.dot(place, tokens, preferred_element_type=jnp.float32).astype(jnp.bfloat16)
     code_ref[...] = code.astype(jnp.bfloat16)
     lane = iota(tail.shape, 1)
@@ -221,17 +217,14 @@
     total_ref[...] = jnp.broadcast_to(jnp.sum(listed, axis=-1, keepdims=True), tail.shape)
 
 
-def dispatch(here, payload, static):
+def dispatch(here, payloads, static):
     seqs, _, ys = static["experts_shape"]
-    planes, rows, wide = payload.shape
-    wide = wide - LANES
+    planes, rows, wide = len(payloads), payloads[0].shape[0], payloads[0].shape[1] - LANES
     tokens, slots = planes * rows, seqs * ys * planes * static["capacity"]
     out, code, total = pl.pallas_call(
         lambda *refs: dispatch_body(*refs, static=static),
-        in_specs=[
-            pl.BlockSpec(memory_space=pltpu.SMEM),
-            pl.BlockSpec(memory_space=pltpu.VMEM),
-        ],
+        in_specs=[pl.BlockSpec(memory_space=pltpu.SMEM)]
+        + [pl.BlockSpec(memory_space=pltpu.VMEM)] * planes,
         out_shape=[
             jax.ShapeDtypeStruct((slots, wide), jnp.bfloat16),
             jax.ShapeDtypeStruct((tokens, slots), jnp.bfloat16),
@@ -239,7 +232,7 @@
         ],
         compiler_params=grant(16),
         name="dispatch",
-    )(here, payload)
+    )(here, *payloads)
     return out.reshape(seqs * ys, -1, wide), (code, total)
 
 
@@ -277,40 +270,56 @@
     ).reshape(shape)
 
 
-def combine_body(code_ref, total_ref, returned_ref, out_ref):
+def combine_body(code_ref, total_ref, returned_ref, *outs):
     part = jnp.dot(code_ref[...], returned_ref[...], preferred_element_type=jnp.float32)
-    out_ref[...] = (part / total_ref[:, :1]).astype(jnp.bfloat16)
+    part = (part / total_ref[:, :1]).astype(jnp.bfloat16)
+    rows = part.shape[0] // len(outs)
+    for b, out_ref in enumerate(outs):
+        out_ref[...] = part[b * rows : (b + 1) * rows]
 
 
 def combine(code, total, returned, planes):
     wide = returned.shape[-1]
-    out = pl.pallas_call(
+    rows = code.shape[0] // planes
+    return pl.pallas_call(
         combine_body,
-        out_shape=jax.ShapeDtypeStruct((code.shape[0], wide), jnp.bfloat16),
+        out_shape=[jax.ShapeDtypeStruct((rows, wide), jnp.bfloat16)] * planes,
         compiler_params=grant(10),
         name="combine",
     )(code, total, returned.reshape(-1, wide))
-    return out.reshape(planes, -1, wide)
-
-
-def finish_body(residual_ref, sums_ref, out_ref):
+
+
+def finish_body(residual_ref, *refs):
+    *sum_refs, out_ref = refs
     part = residual_ref[...].astype(jnp.float32)
-    for z in range(sums_ref.shape[0]):
-        part = part + sums_ref[z].astype(jnp.float32)
+    for ref in sum_refs:
+        part = part + ref[...].astype(jnp.float32)
     out_ref[...] = part.astype(jnp.bfloat16)
 
 
-def finish(residual, sums):
+def finish(residual, *sums):
     return pl.pallas_call(
         finish_body,
         out_shape=jax.ShapeDtypeStruct(residual.shape, jnp.bfloat16),
         compiler_params=grant(8),
         name="finish",
-    )(residual, sums)
+    )(residual, *sums)
 
 
 def shift(size, by):
     return [(i, (i + by) % size) for i in range(size)]
+
+
+def z_moves(lows, highs):
+    size = lows * highs
+
+    def index(z):
+        return z % size % lows * highs + z % size // lows
+
+    return [
+        [(index(z), index(z + (far if z % lows == 0 else -far))) for z in range(size)]
+        for far in (2, -1, -3)
+    ]
 
 
 def exchange(blocks, axes):
@@ -352,12 +361,16 @@
     parts = exchange(parts.reshape(-1, rows, parts.shape[-1]), ("seq",) + HEADS)
     parts = parts.reshape(seqs, -1, rows, parts.shape[-1])
     residual, payload = norm(
-        parts, stream, norm_gain.reshape(1, -1), routes.T, gate_codes.T, zs
-    )
-    sent, mix = dispatch(here, exchange(payload, "zh"), static)
+        parts, stream, norm_gain.reshape(1, -1), routes.T, gate_codes.T
+    )
+    moves = z_moves(lax.axis_size("zl"), zs)
+    payloads = [payload] + [lax.ppermute(payload, ("zl", "zh"), m) for m in moves]
+    sent, mix = dispatch(here, payloads, static)
     made = expert(exchange(sent, PLANE), gate_weight, up_weight, down_weight)
-    sums = combine(*mix, exchange(made, PLANE), zs)
-    return finish(residual, exchange(sums, "zh"))
+    own, *sums = combine(*mix, exchange(made, PLANE), len(payloads))
+    back = [[(b, a) for a, b in m] for m in moves]
+    sums = [lax.ppermute(v, ("zl", "zh"), m) for v, m in zip(sums, back)]
+    return finish(residual, own, *sums)
 
 
 def solution(mesh):

time: 154 us -> 146 us (0.948)
  the two profiles are of different devices: /device:TPU:8 before, /device:TPU:1 now
where the time goes in v4:
time: 146 us; the launch traced here: 144 us
  blocking collectives  78.8 us (54%)
  waiting for transfers between devices  28.7 us (20%)
  Pallas kernels  18.5 us (13%)
  starting transfers between devices  17.2 us (12%)
    all_to_all x3, blocking collectives, exchange(): return lax.all_to_all(blocks, axes, split_axis=0, concat_axis=0, tiled=True)  78.8 us
    ppermute x3, waiting for transfers between devices, on_device(): lax.ppermute(head_out, 'seq', shift(seqs, d))  10.6 us
    ppermute x3, waiting for transfers between devices, on_device(): lax.ppermute(payload, ('zl', 'zh'), m)  10.3 us
    ppermute x3, waiting for transfers between devices, on_device(): sums = [lax.ppermute(v, ('zl', 'zh'), m) for v, m in zip(sums, back)]  7.82 us
    ppermute x3, starting transfers between devices, on_device(): lax.ppermute(payload, ('zl', 'zh'), m)  7.56 us
    pallas_call x1, Pallas kernels, attention(): pl.pallas_call(attention_body, grid=(rows // block,), in_specs=[pl.BlockS...  7.35 us
    pallas_call x1, Pallas kernels, expert(): pl.pallas_call(expert_body, in_specs=[pl.BlockSpec(memory_space=pltpu.VME...  6.77 us
    ppermute x3, starting transfers between devices, on_device(): lax.ppermute(head_out, 'seq', shift(seqs, d))  5.11 us
  transfers between devices with their start and end apart: 9, of which 8 were waited for; matrix products, arithmetic and copies ran while one was open for 0% of the time, Pallas kernels for 0%

profile of v4, /device:TPU:1, one launch (start us, length us, event | category | flops | bytes accessed | tf_op | source)
XLA Modules:
  0.0 143.5 jit_solution(10606597049056065603)
XLA Ops:
  0.0 7.3 %attention.1.refs_0_ = bf16[128,1024]{1,0:T(8,128)(2,1)S(1)} custom-call(s32[96,128]{1,0:T(8,128)} %bitcast.28, s32[4,128]{1,0:T(4,128)} %bitcast.29, bf16[128,1024]{1,0:T(8,128)(2,1)} %query_ref.1, bf16[128,1,128,256]{3,2,1,0:T(8,128)(2,1)} %cache_ref.1, bf16[128,256]{1,0:T(8,128)(2,1)} %bitcast.27), custom_call_target="tpu_custom_call" | custom-call | tf_op jit(solution)/shard_map/attention/pallas_call | solution.py:90
  7.4 3.6 %collective-permute-start.2 = (bf16[128,1024]{1,0:T(8,128)(2,1)S(1)}, bf16[128,1024]{1,0:T(8,128)(2,1)S(1)}, u32[]{:S(2)}, u32[]{:S(2)}) collective-permute-start(bf16[128,1024]{1,0:T(8,128)(2,1)S(1)} %attention.1.refs_0_), channel_id=1, source_target_pairs={{0,32},{16,48},{32,0},{48,16},{1,33},{17,49},{33,1},{49,17},{2,34}... | collective-permute-start | bytes 786440 | tf_op jit(solution)/shard_map/ppermute | solution.py:358
  11.1 0.9 collective-permute-start.1
  11.9 0.6 collective-permute-start
  12.6 3.5 %collective-permute-done.2.refs_3_ = bf16[128,1024]{1,0:T(8,128)(2,1)S(1)} collective-permute-done((bf16[128,1024]{1,0:T(8,128)(2,1)S(1)}, bf16[128,1024]{1,0:T(8,128)(2,1)S(1)}, u32[]{:S(2)}, u32[]{:S(2)}) %collective-permute-start.2) | collective-permute-done | bytes 262176 | tf_op jit(solution)/shard_map/ppermute | solution.py:358
  16.1 6.7 %collective-permute-done.1.refs_2_ = bf16[128,1024]{1,0:T(8,128)(2,1)S(1)} collective-permute-done((bf16[128,1024]{1,0:T(8,128)(2,1)S(1)}, bf16[128,1024]{1,0:T(8,128)(2,1)S(1)}, u32[]{:S(2)}, u32[]{:S(2)}) %collective-permute-start.1) | collective-permute-done | bytes 262176 | tf_op jit(solution)/shard_map/ppermute | solution.py:358
  22.8 0.4 collective-permute-done.refs_1_
  23.2 1.3 project.1
  24.5 16.4 %all_to_all.15 = bf16[16,32,512]{2,1,0:T(8,128)(2,1)S(1)} all-to-all(bf16[16,32,512]{2,1,0:T(8,128)(2,1)S(1)} %bitcast.23), channel_id=1, replica_groups=mesh['zl'=2,'core'=2,'seq'=4,'zh'=4,'y'=4] {'seq','zl','core'}, dimensions={0} | all-to-all | bytes 1048576 | tf_op jit(solution)/shard_map/all_to_all | solution.py:326
  41.1 6.3 %collective-permute-start.5 = (bf16[32,2176]{1,0:T(8,128)(2,1)S(1)}, bf16[32,2176]{1,0:T(8,128)(2,1)S(1)}, u32[]{:S(2)}, u32[]{:S(2)}) collective-permute-start(bf16[32,2176]{1,0:T(8,128)(2,1)S(1)} %get-tuple-element.15.refs_1_), channel_id=1, source_target_pairs={{0,136},{128,8},{4,140},{132,12},{8,128},{136,0},{12,132},{140,4},... | collective-permute-start | bytes 417800 | tf_op jit(solution)/shard_map/ppermute | solution.py:367
  47.4 1.3 collective-permute-start.3
  48.6 2.4 %collective-permute-done.5.refs_4_ = bf16[32,2176]{1,0:T(8,128)(2,1)S(1)} collective-permute-done((bf16[32,2176]{1,0:T(8,128)(2,1)S(1)}, bf16[32,2176]{1,0:T(8,128)(2,1)S(1)}, u32[]{:S(2)}, u32[]{:S(2)}) %collective-permute-start.5) | collective-permute-done | bytes 139296 | tf_op jit(solution)/shard_map/ppermute | solution.py:367
  51.0 7.9 %collective-permute-done.4.refs_3_ = bf16[32,2176]{1,0:T(8,128)(2,1)S(1)} collective-permute-done((bf16[32,2176]{1,0:T(8,128)(2,1)S(1)}, bf16[32,2176]{1,0:T(8,128)(2,1)S(1)}, u32[]{:S(2)}, u32[]{:S(2)}) %collective-permute-start.4) | collective-permute-done | bytes 139296 | tf_op jit(solution)/shard_map/ppermute | solution.py:367
  59.0 1.8 %dispatch.1 = (bf16[512,2048]{1,0:T(8,128)(2,1)S(1)}, bf16[128,512]{1,0:T(8,128)(2,1)S(1)}, f32[128,128]{1,0:T(8,128)S(1)}) custom-call(s32[2]{0:T(128)S(1)} %pad_add_fusion.here_ref.refs_0_, bf16[32,2176]{1,0:T(8,128)(2,1)S(1)} %get-tuple-element.15.refs_1_, bf16[32,2176]{1,0:T(8,128)(2,1)S(1)} %collective-permute-done.3.refs_2_, ...), custom_call_target="tpu_custom_call" | custom-call | tf_op jit(solution)/shard_map/dispatch/pallas_call | solution.py:224
  60.7 31.9 %all_to_all.16 = bf16[16,32,2048]{2,1,0:T(8,128)(2,1)S(1)} all-to-all(bf16[16,32,2048]{2,1,0:T(8,128)(2,1)S(1)} %bitcast.21), channel_id=1, replica_groups=mesh['zl'=2,'core'=2,'seq'=4,'zh'=4,'y'=4] {'seq','y'}, dimensions={0} | all-to-all | bytes 4194304 | tf_op jit(solution)/shard_map/all_to_all | solution.py:326
  92.6 6.8 %expert.1 = bf16[512,2048]{1,0:T(8,128)(2,1)S(1)} custom-call(bf16[512,2048]{1,0:T(8,128)(2,1)S(1)} %bitcast.19, bf16[1,2048,768]{2,1,0:T(8,128)(2,1)S(1)} %copy-done, bf16[1,2048,768]{2,1,0:T(8,128)(2,1)S(1)} %copy-done.1, bf16[1,768,2048]{2,1,0:T(8,128)(2,1)} %down_hbm.1), custom_call_target="tpu_custom_call" | custom-call | tf_op jit(solution)/shard_map/expert/pallas_call | solution.py:255
  99.4 30.6 %all_to_all.17 = bf16[16,32,2048]{2,1,0:T(8,128)(2,1)S(1)} all-to-all(bf16[16,32,2048]{2,1,0:T(8,128)(2,1)S(1)} %bitcast.20), channel_id=1, replica_groups=mesh['zl'=2,'core'=2,'seq'=4,'zh'=4,'y'=4] {'seq','y'}, dimensions={0} | all-to-all | bytes 4194304 | tf_op jit(solution)/shard_map/all_to_all | solution.py:326
  130.0 0.4 combine.1
  130.5 3.7 %collective-permute-start.7 = (bf16[32,2048]{1,0:T(8,128)(2,1)S(1)}, bf16[32,2048]{1,0:T(8,128)(2,1)S(1)}, u32[]{:S(2)}, u32[]{:S(2)}) collective-permute-start(bf16[32,2048]{1,0:T(8,128)(2,1)S(1)} %get-tuple-element.21), channel_id=1, source_target_pairs={{140,0},{4,128},{128,4},{8,132},{132,8},{12,136},{136,12},{0,140},... | collective-permute-start | bytes 393224 | tf_op jit(solution)/shard_map/ppermute | solution.py:372
  134.2 0.7 collective-permute-start.8
  134.9 0.3 collective-permute-done.6.refs_1_
  135.2 2.9 %collective-permute-done.7.refs_2_ = bf16[32,2048]{1,0:T(8,128)(2,1)S(1)} collective-permute-done((bf16[32,2048]{1,0:T(8,128)(2,1)S(1)}, bf16[32,2048]{1,0:T(8,128)(2,1)S(1)}, u32[]{:S(2)}, u32[]{:S(2)}) %collective-permute-start.7) | collective-permute-done | bytes 131104 | tf_op jit(solution)/shard_map/ppermute | solution.py:372
  138.1 4.7 %collective-permute-done.8.refs_3_ = bf16[32,2048]{1,0:T(8,128)(2,1)S(1)} collective-permute-done((bf16[32,2048]{1,0:T(8,128)(2,1)S(1)}, bf16[32,2048]{1,0:T(8,128)(2,1)S(1)}, u32[]{:S(2)}, u32[]{:S(2)}) %collective-permute-start.8) | collective-permute-done | bytes 131104 | tf_op jit(solution)/shard_map/ppermute | solution.py:372
  142.8 0.7 finish.1
  (19 shorter events, 0.4 us)
Async XLA Ops:
  0.0 23.2 %copy-start.2 = (bf16[1024,512]{1,0:T(8,128)(2,1)S(1)}, bf16[1024,512]{1,0:T(8,128)(2,1)}, u32[]{:S(2)}) copy-start(bf16[1024,512]{1,0:T(8,128)(2,1)} %refs_4_.1) | copy-start | bytes 3145732
  7.4 33.5 %copy-start.3 = (bf16[32,2048]{1,0:T(8,128)(2,1)S(1)}, bf16[32,2048]{1,0:T(8,128)(2,1)}, u32[]{:S(2)}) copy-start(bf16[32,2048]{1,0:T(8,128)(2,1)} %stream_ref.1) | copy-start | bytes 393220
  7.4 33.5 %copy-start.4 = (f32[2048]{0:T(1024)S(1)}, f32[2048]{0:T(1024)}, u32[]{:S(2)}) copy-start(f32[2048]{0:T(1024)} %param.20) | copy-start | bytes 24580
  7.4 33.5 %copy-start.5 = (s32[32,8]{0,1:T(8,128)S(1)}, s32[32,8]{0,1:T(8,128)}, u32[]{:S(2)}) copy-start(s32[32,8]{0,1:T(8,128)} %param.21) | copy-start | bytes 3076
  7.4 33.4 %copy-start.6 = (s32[32,8]{0,1:T(8,128)S(1)}, s32[32,8]{0,1:T(8,128)}, u32[]{:S(2)}) copy-start(s32[32,8]{0,1:T(8,128)} %param.22) | copy-start | bytes 3076
  7.4 8.7 %collective-permute-start.2 = (bf16[128,1024]{1,0:T(8,128)(2,1)S(1)}, bf16[128,1024]{1,0:T(8,128)(2,1)S(1)}, u32[]{:S(2)}, u32[]{:S(2)}) collective-permute-start(bf16[128,1024]{1,0:T(8,128)(2,1)S(1)} %attention.1.refs_0_), channel_id=1, source_target_pairs={{0,32},{16,48},{32,0},{48,16},{1,33},{17,49},{33,1},{49,17},{2,34}... | collective-permute-start | bytes 786440 | tf_op jit(solution)/shard_map/ppermute | solution.py:358
  11.1 11.7 %collective-permute-start.1 = (bf16[128,1024]{1,0:T(8,128)(2,1)S(1)}, bf16[128,1024]{1,0:T(8,128)(2,1)S(1)}, u32[]{:S(2)}, u32[]{:S(2)}) collective-permute-start(bf16[128,1024]{1,0:T(8,128)(2,1)S(1)} %attention.1.refs_0_), channel_id=1, source_target_pairs={{0,48},{16,0},{32,16},{48,32},{1,49},{17,1},{33,17},{49,33},{2,50}... | collective-permute-start | bytes 786440 | tf_op jit(solution)/shard_map/ppermute | solution.py:358
  11.9 11.3 %collective-permute-start = (bf16[128,1024]{1,0:T(8,128)(2,1)S(1)}, bf16[128,1024]{1,0:T(8,128)(2,1)S(1)}, u32[]{:S(2)}, u32[]{:S(2)}) collective-permute-start(bf16[128,1024]{1,0:T(8,128)(2,1)S(1)} %attention.1.refs_0_), channel_id=1, source_target_pairs={{0,16},{16,32},{32,48},{48,0},{1,17},{17,33},{33,49},{49,1},{2,18}... | collective-permute-start | bytes 786440 | tf_op jit(solution)/shard_map/ppermute | solution.py:358
  24.4 68.2 %copy-start = (bf16[1,2048,768]{2,1,0:T(8,128)(2,1)S(1)}, bf16[1,2048,768]{2,1,0:T(8,128)(2,1)}, u32[]{:S(2)}) copy-start(bf16[1,2048,768]{2,1,0:T(8,128)(2,1)} %gate_ref.1) | copy-start | bytes 9437188
  24.5 68.2 %copy-start.1 = (bf16[1,2048,768]{2,1,0:T(8,128)(2,1)S(1)}, bf16[1,2048,768]{2,1,0:T(8,128)(2,1)}, u32[]{:S(2)}) copy-start(bf16[1,2048,768]{2,1,0:T(8,128)(2,1)} %up_ref.1) | copy-start | bytes 9437188
  41.1 10.0 %collective-permute-start.5 = (bf16[32,2176]{1,0:T(8,128)(2,1)S(1)}, bf16[32,2176]{1,0:T(8,128)(2,1)S(1)}, u32[]{:S(2)}, u32[]{:S(2)}) collective-permute-start(bf16[32,2176]{1,0:T(8,128)(2,1)S(1)} %get-tuple-element.15.refs_1_), channel_id=1, source_target_pairs={{0,136},{128,8},{4,140},{132,12},{8,128},{136,0},{12,132},{140,4},... | collective-permute-start | bytes 417800 | tf_op jit(solution)/shard_map/ppermute | solution.py:367
  47.4 11.6 %collective-permute-start.4 = (bf16[32,2176]{1,0:T(8,128)(2,1)S(1)}, bf16[32,2176]{1,0:T(8,128)(2,1)S(1)}, u32[]{:S(2)}, u32[]{:S(2)}) collective-permute-start(bf16[32,2176]{1,0:T(8,128)(2,1)S(1)} %get-tuple-element.15.refs_1_), channel_id=1, source_target_pairs={{0,140},{128,4},{4,128},{132,8},{8,132},{136,12},{12,136},{140,0},... | collective-permute-start | bytes 417800 | tf_op jit(solution)/shard_map/ppermute | solution.py:367
  47.4 11.6 %collective-permute-start.3 = (bf16[32,2176]{1,0:T(8,128)(2,1)S(1)}, bf16[32,2176]{1,0:T(8,128)(2,1)S(1)}, u32[]{:S(2)}, u32[]{:S(2)}) collective-permute-start(bf16[32,2176]{1,0:T(8,128)(2,1)S(1)} %get-tuple-element.15.refs_1_), channel_id=1, source_target_pairs={{0,4},{128,140},{4,8},{132,128},{8,12},{136,132},{12,0},{140,136},... | collective-permute-start | bytes 417800 | tf_op jit(solution)/shard_map/ppermute | solution.py:367
  130.4 4.8 %collective-permute-start.6 = (bf16[32,2048]{1,0:T(8,128)(2,1)S(1)}, bf16[32,2048]{1,0:T(8,128)(2,1)S(1)}, u32[]{:S(2)}, u32[]{:S(2)}) collective-permute-start(bf16[32,2048]{1,0:T(8,128)(2,1)S(1)} %get-tuple-element.20), channel_id=1, source_target_pairs={{4,0},{140,128},{8,4},{128,132},{12,8},{132,136},{0,12},{136,140},... | collective-permute-start | bytes 393224 | tf_op jit(solution)/shard_map/ppermute | solution.py:372
  130.5 7.6 %collective-permute-start.7 = (bf16[32,2048]{1,0:T(8,128)(2,1)S(1)}, bf16[32,2048]{1,0:T(8,128)(2,1)S(1)}, u32[]{:S(2)}, u32[]{:S(2)}) collective-permute-start(bf16[32,2048]{1,0:T(8,128)(2,1)S(1)} %get-tuple-element.21), channel_id=1, source_target_pairs={{140,0},{4,128},{128,4},{8,132},{132,8},{12,136},{136,12},{0,140},... | collective-permute-start | bytes 393224 | tf_op jit(solution)/shard_map/ppermute | solution.py:372
  134.2 8.6 %collective-permute-start.8 = (bf16[32,2048]{1,0:T(8,128)(2,1)S(1)}, bf16[32,2048]{1,0:T(8,128)(2,1)S(1)}, u32[]{:S(2)}, u32[]{:S(2)}) collective-permute-start(bf16[32,2048]{1,0:T(8,128)(2,1)S(1)} %get-tuple-element.22), channel_id=1, source_target_pairs={{136,0},{8,128},{140,4},{12,132},{128,8},{0,136},{132,12},{4,140},... | collective-permute-start | bytes 393224 | tf_op jit(solution)/shard_map/ppermute | solution.py:372

commit v5 on v4

--- a/solution.py
+++ b/solution.py
@@ -8,6 +8,7 @@
 
 epsilon = 1e-06
 LANES = 128
+OFFSET_NS = 14000
 ATT_BLOCK = 32
 MESH_AXES = ("zl", "core", "seq", "zh", "y")
 PLANE = ("seq", "y")
@@ -126,7 +127,7 @@
     )(here, *blocks, weight)
 
 
-def norm_body(parts_ref, stream_ref, gain_ref, routes_ref, codes_ref, residual_ref, payload_ref):
+def norm_body(here_ref, parts_ref, stream_ref, gain_ref, routes_ref, codes_ref, residual_ref, payload_ref):
     seqs, heads, rows, width = parts_ref.shape
     wide = seqs * width
     total = jnp.zeros((rows, 1), jnp.float32)
@@ -156,18 +157,24 @@
     )
     payload_ref[:, wide:] = tail.T.astype(jnp.bfloat16)
 
-
-def norm(parts, stream, gain, routes, codes):
+    @pl.when(here_ref[2] == 1)
+    def _():
+        pl.delay(OFFSET_NS)
+
+
+def norm(here, parts, stream, gain, routes, codes):
     rows, wide = stream.shape
     return pl.pallas_call(
         norm_body,
+        in_specs=[pl.BlockSpec(memory_space=pltpu.SMEM)]
+        + [pl.BlockSpec(memory_space=pltpu.VMEM)] * 5,
         out_shape=[
             jax.ShapeDtypeStruct((rows, wide), jnp.bfloat16),
             jax.ShapeDtypeStruct((rows, wide + LANES), jnp.bfloat16),
         ],
         compiler_params=grant(8),
         name="norm",
-    )(parts, stream, gain, routes, codes)
+    )(here, parts, stream, gain, routes, codes)
 
 
 def placement(tail, zh, blocks, top, experts_shape, capacity):
@@ -343,7 +350,7 @@
 ):
     rows, wide = stream.shape
     seqs, zs, ys = (lax.axis_size(a) for a in ("seq", "zh", "y"))
-    here = jnp.stack([lax.axis_index("seq"), lax.axis_index("zh")]).astype(jnp.int32)
+    here = jnp.stack([lax.axis_index(a) for a in ("seq", "zh", "core")]).astype(jnp.int32)
     experts = seqs * zs * ys
     static = dict(
         top=routes.shape[1],
@@ -361,7 +368,7 @@
     parts = exchange(parts.reshape(-1, rows, parts.shape[-1]), ("seq",) + HEADS)
     parts = parts.reshape(seqs, -1, rows, parts.shape[-1])
     residual, payload = norm(
-        parts, stream, norm_gain.reshape(1, -1), routes.T, gate_codes.T
+        here, parts, stream, norm_gain.reshape(1, -1), routes.T, gate_codes.T
     )
     moves = z_moves(lax.axis_size("zl"), zs)
     payloads = [payload] + [lax.ppermute(payload, ("zl", "zh"), m) for m in moves]

time: 146 us -> 132 us (0.904); the launches traced: 144 us -> 132 us
  blocking collectives: 78.8 us -> 59.2 us
  starting transfers between devices: 17.2 us -> 32.6 us
  waiting for transfers between devices: 28.7 us -> 20.4 us
    all_to_all x3, blocking collectives: 78.8 us -> 59.2 us  [exchange(): return lax.all_to_all(blocks, axes, split_axis=0, concat_axis=0, tiled=True)]
    ppermute x3, starting transfers between devices: 7.56 us -> 21.5 us  [on_device(): lax.ppermute(payload, ('zl', 'zh'), m)]
    ppermute x3, waiting for transfers between devices: 10.3 us -> 5.65 us  [on_device(): lax.ppermute(payload, ('zl', 'zh'), m)]
    ppermute x3, waiting for transfers between devices: 7.82 us -> 4.18 us  [on_device(): sums = [lax.ppermute(v, ('zl', 'zh'), m) for v, m in zip(sums, back)]]
    ppermute x3, starting transfers between devices: 4.51 us -> 6.06 us  [on_device(): sums = [lax.ppermute(v, ('zl', 'zh'), m) for v, m in zip(sums, back)]]
  transfers between devices with their start and end apart: 9 -> 9, of which waited for: 8 -> 7; matrix products, arithmetic and copies ran while one was open for 0% -> 0% of each run, Pallas kernels for 0% -> 0%
where the time goes in v5:
time: 132 us
  blocking collectives  59.2 us (45%)
  starting transfers between devices  32.6 us (25%)
  waiting for transfers between devices  20.4 us (15%)
  Pallas kernels  19.1 us (14%)
    all_to_all x3, blocking collectives, exchange(): return lax.all_to_all(blocks, axes, split_axis=0, concat_axis=0, tiled=True)  59.2 us
    ppermute x3, starting transfers between devices, on_device(): lax.ppermute(payload, ('zl', 'zh'), m)  21.5 us
    ppermute x3, waiting for transfers between devices, on_device(): lax.ppermute(head_out, 'seq', shift(seqs, d))  10.6 us
    pallas_call x1, Pallas kernels, attention(): pl.pallas_call(attention_body, grid=(rows // block,), in_specs=[pl.BlockS...  7.35 us
    pallas_call x1, Pallas kernels, expert(): pl.pallas_call(expert_body, in_specs=[pl.BlockSpec(memory_space=pltpu.VME...  6.77 us
    ppermute x3, starting transfers between devices, on_device(): sums = [lax.ppermute(v, ('zl', 'zh'), m) for v, m in zip(sums, back)]  6.06 us
    ppermute x3, waiting for transfers between devices, on_device(): lax.ppermute(payload, ('zl', 'zh'), m)  5.65 us
    ppermute x3, starting transfers between devices, on_device(): lax.ppermute(head_out, 'seq', shift(seqs, d))  5.11 us
  transfers between devices with their start and end apart: 9, of which 7 were waited for; matrix products, arithmetic and copies ran while one was open for 0% of the time, Pallas kernels for 0%

profile of v5, /device:TPU:1, one launch (start us, length us, event | category | flops | bytes accessed | tf_op | source)
XLA Modules:
  0.0 131.6 jit_solution(1542783364935068159)
XLA Ops:
  0.0 7.3 %attention.1.refs_0_ = bf16[128,1024]{1,0:T(8,128)(2,1)S(1)} custom-call(s32[96,128]{1,0:T(8,128)} %bitcast.29, s32[4,128]{1,0:T(4,128)} %bitcast.30, bf16[128,1024]{1,0:T(8,128)(2,1)} %query_ref.1, bf16[128,1,128,256]{3,2,1,0:T(8,128)(2,1)} %cache_ref.1, bf16[128,256]{1,0:T(8,128)(2,1)} %bitcast.28), custom_call_target="tpu_custom_call" | custom-call | tf_op jit(solution)/shard_map/attention/pallas_call | solution.py:91
  7.4 3.6 %collective-permute-start.2 = (bf16[128,1024]{1,0:T(8,128)(2,1)S(1)}, bf16[128,1024]{1,0:T(8,128)(2,1)S(1)}, u32[]{:S(2)}, u32[]{:S(2)}) collective-permute-start(bf16[128,1024]{1,0:T(8,128)(2,1)S(1)} %attention.1.refs_0_), channel_id=1, source_target_pairs={{0,32},{16,48},{32,0},{48,16},{1,33},{17,49},{33,1},{49,17},{2,34}... | collective-permute-start | bytes 786440 | tf_op jit(solution)/shard_map/ppermute | solution.py:365
  11.1 0.9 collective-permute-start.1
  11.9 0.6 collective-permute-start
  12.6 3.5 %collective-permute-done.2.refs_3_ = bf16[128,1024]{1,0:T(8,128)(2,1)S(1)} collective-permute-done((bf16[128,1024]{1,0:T(8,128)(2,1)S(1)}, bf16[128,1024]{1,0:T(8,128)(2,1)S(1)}, u32[]{:S(2)}, u32[]{:S(2)}) %collective-permute-start.2) | collective-permute-done | bytes 262176 | tf_op jit(solution)/shard_map/ppermute | solution.py:365
  16.1 6.7 %collective-permute-done.1.refs_2_ = bf16[128,1024]{1,0:T(8,128)(2,1)S(1)} collective-permute-done((bf16[128,1024]{1,0:T(8,128)(2,1)S(1)}, bf16[128,1024]{1,0:T(8,128)(2,1)S(1)}, u32[]{:S(2)}, u32[]{:S(2)}) %collective-permute-start.1) | collective-permute-done | bytes 262176 | tf_op jit(solution)/shard_map/ppermute | solution.py:365
  23.2 1.3 project.1
  24.5 16.4 %all_to_all.15 = bf16[16,32,512]{2,1,0:T(8,128)(2,1)S(1)} all-to-all(bf16[16,32,512]{2,1,0:T(8,128)(2,1)S(1)} %bitcast.24), channel_id=1, replica_groups=mesh['zl'=2,'core'=2,'seq'=4,'zh'=4,'y'=4] {'seq','zl','core'}, dimensions={0} | all-to-all | bytes 1048576 | tf_op jit(solution)/shard_map/all_to_all | solution.py:333
  40.9 0.8 norm.1
  41.6 20.2 %collective-permute-start.5 = (bf16[32,2176]{1,0:T(8,128)(2,1)S(1)}, bf16[32,2176]{1,0:T(8,128)(2,1)S(1)}, u32[]{:S(2)}, u32[]{:S(2)}) collective-permute-start(bf16[32,2176]{1,0:T(8,128)(2,1)S(1)} %get-tuple-element.15.refs_1_), channel_id=1, source_target_pairs={{0,136},{128,8},{4,140},{132,12},{8,128},{136,0},{12,132},{140,4},... | collective-permute-start | bytes 417800 | tf_op jit(solution)/shard_map/ppermute | solution.py:374
  61.8 1.3 collective-permute-start.3
  63.1 2.2 %collective-permute-done.5.refs_4_ = bf16[32,2176]{1,0:T(8,128)(2,1)S(1)} collective-permute-done((bf16[32,2176]{1,0:T(8,128)(2,1)S(1)}, bf16[32,2176]{1,0:T(8,128)(2,1)S(1)}, u32[]{:S(2)}, u32[]{:S(2)}) %collective-permute-start.5) | collective-permute-done | bytes 139296 | tf_op jit(solution)/shard_map/ppermute | solution.py:374
  65.3 3.4 %collective-permute-done.4.refs_3_ = bf16[32,2176]{1,0:T(8,128)(2,1)S(1)} collective-permute-done((bf16[32,2176]{1,0:T(8,128)(2,1)S(1)}, bf16[32,2176]{1,0:T(8,128)(2,1)S(1)}, u32[]{:S(2)}, u32[]{:S(2)}) %collective-permute-start.4) | collective-permute-done | bytes 139296 | tf_op jit(solution)/shard_map/ppermute | solution.py:374
  68.7 1.8 %dispatch.1 = (bf16[512,2048]{1,0:T(8,128)(2,1)S(1)}, bf16[128,512]{1,0:T(8,128)(2,1)S(1)}, f32[128,128]{1,0:T(8,128)S(1)}) custom-call(s32[3]{0:T(128)S(1)} %pad_add_fusion.here_ref.refs_0_, bf16[32,2176]{1,0:T(8,128)(2,1)S(1)} %get-tuple-element.15.refs_1_, bf16[32,2176]{1,0:T(8,128)(2,1)S(1)} %collective-permute-done.3.refs_2_, ...), custom_call_target="tpu_custom_call" | custom-call | tf_op jit(solution)/shard_map/dispatch/pallas_call | solution.py:231
  70.5 21.9 %all_to_all.16 = bf16[16,32,2048]{2,1,0:T(8,128)(2,1)S(1)} all-to-all(bf16[16,32,2048]{2,1,0:T(8,128)(2,1)S(1)} %bitcast.22), channel_id=1, replica_groups=mesh['zl'=2,'core'=2,'seq'=4,'zh'=4,'y'=4] {'seq','y'}, dimensions={0} | all-to-all | bytes 4194304 | tf_op jit(solution)/shard_map/all_to_all | solution.py:333
  92.4 6.8 %expert.1 = bf16[512,2048]{1,0:T(8,128)(2,1)S(1)} custom-call(bf16[512,2048]{1,0:T(8,128)(2,1)S(1)} %bitcast.20, bf16[1,2048,768]{2,1,0:T(8,128)(2,1)S(1)} %copy-done, bf16[1,2048,768]{2,1,0:T(8,128)(2,1)S(1)} %copy-done.1, bf16[1,768,2048]{2,1,0:T(8,128)(2,1)} %down_hbm.1), custom_call_target="tpu_custom_call" | custom-call | tf_op jit(solution)/shard_map/expert/pallas_call | solution.py:262
  99.2 21.0 %all_to_all.17 = bf16[16,32,2048]{2,1,0:T(8,128)(2,1)S(1)} all-to-all(bf16[16,32,2048]{2,1,0:T(8,128)(2,1)S(1)} %bitcast.21), channel_id=1, replica_groups=mesh['zl'=2,'core'=2,'seq'=4,'zh'=4,'y'=4] {'seq','y'}, dimensions={0} | all-to-all | bytes 4194304 | tf_op jit(solution)/shard_map/all_to_all | solution.py:333
  120.2 0.4 combine.1
  120.6 1.6 %collective-permute-start.6 = (bf16[32,2048]{1,0:T(8,128)(2,1)S(1)}, bf16[32,2048]{1,0:T(8,128)(2,1)S(1)}, u32[]{:S(2)}, u32[]{:S(2)}) collective-permute-start(bf16[32,2048]{1,0:T(8,128)(2,1)S(1)} %get-tuple-element.20), channel_id=1, source_target_pairs={{4,0},{140,128},{8,4},{128,132},{12,8},{132,136},{0,12},{136,140},... | collective-permute-start | bytes 393224 | tf_op jit(solution)/shard_map/ppermute | solution.py:379
  122.2 1.8 %collective-permute-start.7 = (bf16[32,2048]{1,0:T(8,128)(2,1)S(1)}, bf16[32,2048]{1,0:T(8,128)(2,1)S(1)}, u32[]{:S(2)}, u32[]{:S(2)}) collective-permute-start(bf16[32,2048]{1,0:T(8,128)(2,1)S(1)} %get-tuple-element.21), channel_id=1, source_target_pairs={{140,0},{4,128},{128,4},{8,132},{132,8},{12,136},{136,12},{0,140},... | collective-permute-start | bytes 393224 | tf_op jit(solution)/shard_map/ppermute | solution.py:379
  124.0 2.6 %collective-permute-start.8 = (bf16[32,2048]{1,0:T(8,128)(2,1)S(1)}, bf16[32,2048]{1,0:T(8,128)(2,1)S(1)}, u32[]{:S(2)}, u32[]{:S(2)}) collective-permute-start(bf16[32,2048]{1,0:T(8,128)(2,1)S(1)} %get-tuple-element.22), channel_id=1, source_target_pairs={{136,0},{8,128},{140,4},{12,132},{128,8},{0,136},{132,12},{4,140},... | collective-permute-start | bytes 393224 | tf_op jit(solution)/shard_map/ppermute | solution.py:379
  126.7 1.1 collective-permute-done.7.refs_2_
  127.8 3.1 %collective-permute-done.8.refs_3_ = bf16[32,2048]{1,0:T(8,128)(2,1)S(1)} collective-permute-done((bf16[32,2048]{1,0:T(8,128)(2,1)S(1)}, bf16[32,2048]{1,0:T(8,128)(2,1)S(1)}, u32[]{:S(2)}, u32[]{:S(2)}) %collective-permute-start.8) | collective-permute-done | bytes 131104 | tf_op jit(solution)/shard_map/ppermute | solution.py:379
  130.9 0.7 finish.1
  (19 shorter events, 0.5 us)
Async XLA Ops:
  0.0 23.2 %copy-start.2 = (bf16[1024,512]{1,0:T(8,128)(2,1)S(1)}, bf16[1024,512]{1,0:T(8,128)(2,1)}, u32[]{:S(2)}) copy-start(bf16[1024,512]{1,0:T(8,128)(2,1)} %refs_4_.1) | copy-start | bytes 3145732
  7.4 33.5 %copy-start.3 = (bf16[32,2048]{1,0:T(8,128)(2,1)S(1)}, bf16[32,2048]{1,0:T(8,128)(2,1)}, u32[]{:S(2)}) copy-start(bf16[32,2048]{1,0:T(8,128)(2,1)} %stream_ref.1) | copy-start | bytes 393220
  7.4 33.5 %copy-start.4 = (f32[2048]{0:T(1024)S(1)}, f32[2048]{0:T(1024)}, u32[]{:S(2)}) copy-start(f32[2048]{0:T(1024)} %param.20) | copy-start | bytes 24580
  7.4 33.5 %copy-start.5 = (s32[32,8]{0,1:T(8,128)S(1)}, s32[32,8]{0,1:T(8,128)}, u32[]{:S(2)}) copy-start(s32[32,8]{0,1:T(8,128)} %param.21) | copy-start | bytes 3076
  7.4 33.4 %copy-start.6 = (s32[32,8]{0,1:T(8,128)S(1)}, s32[32,8]{0,1:T(8,128)}, u32[]{:S(2)}) copy-start(s32[32,8]{0,1:T(8,128)} %param.22) | copy-start | bytes 3076
  7.4 8.7 %collective-permute-start.2 = (bf16[128,1024]{1,0:T(8,128)(2,1)S(1)}, bf16[128,1024]{1,0:T(8,128)(2,1)S(1)}, u32[]{:S(2)}, u32[]{:S(2)}) collective-permute-start(bf16[128,1024]{1,0:T(8,128)(2,1)S(1)} %attention.1.refs_0_), channel_id=1, source_target_pairs={{0,32},{16,48},{32,0},{48,16},{1,33},{17,49},{33,1},{49,17},{2,34}... | collective-permute-start | bytes 786440 | tf_op jit(solution)/shard_map/ppermute | solution.py:365
  11.1 11.7 %collective-permute-start.1 = (bf16[128,1024]{1,0:T(8,128)(2,1)S(1)}, bf16[128,1024]{1,0:T(8,128)(2,1)S(1)}, u32[]{:S(2)}, u32[]{:S(2)}) collective-permute-start(bf16[128,1024]{1,0:T(8,128)(2,1)S(1)} %attention.1.refs_0_), channel_id=1, source_target_pairs={{0,48},{16,0},{32,16},{48,32},{1,49},{17,1},{33,17},{49,33},{2,50}... | collective-permute-start | bytes 786440 | tf_op jit(solution)/shard_map/ppermute | solution.py:365
  11.9 11.3 %collective-permute-start = (bf16[128,1024]{1,0:T(8,128)(2,1)S(1)}, bf16[128,1024]{1,0:T(8,128)(2,1)S(1)}, u32[]{:S(2)}, u32[]{:S(2)}) collective-permute-start(bf16[128,1024]{1,0:T(8,128)(2,1)S(1)} %attention.1.refs_0_), channel_id=1, source_target_pairs={{0,16},{16,32},{32,48},{48,0},{1,17},{17,33},{33,49},{49,1},{2,18}... | collective-permute-start | bytes 786440 | tf_op jit(solution)/shard_map/ppermute | solution.py:365
  24.4 67.9 %copy-start = (bf16[1,2048,768]{2,1,0:T(8,128)(2,1)S(1)}, bf16[1,2048,768]{2,1,0:T(8,128)(2,1)}, u32[]{:S(2)}) copy-start(bf16[1,2048,768]{2,1,0:T(8,128)(2,1)} %gate_ref.1) | copy-start | bytes 9437188
  24.5 67.9 %copy-start.1 = (bf16[1,2048,768]{2,1,0:T(8,128)(2,1)S(1)}, bf16[1,2048,768]{2,1,0:T(8,128)(2,1)}, u32[]{:S(2)}) copy-start(bf16[1,2048,768]{2,1,0:T(8,128)(2,1)} %up_ref.1) | copy-start | bytes 9437188
  41.6 23.7 %collective-permute-start.5 = (bf16[32,2176]{1,0:T(8,128)(2,1)S(1)}, bf16[32,2176]{1,0:T(8,128)(2,1)S(1)}, u32[]{:S(2)}, u32[]{:S(2)}) collective-permute-start(bf16[32,2176]{1,0:T(8,128)(2,1)S(1)} %get-tuple-element.15.refs_1_), channel_id=1, source_target_pairs={{0,136},{128,8},{4,140},{132,12},{8,128},{136,0},{12,132},{140,4},... | collective-permute-start | bytes 417800 | tf_op jit(solution)/shard_map/ppermute | solution.py:374
  61.8 6.9 %collective-permute-start.4 = (bf16[32,2176]{1,0:T(8,128)(2,1)S(1)}, bf16[32,2176]{1,0:T(8,128)(2,1)S(1)}, u32[]{:S(2)}, u32[]{:S(2)}) collective-permute-start(bf16[32,2176]{1,0:T(8,128)(2,1)S(1)} %get-tuple-element.15.refs_1_), channel_id=1, source_target_pairs={{0,140},{128,4},{4,128},{132,8},{8,132},{136,12},{12,136},{140,0},... | collective-permute-start | bytes 417800 | tf_op jit(solution)/shard_map/ppermute | solution.py:374
  61.8 6.9 %collective-permute-start.3 = (bf16[32,2176]{1,0:T(8,128)(2,1)S(1)}, bf16[32,2176]{1,0:T(8,128)(2,1)S(1)}, u32[]{:S(2)}, u32[]{:S(2)}) collective-permute-start(bf16[32,2176]{1,0:T(8,128)(2,1)S(1)} %get-tuple-element.15.refs_1_), channel_id=1, source_target_pairs={{0,4},{128,140},{4,8},{132,128},{8,12},{136,132},{12,0},{140,136},... | collective-permute-start | bytes 417800 | tf_op jit(solution)/shard_map/ppermute | solution.py:374
  120.6 6.1 %collective-permute-start.6 = (bf16[32,2048]{1,0:T(8,128)(2,1)S(1)}, bf16[32,2048]{1,0:T(8,128)(2,1)S(1)}, u32[]{:S(2)}, u32[]{:S(2)}) collective-permute-start(bf16[32,2048]{1,0:T(8,128)(2,1)S(1)} %get-tuple-element.20), channel_id=1, source_target_pairs={{4,0},{140,128},{8,4},{128,132},{12,8},{132,136},{0,12},{136,140},... | collective-permute-start | bytes 393224 | tf_op jit(solution)/shard_map/ppermute | solution.py:379
  122.2 5.6 %collective-permute-start.7 = (bf16[32,2048]{1,0:T(8,128)(2,1)S(1)}, bf16[32,2048]{1,0:T(8,128)(2,1)S(1)}, u32[]{:S(2)}, u32[]{:S(2)}) collective-permute-start(bf16[32,2048]{1,0:T(8,128)(2,1)S(1)} %get-tuple-element.21), channel_id=1, source_target_pairs={{140,0},{4,128},{128,4},{8,132},{132,8},{12,136},{136,12},{0,140},... | collective-permute-start | bytes 393224 | tf_op jit(solution)/shard_map/ppermute | solution.py:379
  124.0 6.8 %collective-permute-start.8 = (bf16[32,2048]{1,0:T(8,128)(2,1)S(1)}, bf16[32,2048]{1,0:T(8,128)(2,1)S(1)}, u32[]{:S(2)}, u32[]{:S(2)}) collective-permute-start(bf16[32,2048]{1,0:T(8,128)(2,1)S(1)} %get-tuple-element.22), channel_id=1, source_target_pairs={{136,0},{8,128},{140,4},{12,132},{128,8},{0,136},{132,12},{4,140},... | collective-permute-start | bytes 393224 | tf_op jit(solution)/shard_map/ppermute | solution.py:379

commit v6 on v5

--- a/solution.py
+++ b/solution.py
@@ -1,3 +1,5 @@
+import functools
+
 import jax
 import jax.numpy as jnp
 from jax import lax
@@ -10,6 +12,7 @@
 LANES = 128
 OFFSET_NS = 14000
 ATT_BLOCK = 32
+ATT_PARTS = 2
 MESH_AXES = ("zl", "core", "seq", "zh", "y")
 PLANE = ("seq", "y")
 HEADS = ("zl", "core")
@@ -36,7 +39,7 @@
     return lax.rem(a, jnp.full_like(a, b))
 
 
-def attention_body(slots_ref, counts_ref, query_ref, cache_ref, fresh_ref, out_ref, bias_ref):
+def attention_body(slots_ref, counts_ref, query_ref, cache_ref, fresh_ref, out_ref, bias_ref, *, first):
     rows, _, positions, pair = cache_ref.shape
     head_dim = pair // 2
     group = query_ref.shape[1] // head_dim
@@ -70,8 +73,15 @@
     keys = cache_ref[:, 0, :, :head_dim]
     values = cache_ref[:, 0, :, head_dim:]
     fresh = fresh_ref[...].astype(jnp.float32)
-    scores = jnp.einsum("rgd,rpd->rgp", query, keys, preferred_element_type=jnp.float32) * scale
-    bias = bias_ref[pl.ds(pl.multiple_of(step * rows, rows), rows), :]
+    both = jnp.einsum(
+        "rgd,rpd->rgp",
+        query.reshape(rows // 2, 2 * group, head_dim),
+        keys.reshape(rows // 2, 2 * positions, head_dim),
+        preferred_element_type=jnp.float32,
+    )
+    scores = jnp.stack([both[:, :group, :positions], both[:, group:, positions:]], axis=1)
+    scores = scores.reshape(rows, group, positions) * scale
+    bias = bias_ref[pl.ds(pl.multiple_of((first + step) * rows, rows), rows), :]
     scores = scores + bias[:, None, :]
     own = jnp.sum(
         query.astype(jnp.float32) * fresh[:, None, :head_dim], axis=-1, keepdims=True
@@ -85,21 +95,23 @@
     out_ref[...] = (numer / denom).astype(jnp.bfloat16).reshape(rows, group * head_dim)
 
 
-def attention(slots, counts, queries, cache_pairs, fresh):
+def attention(slots, counts, queries, cache_pairs, fresh, part, parts):
     rows, width = queries.shape
-    block = min(ATT_BLOCK, rows)
-    return pl.pallas_call(
-        attention_body,
-        grid=(rows // block,),
+    block = min(ATT_BLOCK, rows // parts)
+    steps = rows // parts // block
+    first = part * steps
+    return pl.pallas_call(
+        functools.partial(attention_body, first=first),
+        grid=(steps,),
         in_specs=[
             pl.BlockSpec(slots.shape, lambda i: (0, 0)),
             pl.BlockSpec(counts.shape, lambda i: (0, 0)),
-            pl.BlockSpec((block, width), lambda i: (i, 0)),
-            pl.BlockSpec((block,) + cache_pairs.shape[1:], lambda i: (i, 0, 0, 0)),
-            pl.BlockSpec((block, fresh.shape[1]), lambda i: (i, 0)),
+            pl.BlockSpec((block, width), lambda i: (first + i, 0)),
+            pl.BlockSpec((block,) + cache_pairs.shape[1:], lambda i: (first + i, 0, 0, 0)),
+            pl.BlockSpec((block, fresh.shape[1]), lambda i: (first + i, 0)),
         ],
         out_specs=pl.BlockSpec((block, width), lambda i: (i, 0)),
-        out_shape=jax.ShapeDtypeStruct((rows, width), jnp.bfloat16),
+        out_shape=jax.ShapeDtypeStruct((rows // parts, width), jnp.bfloat16),
         scratch_shapes=[pltpu.VMEM((rows, cache_pairs.shape[2]), jnp.float32)],
         compiler_params=grant(24),
         name="attention",
@@ -108,23 +120,33 @@
 
 def project_body(here_ref, *refs):
     *head_refs, weight_ref, out_ref = refs
-    count = len(head_refs)
-    weight = weight_ref[...]
-    for step, head_ref in zip(STEPS, head_refs):
-        part = jnp.dot(head_ref[...], weight, preferred_element_type=jnp.float32)
-        out_ref[(here_ref[0] + (count - step)) & (count - 1)] = part.astype(jnp.bfloat16)
-
-
-def project(here, blocks, weight):
-    rows = blocks[0].shape[0]
+    earlier_ref = None
+    if len(head_refs) > len(STEPS):
+        earlier_ref, *head_refs = head_refs
+    count, half = len(STEPS), head_refs[0].shape[0]
+    heads = jnp.concatenate([r[...] for r in head_refs], axis=0)
+    made = jnp.dot(heads, weight_ref[...], preferred_element_type=jnp.float32)
+    made = made.astype(jnp.bfloat16)
+    start = 0
+    if earlier_ref is not None:
+        start = earlier_ref.shape[1]
+        out_ref[:, :start] = earlier_ref[...]
+    for n, step in enumerate(STEPS):
+        at = (here_ref[0] + (count - step)) & (count - 1)
+        out_ref[at, start : start + half] = made[n * half : (n + 1) * half]
+
+
+def project(here, earlier, blocks, weight):
+    rows = blocks[0].shape[0] + sum(e.shape[1] for e in earlier)
+    operands = [*earlier, *blocks, weight]
     return pl.pallas_call(
         project_body,
         in_specs=[pl.BlockSpec(memory_space=pltpu.SMEM)]
-        + [pl.BlockSpec(memory_space=pltpu.VMEM)] * (len(blocks) + 1),
+        + [pl.BlockSpec(memory_space=pltpu.VMEM)] * len(operands),
         out_shape=jax.ShapeDtypeStruct((len(blocks), rows, weight.shape[1]), jnp.bfloat16),
         compiler_params=grant(12),
         name="project",
-    )(here, *blocks, weight)
+    )(here, *operands)
 
 
 def norm_body(here_ref, parts_ref, stream_ref, gain_ref, routes_ref, codes_ref, residual_ref, payload_ref):
@@ -358,13 +380,20 @@
         capacity=min(rows, max(2, 2 * rows * routes.shape[1] // experts)),
     )
 
-    head_out = attention(
-        kept_slots[:, 0].T, segment_kept_count[:, 0].T, queries, cache_pairs, fresh_pairs[:, 0]
-    )
-    head_blocks = [head_out] + [
-        lax.ppermute(head_out, "seq", shift(seqs, d)) for d in STEPS[1:]
-    ]
-    parts = project(here, head_blocks, output_weight)
+    made = []
+    for part in range(ATT_PARTS):
+        head_out = attention(
+            kept_slots[:, 0].T,
+            segment_kept_count[:, 0].T,
+            queries,
+            cache_pairs,
+            fresh_pairs[:, 0],
+            part,
+            ATT_PARTS,
+        )
+        blocks = [head_out] + [lax.ppermute(head_out, "seq", shift(seqs, d)) for d in STEPS[1:]]
+        made = [project(here, made, blocks, output_weight)]
+    parts = made[0]
     parts = exchange(parts.reshape(-1, rows, parts.shape[-1]), ("seq",) + HEADS)
     parts = parts.reshape(seqs, -1, rows, parts.shape[-1])
     residual, payload = norm(

time: 132 us -> 130 us (0.985)
  waiting for transfers between devices: 20.4 us -> 15.3 us
  starting transfers between devices: 32.6 us -> 35.4 us
    ppermute x3 -> x6, waiting for transfers between devices: 10.6 us -> 5.49 us  [on_device(): lax.ppermute(head_out, 'seq', shift(seqs, d))]
    ppermute x3 -> x6, starting transfers between devices: 5.11 us -> 7.91 us  [on_device(): lax.ppermute(head_out, 'seq', shift(seqs, d))]
    pallas_call x1 -> x2, Pallas kernels: 7.35 us -> 8.02 us  [attention(): pl.pallas_call(functools.partial(attention_body, first=first), grid=(step...]
  transfers between devices with their start and end apart: 9 -> 12, of which waited for: 7 -> 7; matrix products, arithmetic and copies ran while one was open for 0% -> 0% of each run, Pallas kernels for 0% -> 4%
where the time goes in v6:
time: 130 us
  blocking collectives  58.6 us (45%)
  starting transfers between devices  35.4 us (27%)
  Pallas kernels  20.4 us (16%)
  waiting for transfers between devices  15.3 us (12%)
    all_to_all x3, blocking collectives, exchange(): return lax.all_to_all(blocks, axes, split_axis=0, concat_axis=0, tiled=True)  58.6 us
    ppermute x3, starting transfers between devices, on_device(): lax.ppermute(payload, ('zl', 'zh'), m)  21.5 us
    pallas_call x2, Pallas kernels, attention(): pl.pallas_call(functools.partial(attention_body, first=first), grid=(step...  8.02 us
    ppermute x6, starting transfers between devices, on_device(): lax.ppermute(head_out, 'seq', shift(seqs, d))  7.91 us
    pallas_call x1, Pallas kernels, expert(): pl.pallas_call(expert_body, in_specs=[pl.BlockSpec(memory_space=pltpu.VME...  6.77 us
    ppermute x3, starting transfers between devices, on_device(): sums = [lax.ppermute(v, ('zl', 'zh'), m) for v, m in zip(sums, back)]  6.06 us
    ppermute x3, waiting for transfers between devices, on_device(): lax.ppermute(payload, ('zl', 'zh'), m)  5.65 us
    ppermute x6, waiting for transfers between devices, on_device(): lax.ppermute(head_out, 'seq', shift(seqs, d))  5.49 us
  transfers between devices with their start and end apart: 12, of which 7 were waited for; matrix products, arithmetic and copies ran while one was open for 0% of the time, Pallas kernels for 4%

profile of v6, /device:TPU:1, one launch (start us, length us, event | category | flops | bytes accessed | tf_op | source)
XLA Modules:
  0.0 130.0 jit_solution(18088267644623300764)
XLA Ops:
  0.0 4.0 %attention.2.refs_0_ = bf16[64,1024]{1,0:T(8,128)(2,1)S(1)} custom-call(s32[96,128]{1,0:T(8,128)} %bitcast.30, s32[4,128]{1,0:T(4,128)} %bitcast.32, bf16[128,1024]{1,0:T(8,128)(2,1)} %query_ref.3, bf16[128,1,128,256]{3,2,1,0:T(8,128)(2,1)} %cache_ref.3, bf16[128,256]{1,0:T(8,128)(2,1)} %bitcast.28), custom_call_target="tpu_custom_call" | custom-call | tf_op jit(solution)/shard_map/attention/pallas_call | solution.py:103
  4.0 3.6 %collective-permute-start.2 = (bf16[64,1024]{1,0:T(8,128)(2,1)S(1)}, bf16[64,1024]{1,0:T(8,128)(2,1)S(1)}, u32[]{:S(2)}, u32[]{:S(2)}) collective-permute-start(bf16[64,1024]{1,0:T(8,128)(2,1)S(1)} %attention.2.refs_0_), channel_id=1, source_target_pairs={{0,32},{16,48},{32,0},{48,16},{1,33},{17,49},{33,1},{49,17},{2,34}... | collective-permute-start | bytes 393224 | tf_op jit(solution)/shard_map/ppermute | solution.py:394
  7.7 0.9 collective-permute-start.1
  9.1 4.0 %attention.3.refs_1_ = bf16[64,1024]{1,0:T(8,128)(2,1)S(1)} custom-call(s32[96,128]{1,0:T(8,128)} %bitcast.31, s32[4,128]{1,0:T(4,128)} %bitcast.33, bf16[128,1024]{1,0:T(8,128)(2,1)} %query_ref.3, bf16[128,1,128,256]{3,2,1,0:T(8,128)(2,1)} %cache_ref.3, bf16[128,256]{1,0:T(8,128)(2,1)} %bitcast.29), custom_call_target="tpu_custom_call" | custom-call | tf_op jit(solution)/shard_map/attention/pallas_call | solution.py:103
  13.9 2.1 %collective-permute-start.4 = (bf16[64,1024]{1,0:T(8,128)(2,1)S(1)}, bf16[64,1024]{1,0:T(8,128)(2,1)S(1)}, u32[]{:S(2)}, u32[]{:S(2)}) collective-permute-start(bf16[64,1024]{1,0:T(8,128)(2,1)S(1)} %attention.3.refs_1_), channel_id=1, source_target_pairs={{0,48},{16,0},{32,16},{48,32},{1,49},{17,1},{33,17},{49,33},{2,50}... | collective-permute-start | bytes 393224 | tf_op jit(solution)/shard_map/ppermute | solution.py:394
  16.1 1.0 project.2.refs_0_
  17.1 1.5 %collective-permute-done.5.refs_4_ = bf16[64,1024]{1,0:T(8,128)(2,1)S(1)} collective-permute-done((bf16[64,1024]{1,0:T(8,128)(2,1)S(1)}, bf16[64,1024]{1,0:T(8,128)(2,1)S(1)}, u32[]{:S(2)}, u32[]{:S(2)}) %collective-permute-start.5) | collective-permute-done | bytes 131104 | tf_op jit(solution)/shard_map/ppermute | solution.py:394
  18.6 2.2 %collective-permute-done.4.refs_3_ = bf16[64,1024]{1,0:T(8,128)(2,1)S(1)} collective-permute-done((bf16[64,1024]{1,0:T(8,128)(2,1)S(1)}, bf16[64,1024]{1,0:T(8,128)(2,1)S(1)}, u32[]{:S(2)}, u32[]{:S(2)}) %collective-permute-start.4) | collective-permute-done | bytes 131104 | tf_op jit(solution)/shard_map/ppermute | solution.py:394
  20.8 1.7 %collective-permute-done.3.refs_2_ = bf16[64,1024]{1,0:T(8,128)(2,1)S(1)} collective-permute-done((bf16[64,1024]{1,0:T(8,128)(2,1)S(1)}, bf16[64,1024]{1,0:T(8,128)(2,1)S(1)}, u32[]{:S(2)}, u32[]{:S(2)}) %collective-permute-start.3) | collective-permute-done | bytes 131104 | tf_op jit(solution)/shard_map/ppermute | solution.py:394
  22.6 1.0 project.3
  23.6 15.7 %all_to_all.15 = bf16[16,32,512]{2,1,0:T(8,128)(2,1)S(1)} all-to-all(bf16[16,32,512]{2,1,0:T(8,128)(2,1)S(1)} %bitcast.22), channel_id=1, replica_groups=mesh['zl'=2,'core'=2,'seq'=4,'zh'=4,'y'=4] {'seq','zl','core'}, dimensions={0} | all-to-all | bytes 1048576 | tf_op jit(solution)/shard_map/all_to_all | solution.py:355
  40.0 20.2 %collective-permute-start.8 = (bf16[32,2176]{1,0:T(8,128)(2,1)S(1)}, bf16[32,2176]{1,0:T(8,128)(2,1)S(1)}, u32[]{:S(2)}, u32[]{:S(2)}) collective-permute-start(bf16[32,2176]{1,0:T(8,128)(2,1)S(1)} %get-tuple-element.15.refs_1_), channel_id=1, source_target_pairs={{0,136},{128,8},{4,140},{132,12},{8,128},{136,0},{12,132},{140,4},... | collective-permute-start | bytes 417800 | tf_op jit(solution)/shard_map/ppermute | solution.py:403
  60.2 1.3 collective-permute-start.6
  61.5 2.2 %collective-permute-done.8.refs_4_ = bf16[32,2176]{1,0:T(8,128)(2,1)S(1)} collective-permute-done((bf16[32,2176]{1,0:T(8,128)(2,1)S(1)}, bf16[32,2176]{1,0:T(8,128)(2,1)S(1)}, u32[]{:S(2)}, u32[]{:S(2)}) %collective-permute-start.8) | collective-permute-done | bytes 139296 | tf_op jit(solution)/shard_map/ppermute | solution.py:403
  63.7 3.4 %collective-permute-done.7.refs_3_ = bf16[32,2176]{1,0:T(8,128)(2,1)S(1)} collective-permute-done((bf16[32,2176]{1,0:T(8,128)(2,1)S(1)}, bf16[32,2176]{1,0:T(8,128)(2,1)S(1)}, u32[]{:S(2)}, u32[]{:S(2)}) %collective-permute-start.7) | collective-permute-done | bytes 139296 | tf_op jit(solution)/shard_map/ppermute | solution.py:403
  67.1 1.8 %dispatch.1 = (bf16[512,2048]{1,0:T(8,128)(2,1)S(1)}, bf16[128,512]{1,0:T(8,128)(2,1)S(1)}, f32[128,128]{1,0:T(8,128)S(1)}) custom-call(s32[3]{0:T(128)S(1)} %pad_add_fusion.here_ref.refs_0_, bf16[32,2176]{1,0:T(8,128)(2,1)S(1)} %get-tuple-element.15.refs_1_, bf16[32,2176]{1,0:T(8,128)(2,1)S(1)} %collective-permute-done.6.refs_2_, ...), custom_call_target="tpu_custom_call" | custom-call | tf_op jit(solution)/shard_map/dispatch/pallas_call | solution.py:253
  68.9 21.9 %all_to_all.16 = bf16[16,32,2048]{2,1,0:T(8,128)(2,1)S(1)} all-to-all(bf16[16,32,2048]{2,1,0:T(8,128)(2,1)S(1)} %bitcast.23), channel_id=1, replica_groups=mesh['zl'=2,'core'=2,'seq'=4,'zh'=4,'y'=4] {'seq','y'}, dimensions={0} | all-to-all | bytes 4194304 | tf_op jit(solution)/shard_map/all_to_all | solution.py:355
  90.8 6.8 %expert.1 = bf16[512,2048]{1,0:T(8,128)(2,1)S(1)} custom-call(bf16[512,2048]{1,0:T(8,128)(2,1)S(1)} %bitcast.20, bf16[1,2048,768]{2,1,0:T(8,128)(2,1)S(1)} %copy-done.1, bf16[1,2048,768]{2,1,0:T(8,128)(2,1)S(1)} %copy-done.2, bf16[1,768,2048]{2,1,0:T(8,128)(2,1)} %down_hbm.1), custom_call_target="tpu_custom_call" | custom-call | tf_op jit(solution)/shard_map/expert/pallas_call | solution.py:284
  97.6 21.0 %all_to_all.17 = bf16[16,32,2048]{2,1,0:T(8,128)(2,1)S(1)} all-to-all(bf16[16,32,2048]{2,1,0:T(8,128)(2,1)S(1)} %bitcast.21), channel_id=1, replica_groups=mesh['zl'=2,'core'=2,'seq'=4,'zh'=4,'y'=4] {'seq','y'}, dimensions={0} | all-to-all | bytes 4194304 | tf_op jit(solution)/shard_map/all_to_all | solution.py:355
  119.0 1.6 %collective-permute-start.9 = (bf16[32,2048]{1,0:T(8,128)(2,1)S(1)}, bf16[32,2048]{1,0:T(8,128)(2,1)S(1)}, u32[]{:S(2)}, u32[]{:S(2)}) collective-permute-start(bf16[32,2048]{1,0:T(8,128)(2,1)S(1)} %get-tuple-element.20), channel_id=1, source_target_pairs={{4,0},{140,128},{8,4},{128,132},{12,8},{132,136},{0,12},{136,140},... | collective-permute-start | bytes 393224 | tf_op jit(solution)/shard_map/ppermute | solution.py:408
  120.6 1.8 %collective-permute-start.10 = (bf16[32,2048]{1,0:T(8,128)(2,1)S(1)}, bf16[32,2048]{1,0:T(8,128)(2,1)S(1)}, u32[]{:S(2)}, u32[]{:S(2)}) collective-permute-start(bf16[32,2048]{1,0:T(8,128)(2,1)S(1)} %get-tuple-element.21), channel_id=1, source_target_pairs={{140,0},{4,128},{128,4},{8,132},{132,8},{12,136},{136,12},{0,140},... | collective-permute-start | bytes 393224 | tf_op jit(solution)/shard_map/ppermute | solution.py:408
  122.5 2.6 %collective-permute-start.11 = (bf16[32,2048]{1,0:T(8,128)(2,1)S(1)}, bf16[32,2048]{1,0:T(8,128)(2,1)S(1)}, u32[]{:S(2)}, u32[]{:S(2)}) collective-permute-start(bf16[32,2048]{1,0:T(8,128)(2,1)S(1)} %get-tuple-element.22), channel_id=1, source_target_pairs={{136,0},{8,128},{140,4},{12,132},{128,8},{0,136},{132,12},{4,140},... | collective-permute-start | bytes 393224 | tf_op jit(solution)/shard_map/ppermute | solution.py:408
  125.1 1.1 collective-permute-done.10.refs_2_
  126.2 3.1 %collective-permute-done.11.refs_3_ = bf16[32,2048]{1,0:T(8,128)(2,1)S(1)} collective-permute-done((bf16[32,2048]{1,0:T(8,128)(2,1)S(1)}, bf16[32,2048]{1,0:T(8,128)(2,1)S(1)}, u32[]{:S(2)}, u32[]{:S(2)}) %collective-permute-start.11) | collective-permute-done | bytes 131104 | tf_op jit(solution)/shard_map/ppermute | solution.py:408
  (27 shorter events, 3.4 us)
Async XLA Ops:
  4.0 12.1 %copy-start = (bf16[1024,512]{1,0:T(8,128)(2,1)S(1)}, bf16[1024,512]{1,0:T(8,128)(2,1)}, u32[]{:S(2)}) copy-start(bf16[1024,512]{1,0:T(8,128)(2,1)} %refs_5_.1) | copy-start | bytes 3145732
  4.0 12.0 %collective-permute-start.2 = (bf16[64,1024]{1,0:T(8,128)(2,1)S(1)}, bf16[64,1024]{1,0:T(8,128)(2,1)S(1)}, u32[]{:S(2)}, u32[]{:S(2)}) collective-permute-start(bf16[64,1024]{1,0:T(8,128)(2,1)S(1)} %attention.2.refs_0_), channel_id=1, source_target_pairs={{0,32},{16,48},{32,0},{48,16},{1,33},{17,49},{33,1},{49,17},{2,34}... | collective-permute-start | bytes 393224 | tf_op jit(solution)/shard_map/ppermute | solution.py:394
  7.7 8.4 %collective-permute-start.1 = (bf16[64,1024]{1,0:T(8,128)(2,1)S(1)}, bf16[64,1024]{1,0:T(8,128)(2,1)S(1)}, u32[]{:S(2)}, u32[]{:S(2)}) collective-permute-start(bf16[64,1024]{1,0:T(8,128)(2,1)S(1)} %attention.2.refs_0_), channel_id=1, source_target_pairs={{0,48},{16,0},{32,16},{48,32},{1,49},{17,1},{33,17},{49,33},{2,50}... | collective-permute-start | bytes 393224 | tf_op jit(solution)/shard_map/ppermute | solution.py:394
  8.5 7.6 %collective-permute-start = (bf16[64,1024]{1,0:T(8,128)(2,1)S(1)}, bf16[64,1024]{1,0:T(8,128)(2,1)S(1)}, u32[]{:S(2)}, u32[]{:S(2)}) collective-permute-start(bf16[64,1024]{1,0:T(8,128)(2,1)S(1)} %attention.2.refs_0_), channel_id=1, source_target_pairs={{0,16},{16,32},{32,48},{48,0},{1,17},{17,33},{33,49},{49,1},{2,18}... | collective-permute-start | bytes 393224 | tf_op jit(solution)/shard_map/ppermute | solution.py:394
  13.2 26.1 %copy-start.3 = (bf16[32,2048]{1,0:T(8,128)(2,1)S(1)}, bf16[32,2048]{1,0:T(8,128)(2,1)}, u32[]{:S(2)}) copy-start(bf16[32,2048]{1,0:T(8,128)(2,1)} %stream_ref.1) | copy-start | bytes 393220
  13.2 26.1 %copy-start.4 = (f32[2048]{0:T(1024)S(1)}, f32[2048]{0:T(1024)}, u32[]{:S(2)}) copy-start(f32[2048]{0:T(1024)} %param.20) | copy-start | bytes 24580
  13.2 26.1 %copy-start.5 = (s32[32,8]{0,1:T(8,128)S(1)}, s32[32,8]{0,1:T(8,128)}, u32[]{:S(2)}) copy-start(s32[32,8]{0,1:T(8,128)} %param.21) | copy-start | bytes 3076
  13.2 26.1 %copy-start.6 = (s32[32,8]{0,1:T(8,128)S(1)}, s32[32,8]{0,1:T(8,128)}, u32[]{:S(2)}) copy-start(s32[32,8]{0,1:T(8,128)} %param.22) | copy-start | bytes 3076
  13.2 5.4 %collective-permute-start.5 = (bf16[64,1024]{1,0:T(8,128)(2,1)S(1)}, bf16[64,1024]{1,0:T(8,128)(2,1)S(1)}, u32[]{:S(2)}, u32[]{:S(2)}) collective-permute-start(bf16[64,1024]{1,0:T(8,128)(2,1)S(1)} %attention.3.refs_1_), channel_id=1, source_target_pairs={{0,32},{16,48},{32,0},{48,16},{1,33},{17,49},{33,1},{49,17},{2,34}... | collective-permute-start | bytes 393224 | tf_op jit(solution)/shard_map/ppermute | solution.py:394
  13.9 6.9 %collective-permute-start.4 = (bf16[64,1024]{1,0:T(8,128)(2,1)S(1)}, bf16[64,1024]{1,0:T(8,128)(2,1)S(1)}, u32[]{:S(2)}, u32[]{:S(2)}) collective-permute-start(bf16[64,1024]{1,0:T(8,128)(2,1)S(1)} %attention.3.refs_1_), channel_id=1, source_target_pairs={{0,48},{16,0},{32,16},{48,32},{1,49},{17,1},{33,17},{49,33},{2,50}... | collective-permute-start | bytes 393224 | tf_op jit(solution)/shard_map/ppermute | solution.py:394
  16.0 6.6 %collective-permute-start.3 = (bf16[64,1024]{1,0:T(8,128)(2,1)S(1)}, bf16[64,1024]{1,0:T(8,128)(2,1)S(1)}, u32[]{:S(2)}, u32[]{:S(2)}) collective-permute-start(bf16[64,1024]{1,0:T(8,128)(2,1)S(1)} %attention.3.refs_1_), channel_id=1, source_target_pairs={{0,16},{16,32},{32,48},{48,0},{1,17},{17,33},{33,49},{49,1},{2,18}... | collective-permute-start | bytes 393224 | tf_op jit(solution)/shard_map/ppermute | solution.py:394
  23.5 67.2 %copy-start.1 = (bf16[1,2048,768]{2,1,0:T(8,128)(2,1)S(1)}, bf16[1,2048,768]{2,1,0:T(8,128)(2,1)}, u32[]{:S(2)}) copy-start(bf16[1,2048,768]{2,1,0:T(8,128)(2,1)} %gate_ref.1) | copy-start | bytes 9437188
  23.6 67.2 %copy-start.2 = (bf16[1,2048,768]{2,1,0:T(8,128)(2,1)S(1)}, bf16[1,2048,768]{2,1,0:T(8,128)(2,1)}, u32[]{:S(2)}) copy-start(bf16[1,2048,768]{2,1,0:T(8,128)(2,1)} %up_ref.1) | copy-start | bytes 9437188
  40.0 23.7 %collective-permute-start.8 = (bf16[32,2176]{1,0:T(8,128)(2,1)S(1)}, bf16[32,2176]{1,0:T(8,128)(2,1)S(1)}, u32[]{:S(2)}, u32[]{:S(2)}) collective-permute-start(bf16[32,2176]{1,0:T(8,128)(2,1)S(1)} %get-tuple-element.15.refs_1_), channel_id=1, source_target_pairs={{0,136},{128,8},{4,140},{132,12},{8,128},{136,0},{12,132},{140,4},... | collective-permute-start | bytes 417800 | tf_op jit(solution)/shard_map/ppermute | solution.py:403
  60.2 6.9 %collective-permute-start.7 = (bf16[32,2176]{1,0:T(8,128)(2,1)S(1)}, bf16[32,2176]{1,0:T(8,128)(2,1)S(1)}, u32[]{:S(2)}, u32[]{:S(2)}) collective-permute-start(bf16[32,2176]{1,0:T(8,128)(2,1)S(1)} %get-tuple-element.15.refs_1_), channel_id=1, source_target_pairs={{0,140},{128,4},{4,128},{132,8},{8,132},{136,12},{12,136},{140,0},... | collective-permute-start | bytes 417800 | tf_op jit(solution)/shard_map/ppermute | solution.py:403
  60.2 6.9 %collective-permute-start.6 = (bf16[32,2176]{1,0:T(8,128)(2,1)S(1)}, bf16[32,2176]{1,0:T(8,128)(2,1)S(1)}, u32[]{:S(2)}, u32[]{:S(2)}) collective-permute-start(bf16[32,2176]{1,0:T(8,128)(2,1)S(1)} %get-tuple-element.15.refs_1_), channel_id=1, source_target_pairs={{0,4},{128,140},{4,8},{132,128},{8,12},{136,132},{12,0},{140,136},... | collective-permute-start | bytes 417800 | tf_op jit(solution)/shard_map/ppermute | solution.py:403
  119.0 6.1 %collective-permute-start.9 = (bf16[32,2048]{1,0:T(8,128)(2,1)S(1)}, bf16[32,2048]{1,0:T(8,128)(2,1)S(1)}, u32[]{:S(2)}, u32[]{:S(2)}) collective-permute-start(bf16[32,2048]{1,0:T(8,128)(2,1)S(1)} %get-tuple-element.20), channel_id=1, source_target_pairs={{4,0},{140,128},{8,4},{128,132},{12,8},{132,136},{0,12},{136,140},... | collective-permute-start | bytes 393224 | tf_op jit(solution)/shard_map/ppermute | solution.py:408
  120.6 5.6 %collective-permute-start.10 = (bf16[32,2048]{1,0:T(8,128)(2,1)S(1)}, bf16[32,2048]{1,0:T(8,128)(2,1)S(1)}, u32[]{:S(2)}, u32[]{:S(2)}) collective-permute-start(bf16[32,2048]{1,0:T(8,128)(2,1)S(1)} %get-tuple-element.21), channel_id=1, source_target_pairs={{140,0},{4,128},{128,4},{8,132},{132,8},{12,136},{136,12},{0,140},... | collective-permute-start | bytes 393224 | tf_op jit(solution)/shard_map/ppermute | solution.py:408
  122.5 6.8 %collective-permute-start.11 = (bf16[32,2048]{1,0:T(8,128)(2,1)S(1)}, bf16[32,2048]{1,0:T(8,128)(2,1)S(1)}, u32[]{:S(2)}, u32[]{:S(2)}) collective-permute-start(bf16[32,2048]{1,0:T(8,128)(2,1)S(1)} %get-tuple-element.22), channel_id=1, source_target_pairs={{136,0},{8,128},{140,4},{12,132},{128,8},{0,136},{132,12},{4,140},... | collective-permute-start | bytes 393224 | tf_op jit(solution)/shard_map/ppermute | solution.py:408

commit v7 on v6

--- a/solution.py
+++ b/solution.py
@@ -10,9 +10,9 @@
 
 epsilon = 1e-06
 LANES = 128
-OFFSET_NS = 14000
+OFFSET_NS = 13500
 ATT_BLOCK = 32
-ATT_PARTS = 2
+ATT_PARTS = (3, 1)
 MESH_AXES = ("zl", "core", "seq", "zh", "y")
 PLANE = ("seq", "y")
 HEADS = ("zl", "core")
@@ -95,11 +95,9 @@
     out_ref[...] = (numer / denom).astype(jnp.bfloat16).reshape(rows, group * head_dim)
 
 
-def attention(slots, counts, queries, cache_pairs, fresh, part, parts):
+def attention(slots, counts, queries, cache_pairs, fresh, first, steps):
     rows, width = queries.shape
-    block = min(ATT_BLOCK, rows // parts)
-    steps = rows // parts // block
-    first = part * steps
+    block = ATT_BLOCK
     return pl.pallas_call(
         functools.partial(attention_body, first=first),
         grid=(steps,),
@@ -111,7 +109,7 @@
             pl.BlockSpec((block, fresh.shape[1]), lambda i: (first + i, 0)),
         ],
         out_specs=pl.BlockSpec((block, width), lambda i: (i, 0)),
-        out_shape=jax.ShapeDtypeStruct((rows // parts, width), jnp.bfloat16),
+        out_shape=jax.ShapeDtypeStruct((steps * block, width), jnp.bfloat16),
         scratch_shapes=[pltpu.VMEM((rows, cache_pairs.shape[2]), jnp.float32)],
         compiler_params=grant(24),
         name="attention",
@@ -237,9 +235,12 @@
     top = static["top"]
     tail = jnp.concatenate([r[:, wide:].astype(jnp.float32) for r in payload_refs], axis=0)
     code = placement(tail, here_ref[1], planes, **static)
-    place = jnp.where(code > 0.0, 1.0, 0.0).T.astype(jnp.bfloat16)
+    place = jnp.where(code > 0.0, 1.0, 0.0).astype(jnp.bfloat16)
     tokens = jnp.concatenate([r[:, :wide] for r in payload_refs], axis=0)
-    out_ref[...] = jnp.dot(place, tokens, preferred_element_type=jnp.float32).astype(jnp.bfloat16)
+    sent = lax.dot_general(
+        place, tokens, (((0,), (0,)), ((), ())), preferred_element_type=jnp.float32
+    )
+    out_ref[...] = sent.astype(jnp.bfloat16)
     code_ref[...] = code.astype(jnp.bfloat16)
     lane = iota(tail.shape, 1)
     listed = jnp.where((lane >= top) & (lane < 2 * top), tail, 0.0)
@@ -381,15 +382,15 @@
     )
 
     made = []
-    for part in range(ATT_PARTS):
+    for part, steps in enumerate(ATT_PARTS):
         head_out = attention(
             kept_slots[:, 0].T,
             segment_kept_count[:, 0].T,
             queries,
             cache_pairs,
             fresh_pairs[:, 0],
-            part,
-            ATT_PARTS,
+            sum(ATT_PARTS[:part]),
+            steps,
         )
         blocks = [head_out] + [lax.ppermute(head_out, "seq", shift(seqs, d)) for d in STEPS[1:]]
         made = [project(here, made, blocks, output_weight)]

time: 130 us -> 130 us (level)
  transfers between devices with their start and end apart: 12 -> 12, of which waited for: 7 -> 7; matrix products, arithmetic and copies ran while one was open for 0% -> 0% of each run, Pallas kernels for 4% -> 3%
where the time goes in v7:
time: 130 us; the launch traced here: 129 us
  blocking collectives  59 us (45%)
  starting transfers between devices  35.1 us (27%)
  Pallas kernels  20.6 us (16%)
  waiting for transfers between devices  14.4 us (11%)
    all_to_all x3, blocking collectives, exchange(): return lax.all_to_all(blocks, axes, split_axis=0, concat_axis=0, tiled=True)  59 us
    ppermute x3, starting transfers between devices, on_device(): lax.ppermute(payload, ('zl', 'zh'), m)  21 us
    pallas_call x2, Pallas kernels, attention(): pl.pallas_call(functools.partial(attention_body, first=first), grid=(step...  8.14 us
    ppermute x6, starting transfers between devices, on_device(): lax.ppermute(head_out, 'seq', shift(seqs, d))  7.92 us
    pallas_call x1, Pallas kernels, expert(): pl.pallas_call(expert_body, in_specs=[pl.BlockSpec(memory_space=pltpu.VME...  6.77 us
    ppermute x3, starting transfers between devices, on_device(): sums = [lax.ppermute(v, ('zl', 'zh'), m) for v, m in zip(sums, back)]  6.24 us
    ppermute x3, waiting for transfers between devices, on_device(): lax.ppermute(payload, ('zl', 'zh'), m)  5.65 us
    ppermute x6, waiting for transfers between devices, on_device(): lax.ppermute(head_out, 'seq', shift(seqs, d))  4.81 us
  transfers between devices with their start and end apart: 12, of which 7 were waited for; matrix products, arithmetic and copies ran while one was open for 0% of the time, Pallas kernels for 3%

profile of v7, /device:TPU:1, one launch (start us, length us, event | category | flops | bytes accessed | tf_op | source)
XLA Modules:
  0.0 129.4 jit_solution(7952079262263472201)
XLA Ops:
  0.0 5.6 %attention.2.refs_0_ = bf16[96,1024]{1,0:T(8,128)(2,1)S(1)} custom-call(s32[96,128]{1,0:T(8,128)} %bitcast.30, s32[4,128]{1,0:T(4,128)} %bitcast.32, bf16[128,1024]{1,0:T(8,128)(2,1)} %query_ref.3, bf16[128,1,128,256]{3,2,1,0:T(8,128)(2,1)} %cache_ref.3, bf16[128,256]{1,0:T(8,128)(2,1)} %bitcast.28), custom_call_target="tpu_custom_call" | custom-call | tf_op jit(solution)/shard_map/attention/pallas_call | solution.py:101
  5.6 3.6 %collective-permute-start.2 = (bf16[96,1024]{1,0:T(8,128)(2,1)S(1)}, bf16[96,1024]{1,0:T(8,128)(2,1)S(1)}, u32[]{:S(2)}, u32[]{:S(2)}) collective-permute-start(bf16[96,1024]{1,0:T(8,128)(2,1)S(1)} %attention.2.refs_0_), channel_id=1, source_target_pairs={{0,32},{16,48},{32,0},{48,16},{1,33},{17,49},{33,1},{49,17},{2,34}... | collective-permute-start | bytes 589832 | tf_op jit(solution)/shard_map/ppermute | solution.py:395
  9.2 0.9 collective-permute-start.1
  10.7 2.6 %attention.3.refs_1_ = bf16[32,1024]{1,0:T(8,128)(2,1)S(1)} custom-call(s32[96,128]{1,0:T(8,128)} %bitcast.31, s32[4,128]{1,0:T(4,128)} %bitcast.33, bf16[128,1024]{1,0:T(8,128)(2,1)} %query_ref.3, bf16[128,1,128,256]{3,2,1,0:T(8,128)(2,1)} %cache_ref.3, bf16[128,256]{1,0:T(8,128)(2,1)} %bitcast.29), custom_call_target="tpu_custom_call" | custom-call | tf_op jit(solution)/shard_map/attention/pallas_call | solution.py:101
  14.1 2.1 %collective-permute-start.4 = (bf16[32,1024]{1,0:T(8,128)(2,1)S(1)}, bf16[32,1024]{1,0:T(8,128)(2,1)S(1)}, u32[]{:S(2)}, u32[]{:S(2)}) collective-permute-start(bf16[32,1024]{1,0:T(8,128)(2,1)S(1)} %attention.3.refs_1_), channel_id=1, source_target_pairs={{0,48},{16,0},{32,16},{48,32},{1,49},{17,1},{33,17},{49,33},{2,50}... | collective-permute-start | bytes 196616 | tf_op jit(solution)/shard_map/ppermute | solution.py:395
  16.2 2.4 %collective-permute-done.1.refs_2_ = bf16[96,1024]{1,0:T(8,128)(2,1)S(1)} collective-permute-done((bf16[96,1024]{1,0:T(8,128)(2,1)S(1)}, bf16[96,1024]{1,0:T(8,128)(2,1)S(1)}, u32[]{:S(2)}, u32[]{:S(2)}) %collective-permute-start.1) | collective-permute-done | bytes 196640 | tf_op jit(solution)/shard_map/ppermute | solution.py:395
  18.6 1.4 %collective-permute-done.refs_1_ = bf16[96,1024]{1,0:T(8,128)(2,1)S(1)} collective-permute-done((bf16[96,1024]{1,0:T(8,128)(2,1)S(1)}, bf16[96,1024]{1,0:T(8,128)(2,1)S(1)}, u32[]{:S(2)}, u32[]{:S(2)}) %collective-permute-start) | collective-permute-done | bytes 196640 | tf_op jit(solution)/shard_map/ppermute | solution.py:395
  20.0 1.1 project.2.refs_0_
  21.1 1.1 collective-permute-done.3.refs_2_
  22.2 0.8 project.3
  23.0 15.6 %all_to_all.15 = bf16[16,32,512]{2,1,0:T(8,128)(2,1)S(1)} all-to-all(bf16[16,32,512]{2,1,0:T(8,128)(2,1)S(1)} %bitcast.22), channel_id=1, replica_groups=mesh['zl'=2,'core'=2,'seq'=4,'zh'=4,'y'=4] {'seq','zl','core'}, dimensions={0} | all-to-all | bytes 1048576 | tf_op jit(solution)/shard_map/all_to_all | solution.py:356
  39.4 19.7 %collective-permute-start.8 = (bf16[32,2176]{1,0:T(8,128)(2,1)S(1)}, bf16[32,2176]{1,0:T(8,128)(2,1)S(1)}, u32[]{:S(2)}, u32[]{:S(2)}) collective-permute-start(bf16[32,2176]{1,0:T(8,128)(2,1)S(1)} %get-tuple-element.15.refs_1_), channel_id=1, source_target_pairs={{0,136},{128,8},{4,140},{132,12},{8,128},{136,0},{12,132},{140,4},... | collective-permute-start | bytes 417800 | tf_op jit(solution)/shard_map/ppermute | solution.py:404
  59.1 1.3 collective-permute-start.6
  60.4 2.2 %collective-permute-done.8.refs_4_ = bf16[32,2176]{1,0:T(8,128)(2,1)S(1)} collective-permute-done((bf16[32,2176]{1,0:T(8,128)(2,1)S(1)}, bf16[32,2176]{1,0:T(8,128)(2,1)S(1)}, u32[]{:S(2)}, u32[]{:S(2)}) %collective-permute-start.8) | collective-permute-done | bytes 139296 | tf_op jit(solution)/shard_map/ppermute | solution.py:404
  62.6 3.4 %collective-permute-done.7.refs_3_ = bf16[32,2176]{1,0:T(8,128)(2,1)S(1)} collective-permute-done((bf16[32,2176]{1,0:T(8,128)(2,1)S(1)}, bf16[32,2176]{1,0:T(8,128)(2,1)S(1)}, u32[]{:S(2)}, u32[]{:S(2)}) %collective-permute-start.7) | collective-permute-done | bytes 139296 | tf_op jit(solution)/shard_map/ppermute | solution.py:404
  66.0 1.8 %dispatch.1 = (bf16[512,2048]{1,0:T(8,128)(2,1)S(1)}, bf16[128,512]{1,0:T(8,128)(2,1)S(1)}, f32[128,128]{1,0:T(8,128)S(1)}) custom-call(s32[3]{0:T(128)S(1)} %pad_add_fusion.here_ref.refs_0_, bf16[32,2176]{1,0:T(8,128)(2,1)S(1)} %get-tuple-element.15.refs_1_, bf16[32,2176]{1,0:T(8,128)(2,1)S(1)} %collective-permute-done.6.refs_2_, ...), custom_call_target="tpu_custom_call" | custom-call | tf_op jit(solution)/shard_map/dispatch/pallas_call | solution.py:254
  67.8 21.7 %all_to_all.16 = bf16[16,32,2048]{2,1,0:T(8,128)(2,1)S(1)} all-to-all(bf16[16,32,2048]{2,1,0:T(8,128)(2,1)S(1)} %bitcast.23), channel_id=1, replica_groups=mesh['zl'=2,'core'=2,'seq'=4,'zh'=4,'y'=4] {'seq','y'}, dimensions={0} | all-to-all | bytes 4194304 | tf_op jit(solution)/shard_map/all_to_all | solution.py:356
  89.5 6.8 %expert.1 = bf16[512,2048]{1,0:T(8,128)(2,1)S(1)} custom-call(bf16[512,2048]{1,0:T(8,128)(2,1)S(1)} %bitcast.20, bf16[1,2048,768]{2,1,0:T(8,128)(2,1)S(1)} %copy-done.1, bf16[1,2048,768]{2,1,0:T(8,128)(2,1)S(1)} %copy-done.2, bf16[1,768,2048]{2,1,0:T(8,128)(2,1)} %down_hbm.1), custom_call_target="tpu_custom_call" | custom-call | tf_op jit(solution)/shard_map/expert/pallas_call | solution.py:285
  96.3 21.7 %all_to_all.17 = bf16[16,32,2048]{2,1,0:T(8,128)(2,1)S(1)} all-to-all(bf16[16,32,2048]{2,1,0:T(8,128)(2,1)S(1)} %bitcast.21), channel_id=1, replica_groups=mesh['zl'=2,'core'=2,'seq'=4,'zh'=4,'y'=4] {'seq','y'}, dimensions={0} | all-to-all | bytes 4194304 | tf_op jit(solution)/shard_map/all_to_all | solution.py:356
  118.5 1.9 %collective-permute-start.9 = (bf16[32,2048]{1,0:T(8,128)(2,1)S(1)}, bf16[32,2048]{1,0:T(8,128)(2,1)S(1)}, u32[]{:S(2)}, u32[]{:S(2)}) collective-permute-start(bf16[32,2048]{1,0:T(8,128)(2,1)S(1)} %get-tuple-element.20), channel_id=1, source_target_pairs={{4,0},{140,128},{8,4},{128,132},{12,8},{132,136},{0,12},{136,140},... | collective-permute-start | bytes 393224 | tf_op jit(solution)/shard_map/ppermute | solution.py:409
  120.4 1.4 %collective-permute-start.10 = (bf16[32,2048]{1,0:T(8,128)(2,1)S(1)}, bf16[32,2048]{1,0:T(8,128)(2,1)S(1)}, u32[]{:S(2)}, u32[]{:S(2)}) collective-permute-start(bf16[32,2048]{1,0:T(8,128)(2,1)S(1)} %get-tuple-element.21), channel_id=1, source_target_pairs={{140,0},{4,128},{128,4},{8,132},{132,8},{12,136},{136,12},{0,140},... | collective-permute-start | bytes 393224 | tf_op jit(solution)/shard_map/ppermute | solution.py:409
  121.8 2.9 %collective-permute-start.11 = (bf16[32,2048]{1,0:T(8,128)(2,1)S(1)}, bf16[32,2048]{1,0:T(8,128)(2,1)S(1)}, u32[]{:S(2)}, u32[]{:S(2)}) collective-permute-start(bf16[32,2048]{1,0:T(8,128)(2,1)S(1)} %get-tuple-element.22), channel_id=1, source_target_pairs={{136,0},{8,128},{140,4},{12,132},{128,8},{0,136},{132,12},{4,140},... | collective-permute-start | bytes 393224 | tf_op jit(solution)/shard_map/ppermute | solution.py:409
  124.7 0.9 collective-permute-done.10.refs_2_
  125.6 3.1 %collective-permute-done.11.refs_3_ = bf16[32,2048]{1,0:T(8,128)(2,1)S(1)} collective-permute-done((bf16[32,2048]{1,0:T(8,128)(2,1)S(1)}, bf16[32,2048]{1,0:T(8,128)(2,1)S(1)}, u32[]{:S(2)}, u32[]{:S(2)}) %collective-permute-start.11) | collective-permute-done | bytes 131104 | tf_op jit(solution)/shard_map/ppermute | solution.py:409
  (27 shorter events, 3.4 us)
Async XLA Ops:
  5.6 14.4 %copy-start = (bf16[1024,512]{1,0:T(8,128)(2,1)S(1)}, bf16[1024,512]{1,0:T(8,128)(2,1)}, u32[]{:S(2)}) copy-start(bf16[1024,512]{1,0:T(8,128)(2,1)} %refs_5_.1) | copy-start | bytes 3145732
  5.6 10.5 %collective-permute-start.2 = (bf16[96,1024]{1,0:T(8,128)(2,1)S(1)}, bf16[96,1024]{1,0:T(8,128)(2,1)S(1)}, u32[]{:S(2)}, u32[]{:S(2)}) collective-permute-start(bf16[96,1024]{1,0:T(8,128)(2,1)S(1)} %attention.2.refs_0_), channel_id=1, source_target_pairs={{0,32},{16,48},{32,0},{48,16},{1,33},{17,49},{33,1},{49,17},{2,34}... | collective-permute-start | bytes 589832 | tf_op jit(solution)/shard_map/ppermute | solution.py:395
  9.2 9.4 %collective-permute-start.1 = (bf16[96,1024]{1,0:T(8,128)(2,1)S(1)}, bf16[96,1024]{1,0:T(8,128)(2,1)S(1)}, u32[]{:S(2)}, u32[]{:S(2)}) collective-permute-start(bf16[96,1024]{1,0:T(8,128)(2,1)S(1)} %attention.2.refs_0_), channel_id=1, source_target_pairs={{0,48},{16,0},{32,16},{48,32},{1,49},{17,1},{33,17},{49,33},{2,50}... | collective-permute-start | bytes 589832 | tf_op jit(solution)/shard_map/ppermute | solution.py:395
  10.1 9.9 %collective-permute-start = (bf16[96,1024]{1,0:T(8,128)(2,1)S(1)}, bf16[96,1024]{1,0:T(8,128)(2,1)S(1)}, u32[]{:S(2)}, u32[]{:S(2)}) collective-permute-start(bf16[96,1024]{1,0:T(8,128)(2,1)S(1)} %attention.2.refs_0_), channel_id=1, source_target_pairs={{0,16},{16,32},{32,48},{48,0},{1,17},{17,33},{33,49},{49,1},{2,18}... | collective-permute-start | bytes 589832 | tf_op jit(solution)/shard_map/ppermute | solution.py:395
  13.3 25.3 %copy-start.3 = (bf16[32,2048]{1,0:T(8,128)(2,1)S(1)}, bf16[32,2048]{1,0:T(8,128)(2,1)}, u32[]{:S(2)}) copy-start(bf16[32,2048]{1,0:T(8,128)(2,1)} %stream_ref.1) | copy-start | bytes 393220
  13.3 25.3 %copy-start.4 = (f32[2048]{0:T(1024)S(1)}, f32[2048]{0:T(1024)}, u32[]{:S(2)}) copy-start(f32[2048]{0:T(1024)} %param.20) | copy-start | bytes 24580
  13.3 25.3 %copy-start.5 = (s32[32,8]{0,1:T(8,128)S(1)}, s32[32,8]{0,1:T(8,128)}, u32[]{:S(2)}) copy-start(s32[32,8]{0,1:T(8,128)} %param.21) | copy-start | bytes 3076
  13.3 25.3 %copy-start.6 = (s32[32,8]{0,1:T(8,128)S(1)}, s32[32,8]{0,1:T(8,128)}, u32[]{:S(2)}) copy-start(s32[32,8]{0,1:T(8,128)} %param.22) | copy-start | bytes 3076
  13.3 7.7 %collective-permute-start.5 = (bf16[32,1024]{1,0:T(8,128)(2,1)S(1)}, bf16[32,1024]{1,0:T(8,128)(2,1)S(1)}, u32[]{:S(2)}, u32[]{:S(2)}) collective-permute-start(bf16[32,1024]{1,0:T(8,128)(2,1)S(1)} %attention.3.refs_1_), channel_id=1, source_target_pairs={{0,32},{16,48},{32,0},{48,16},{1,33},{17,49},{33,1},{49,17},{2,34}... | collective-permute-start | bytes 196616 | tf_op jit(solution)/shard_map/ppermute | solution.py:395
  14.1 7.0 %collective-permute-start.4 = (bf16[32,1024]{1,0:T(8,128)(2,1)S(1)}, bf16[32,1024]{1,0:T(8,128)(2,1)S(1)}, u32[]{:S(2)}, u32[]{:S(2)}) collective-permute-start(bf16[32,1024]{1,0:T(8,128)(2,1)S(1)} %attention.3.refs_1_), channel_id=1, source_target_pairs={{0,48},{16,0},{32,16},{48,32},{1,49},{17,1},{33,17},{49,33},{2,50}... | collective-permute-start | bytes 196616 | tf_op jit(solution)/shard_map/ppermute | solution.py:395
  16.1 6.0 %collective-permute-start.3 = (bf16[32,1024]{1,0:T(8,128)(2,1)S(1)}, bf16[32,1024]{1,0:T(8,128)(2,1)S(1)}, u32[]{:S(2)}, u32[]{:S(2)}) collective-permute-start(bf16[32,1024]{1,0:T(8,128)(2,1)S(1)} %attention.3.refs_1_), channel_id=1, source_target_pairs={{0,16},{16,32},{32,48},{48,0},{1,17},{17,33},{33,49},{49,1},{2,18}... | collective-permute-start | bytes 196616 | tf_op jit(solution)/shard_map/ppermute | solution.py:395
  23.0 66.5 %copy-start.1 = (bf16[1,2048,768]{2,1,0:T(8,128)(2,1)S(1)}, bf16[1,2048,768]{2,1,0:T(8,128)(2,1)}, u32[]{:S(2)}) copy-start(bf16[1,2048,768]{2,1,0:T(8,128)(2,1)} %gate_ref.1) | copy-start | bytes 9437188
  23.0 66.5 %copy-start.2 = (bf16[1,2048,768]{2,1,0:T(8,128)(2,1)S(1)}, bf16[1,2048,768]{2,1,0:T(8,128)(2,1)}, u32[]{:S(2)}) copy-start(bf16[1,2048,768]{2,1,0:T(8,128)(2,1)} %up_ref.1) | copy-start | bytes 9437188
  39.4 23.2 %collective-permute-start.8 = (bf16[32,2176]{1,0:T(8,128)(2,1)S(1)}, bf16[32,2176]{1,0:T(8,128)(2,1)S(1)}, u32[]{:S(2)}, u32[]{:S(2)}) collective-permute-start(bf16[32,2176]{1,0:T(8,128)(2,1)S(1)} %get-tuple-element.15.refs_1_), channel_id=1, source_target_pairs={{0,136},{128,8},{4,140},{132,12},{8,128},{136,0},{12,132},{140,4},... | collective-permute-start | bytes 417800 | tf_op jit(solution)/shard_map/ppermute | solution.py:404
  59.1 6.9 %collective-permute-start.7 = (bf16[32,2176]{1,0:T(8,128)(2,1)S(1)}, bf16[32,2176]{1,0:T(8,128)(2,1)S(1)}, u32[]{:S(2)}, u32[]{:S(2)}) collective-permute-start(bf16[32,2176]{1,0:T(8,128)(2,1)S(1)} %get-tuple-element.15.refs_1_), channel_id=1, source_target_pairs={{0,140},{128,4},{4,128},{132,8},{8,132},{136,12},{12,136},{140,0},... | collective-permute-start | bytes 417800 | tf_op jit(solution)/shard_map/ppermute | solution.py:404
  59.1 6.9 %collective-permute-start.6 = (bf16[32,2176]{1,0:T(8,128)(2,1)S(1)}, bf16[32,2176]{1,0:T(8,128)(2,1)S(1)}, u32[]{:S(2)}, u32[]{:S(2)}) collective-permute-start(bf16[32,2176]{1,0:T(8,128)(2,1)S(1)} %get-tuple-element.15.refs_1_), channel_id=1, source_target_pairs={{0,4},{128,140},{4,8},{132,128},{8,12},{136,132},{12,0},{140,136},... | collective-permute-start | bytes 417800 | tf_op jit(solution)/shard_map/ppermute | solution.py:404
  118.5 6.2 %collective-permute-start.9 = (bf16[32,2048]{1,0:T(8,128)(2,1)S(1)}, bf16[32,2048]{1,0:T(8,128)(2,1)S(1)}, u32[]{:S(2)}, u32[]{:S(2)}) collective-permute-start(bf16[32,2048]{1,0:T(8,128)(2,1)S(1)} %get-tuple-element.20), channel_id=1, source_target_pairs={{4,0},{140,128},{8,4},{128,132},{12,8},{132,136},{0,12},{136,140},... | collective-permute-start | bytes 393224 | tf_op jit(solution)/shard_map/ppermute | solution.py:409
  120.4 5.2 %collective-permute-start.10 = (bf16[32,2048]{1,0:T(8,128)(2,1)S(1)}, bf16[32,2048]{1,0:T(8,128)(2,1)S(1)}, u32[]{:S(2)}, u32[]{:S(2)}) collective-permute-start(bf16[32,2048]{1,0:T(8,128)(2,1)S(1)} %get-tuple-element.21), channel_id=1, source_target_pairs={{140,0},{4,128},{128,4},{8,132},{132,8},{12,136},{136,12},{0,140},... | collective-permute-start | bytes 393224 | tf_op jit(solution)/shard_map/ppermute | solution.py:409
  121.8 6.8 %collective-permute-start.11 = (bf16[32,2048]{1,0:T(8,128)(2,1)S(1)}, bf16[32,2048]{1,0:T(8,128)(2,1)S(1)}, u32[]{:S(2)}, u32[]{:S(2)}) collective-permute-start(bf16[32,2048]{1,0:T(8,128)(2,1)S(1)} %get-tuple-element.22), channel_id=1, source_target_pairs={{136,0},{8,128},{140,4},{12,132},{128,8},{0,136},{132,12},{4,140},... | collective-permute-start | bytes 393224 | tf_op jit(solution)/shard_map/ppermute | solution.py:409
